TPU v7x, 32 devices: a whole 2x2x4 slice. The times are simulated.
32 devices in a mesh: ctx: 16 (over z, x, core), fsdp: 2 (over y).
Axes of the slice: x: 2, y: 2, z: 4, core: 2. Of those that a mesh axis runs over, the one named last changes fastest.
Arguments:
- tokens: bfloat16 [2, 4096, 1024], P('fsdp', 'ctx'), may hold values from -6 to 6
- encoder: bfloat16 [2, 2048, 1024], P('fsdp', 'ctx'), may hold values from -6 to 6
- cotangent: bfloat16 [2, 4096, 1024], P('fsdp', 'ctx'), may hold values from -6 to 6
- seq_lengths: int32 [2, 2], P('fsdp'), may hold values from 1024 to 3072, as said below
- source_lengths: int32 [2, 2], P('fsdp'), may hold values from 512 to 1536, as said below
- pair_order: int32 [2, 16], P('fsdp'), may hold values from 0 to 15, each once within a row
- pair_flip: int32 [2, 16], P('fsdp'), may hold values 0 or 1
- ln_gain: bfloat16 [3, 1024], P(None, 'fsdp'), may hold values from 0.25 to 1.75
- ln_bias: bfloat16 [3, 1024], P(None, 'fsdp'), may hold values from -4 to 4
- attn_bias: bfloat16 [2, 3, 1024], P(None, None, 'fsdp'), may hold values from -4 to 4
- self_qkv: bfloat16 [1024, 3072], P('fsdp'), may hold values from -0.1875 to 0.1875
- self_out: bfloat16 [1024, 1024], P('fsdp'), may hold values from -1.5 to 1.5
- cross_q: bfloat16 [1024, 1024], P('fsdp'), may hold values from -0.1875 to 0.1875
- cross_kv: bfloat16 [1024, 2048], P('fsdp'), may hold values from -0.1875 to 0.1875
- cross_out: bfloat16 [1024, 1024], P('fsdp'), may hold values from -1.5 to 1.5
- w_up: bfloat16 [1024, 8192], P('fsdp'), may hold values from -0.1875 to 0.1875
- up_bias: bfloat16 [8192], P('fsdp'), may hold values from -4 to 4
- w_down: bfloat16 [8192, 1024], P('fsdp'), may hold values from -0.0625 to 0.0625
- down_bias: bfloat16 [1024], P('fsdp'), may hold values from -4 to 4
Outputs:
- output: bfloat16 [2, 4096, 1024], P('fsdp', 'ctx')
- grad_tokens: float32 [2, 4096, 1024], P('fsdp', 'ctx')
- grad_encoder: float32 [2, 2048, 1024], P('fsdp', 'ctx')
- grad_ln_gain: float32 [3, 1024], P(None, ('ctx', 'fsdp'))
- grad_ln_bias: float32 [3, 1024], P(None, ('ctx', 'fsdp'))
- grad_attn_bias: float32 [2, 3, 1024], P(None, None, ('ctx', 'fsdp'))
- grad_self_qkv: float32 [1024, 3072], P(('ctx', 'fsdp'))
- grad_self_out: float32 [1024, 1024], P(('ctx', 'fsdp'))
- grad_cross_q: float32 [1024, 1024], P(('ctx', 'fsdp'))
- grad_cross_kv: float32 [1024, 2048], P(('ctx', 'fsdp'))
- grad_cross_out: float32 [1024, 1024], P(('ctx', 'fsdp'))
- grad_w_up: float32 [1024, 8192], P(('ctx', 'fsdp'))
- grad_up_bias: float32 [8192], P(('ctx', 'fsdp'))
- grad_w_down: float32 [8192, 1024], P(('ctx', 'fsdp'))
- grad_down_bias: float32 [1024], P(('ctx', 'fsdp'))
Inputs may be any that keep to these rules, and one draw needn't show every extreme that they name: `seq_lengths`: each row has 2 lengths summing to 4096; the least and the largest are both reached in every row. `source_lengths`: each row has 2 lengths summing to 2048; the least and the largest are both reached in every row. `pair_order`: each row names every pair once; slot j lies on device j // 1 of ctx.
All inputs are finite; a program needn't handle non-finite values. No bound on the sum of `pair_flip` on one device may be relied on, other than what follows from the above.
Results may differ from a plain program's by a relative error of at most 0.025.
Values may be sent and summed in bfloat16 or wider, within the bound.
No kernel may reach another device: no remote copies, remote signals or barrier semaphores. Data moves between devices by JAX's collectives and lax.ppermute only.
A program may use at most 320 MiB of HBM per device.

v0:
```python
import jax
import jax.numpy as jnp
from jax import lax
from jax.sharding import PartitionSpec as P

H = 16
BLOCK = 128


ln_eps = 1e-05
score_scale = 0.125


def layer_norm(v, gain, shift):
    centred = v - jnp.mean(v, axis=-1, keepdims=True)
    spread = jnp.mean(centred * centred, axis=-1, keepdims=True)
    return centred * lax.rsqrt(spread + ln_eps) * gain + shift


def gelu_tanh(v):
    return 0.5 * v * (1.0 + jnp.tanh(0.7978845608028654 * (v + 0.044715 * v * v * v)))


def token_positions(order, flip):
    upper = 2 * order.shape[0] - 1 - order
    first = jnp.where(flip == 1, upper, order)
    second = jnp.where(flip == 1, order, upper)
    blocks = jnp.stack([first, second], axis=1).reshape(-1)
    offsets = jnp.arange(BLOCK, dtype=jnp.int32)
    return (blocks[:, None] * BLOCK + offsets[None, :]).reshape(-1)


def document_of(places, lengths):
    ends = jnp.cumsum(lengths, dtype=jnp.int32)
    return jnp.sum((ends[None, :] <= places[:, None]).astype(jnp.int32), axis=1, dtype=jnp.int32)


def inner_rows(left, right):
    return lax.dot_general(
        left, right, (((0,), (0,)), ((), ())), preferred_element_type=jnp.float32
    )


def times_transposed(left, right):
    return lax.dot_general(
        left, right, (((1,), (1,)), ((), ())), preferred_element_type=jnp.float32
    )


def column_sums(values):
    return jnp.sum(values.astype(jnp.float32), axis=0)


def key_blocks(step, carry, pieces):
    count = pieces[0].shape[0]
    width = 512
    stacked = tuple((piece.reshape((count // width, width) + piece.shape[1:]) for piece in pieces))

    def inner(state, item):
        number, block = item
        return (step(state, block, number * width), None)

    result, _ = lax.scan(inner, carry, (jnp.arange(count // width, dtype=jnp.int32), stacked))
    return result


def forward_step(query_heads, allow):
    heads = query_heads.shape[1]

    def step(carry, block, start):
        top, total, accum = carry
        keys, values = block
        count = keys.shape[0]
        key_heads = keys.reshape(count, heads, -1)
        value_heads = values.reshape(count, heads, -1)
        scores = (
            jnp.einsum("rhd,khd->hrk", query_heads, key_heads, preferred_element_type=jnp.float32)
            * score_scale
        )
        scores = jnp.where(allow(start, count)[None], scores, -jnp.inf)
        newtop = jnp.maximum(top, jnp.max(scores, axis=-1))
        weights = jnp.exp(scores - newtop[:, :, None])
        factor = jnp.exp(top - newtop)
        total = total * factor + jnp.sum(weights, axis=-1)
        accum = accum * factor[:, :, None] + jnp.einsum(
            "hrk,khd->hrd",
            weights.astype(jnp.bfloat16),
            value_heads,
            preferred_element_type=jnp.float32,
        )
        return (newtop, total, accum)

    return lambda carry, block, start: key_blocks(step, carry, block)


def backward_step(query_heads, grad_heads, log_total, deltas, allow):
    heads = query_heads.shape[1]

    def step(carry, block, start):
        grad_query = carry[0]
        keys, values = block
        count = keys.shape[0]
        key_heads = keys.reshape(count, heads, -1)
        value_heads = values.reshape(count, heads, -1)
        scores = (
            jnp.einsum("rhd,khd->hrk", query_heads, key_heads, preferred_element_type=jnp.float32)
            * score_scale
        )
        scores = jnp.where(allow(start, count)[None], scores, -jnp.inf)
        probs = jnp.exp(scores - log_total[:, :, None])
        grad_probs = jnp.einsum(
            "rhd,khd->hrk", grad_heads, value_heads, preferred_element_type=jnp.float32
        )
        grad_scores = (probs * (grad_probs - deltas[:, :, None])).astype(jnp.bfloat16)
        grad_query = grad_query + jnp.einsum(
            "hrk,khd->rhd", grad_scores, key_heads, preferred_element_type=jnp.float32
        )
        grad_keys = (
            jnp.einsum("hrk,rhd->khd", grad_scores, query_heads, preferred_element_type=jnp.float32)
            * score_scale
        )
        grad_values = jnp.einsum(
            "hrk,rhd->khd",
            probs.astype(jnp.bfloat16),
            grad_heads,
            preferred_element_type=jnp.float32,
        )
        block_rows = jnp.concatenate(
            [grad_keys.reshape(count, -1), grad_values.reshape(count, -1)], axis=1
        )
        return (grad_query, lax.dynamic_update_slice_in_dim(carry[1], block_rows, start, 0))

    return lambda carry, block, start: key_blocks(step, carry, block)


def finish(carry):
    top, total, accum = carry
    return (accum / total[:, :, None], top + jnp.log(total))


def per_device(
    tokens,
    encoder,
    cotangent,
    seq_lengths,
    source_lengths,
    pair_order,
    pair_flip,
    ln_gain,
    ln_bias,
    attn_bias,
    self_qkv,
    self_out,
    cross_q,
    cross_kv,
    cross_out,
    w_up,
    up_bias,
    w_down,
    down_bias,
):
    resid = tokens[0].astype(jnp.float32)
    source = encoder[0]
    rows = resid.shape[0]
    width = resid.shape[1]
    src_rows = source.shape[0]
    heads = H
    depth = width // heads
    ctx_count = lax.axis_size("ctx")
    here = lax.axis_index("ctx")
    places = token_positions(pair_order[0], pair_flip[0])
    documents = document_of(places, seq_lengths[0])
    src_docs = document_of(jnp.arange(src_rows * ctx_count, dtype=jnp.int32), source_lengths[0])
    my_places = lax.dynamic_slice_in_dim(places, here * rows, rows)
    my_docs = lax.dynamic_slice_in_dim(documents, here * rows, rows)

    def self_allow(start, count):
        key_places = lax.dynamic_slice_in_dim(places, start, count)
        key_docs = lax.dynamic_slice_in_dim(documents, start, count)
        return (my_docs[:, None] == key_docs[None, :]) & (key_places[None, :] <= my_places[:, None])

    def cross_allow(start, count):
        key_docs = lax.dynamic_slice_in_dim(src_docs, start, count)
        return my_docs[:, None] == key_docs[None, :]

    w_qkv, w_out, gains, shifts, biases, bias_up, bias_down = (
        lax.all_gather(self_qkv, "fsdp", axis=0, tiled=True),
        lax.all_gather(self_out, "fsdp", axis=0, tiled=True),
        lax.all_gather(ln_gain, "fsdp", axis=1, tiled=True),
        lax.all_gather(ln_bias, "fsdp", axis=1, tiled=True),
        lax.all_gather(attn_bias, "fsdp", axis=2, tiled=True),
        lax.all_gather(up_bias, "fsdp", axis=0, tiled=True),
        lax.all_gather(down_bias, "fsdp", axis=0, tiled=True),
    )
    gains = gains.astype(jnp.float32)
    shifts = shifts.astype(jnp.float32)
    biases = biases.astype(jnp.float32)
    bias_up = bias_up.astype(jnp.float32)
    bias_down = bias_down.astype(jnp.float32)
    norm_one, back_one = jax.vjp(layer_norm, resid, gains[0], shifts[0])
    normed_one = norm_one.astype(jnp.bfloat16)
    projected = jnp.dot(normed_one, w_qkv, preferred_element_type=jnp.float32)
    query = (projected[:, :width] + biases[0, 0]).astype(jnp.bfloat16)
    keys = projected[:, width : 2 * width].astype(jnp.bfloat16)
    values = (projected[:, 2 * width :] + biases[0, 1]).astype(jnp.bfloat16)
    query_heads = query.reshape(rows, heads, depth)
    start_carry = (
        jnp.full((heads, rows), -1e30, jnp.float32),
        jnp.zeros((heads, rows), jnp.float32),
        jnp.zeros((heads, rows, depth), jnp.float32),
    )
    state = forward_step(query_heads, self_allow)(
        start_carry,
        (
            lax.all_gather(keys, "ctx", axis=0, tiled=True),
            lax.all_gather(values, "ctx", axis=0, tiled=True),
        ),
        jnp.int32(0),
    )
    self_heads, self_lse = finish(state)
    self_att = self_heads.transpose(1, 0, 2).reshape(rows, width).astype(jnp.bfloat16)
    mixed_one = resid + jnp.dot(self_att, w_out, preferred_element_type=jnp.float32) + biases[0, 2]
    w_cq, w_ckv, w_cout = (
        lax.all_gather(cross_q, "fsdp", axis=0, tiled=True),
        lax.all_gather(cross_kv, "fsdp", axis=0, tiled=True),
        lax.all_gather(cross_out, "fsdp", axis=0, tiled=True),
    )
    norm_two, back_two = jax.vjp(layer_norm, mixed_one, gains[1], shifts[1])
    normed_two = norm_two.astype(jnp.bfloat16)
    cross_query = (
        jnp.dot(normed_two, w_cq, preferred_element_type=jnp.float32) + biases[1, 0]
    ).astype(jnp.bfloat16)
    src_proj = jnp.dot(source, w_ckv, preferred_element_type=jnp.float32)
    cross_keys = src_proj[:, :width].astype(jnp.bfloat16)
    cross_values = (src_proj[:, width:] + biases[1, 1]).astype(jnp.bfloat16)
    cross_query_heads = cross_query.reshape(rows, heads, depth)
    state = forward_step(cross_query_heads, cross_allow)(
        start_carry,
        (
            lax.all_gather(cross_keys, "ctx", axis=0, tiled=True),
            lax.all_gather(cross_values, "ctx", axis=0, tiled=True),
        ),
        jnp.int32(0),
    )
    cross_heads, cross_lse = finish(state)
    cross_att = cross_heads.transpose(1, 0, 2).reshape(rows, width).astype(jnp.bfloat16)
    mixed_two = (
        mixed_one + jnp.dot(cross_att, w_cout, preferred_element_type=jnp.float32) + biases[1, 2]
    )
    w_upper, w_lower = (
        lax.all_gather(w_up, "fsdp", axis=0, tiled=True),
        lax.all_gather(w_down, "fsdp", axis=0, tiled=True),
    )
    norm_three, back_three = jax.vjp(layer_norm, mixed_two, gains[2], shifts[2])
    normed_three = norm_three.astype(jnp.bfloat16)
    hidden_pre = jnp.dot(normed_three, w_upper, preferred_element_type=jnp.float32) + bias_up
    activated, back_gelu = jax.vjp(gelu_tanh, hidden_pre)
    act_low = activated.astype(jnp.bfloat16)
    result = mixed_two + jnp.dot(act_low, w_lower, preferred_element_type=jnp.float32) + bias_down
    grad_out = cotangent[0].astype(jnp.float32)
    grad_low = cotangent[0]
    grad_w_lower = inner_rows(act_low, grad_low)
    grad_b_lower = column_sums(grad_low)
    grad_act = times_transposed(grad_low, w_lower)
    grad_hidden = back_gelu(grad_act)[0].astype(jnp.bfloat16)
    grad_w_upper = inner_rows(normed_three, grad_hidden)
    grad_b_upper = column_sums(grad_hidden)
    grad_ln_three, gain_three, shift_three = back_three(times_transposed(grad_hidden, w_upper))
    grad_two = grad_out + grad_ln_three
    upper_own, lower_own = (
        lax.psum_scatter(grad_w_upper, ("ctx", "fsdp"), scatter_dimension=0, tiled=True),
        lax.psum_scatter(grad_w_lower, ("ctx", "fsdp"), scatter_dimension=0, tiled=True),
    )
    grad_two_low = grad_two.astype(jnp.bfloat16)
    grad_w_cout = inner_rows(cross_att, grad_two_low)
    grad_b_cout = column_sums(grad_two_low)
    grad_cross_att = times_transposed(grad_two_low, w_cout).astype(jnp.bfloat16)
    grad_cross_heads = grad_cross_att.reshape(rows, heads, depth)
    cross_delta = jnp.einsum("rhd,hrd->hr", grad_cross_heads.astype(jnp.float32), cross_heads)
    cross_carry = (
        jnp.zeros((rows, heads, depth), jnp.float32),
        jnp.zeros((src_rows * ctx_count, 2 * width), jnp.float32),
    )
    cross_dq, cross_dkv = backward_step(
        cross_query_heads, grad_cross_heads, cross_lse, cross_delta, cross_allow
    )(
        cross_carry,
        (
            lax.all_gather(cross_keys, "ctx", axis=0, tiled=True),
            lax.all_gather(cross_values, "ctx", axis=0, tiled=True),
        ),
        jnp.int32(0),
    )
    own_cross_kv = lax.psum_scatter(
        cross_dkv.astype(jnp.bfloat16), "ctx", scatter_dimension=0, tiled=True
    )
    grad_w_ckv = inner_rows(source, own_cross_kv)
    grad_b_cv = column_sums(own_cross_kv[:, width:])
    grad_source = times_transposed(own_cross_kv, w_ckv)
    grad_cq = (cross_dq * score_scale).reshape(rows, width).astype(jnp.bfloat16)
    grad_w_cq = inner_rows(normed_two, grad_cq)
    grad_b_cq = column_sums(grad_cq)
    grad_ln_two, gain_two, shift_two = back_two(times_transposed(grad_cq, w_cq))
    grad_one = grad_two + grad_ln_two
    cq_own, ckv_own, cout_own = (
        lax.psum_scatter(grad_w_cq, ("ctx", "fsdp"), scatter_dimension=0, tiled=True),
        lax.psum_scatter(grad_w_ckv, ("ctx", "fsdp"), scatter_dimension=0, tiled=True),
        lax.psum_scatter(grad_w_cout, ("ctx", "fsdp"), scatter_dimension=0, tiled=True),
    )
    grad_one_low = grad_one.astype(jnp.bfloat16)
    grad_w_out = inner_rows(self_att, grad_one_low)
    grad_b_out = column_sums(grad_one_low)
    grad_self_att = times_transposed(grad_one_low, w_out).astype(jnp.bfloat16)
    grad_self_heads = grad_self_att.reshape(rows, heads, depth)
    self_delta = jnp.einsum("rhd,hrd->hr", grad_self_heads.astype(jnp.float32), self_heads)
    self_carry = (
        jnp.zeros((rows, heads, depth), jnp.float32),
        jnp.zeros((rows * ctx_count, 2 * width), jnp.float32),
    )
    self_dq, self_dkv = backward_step(
        query_heads, grad_self_heads, self_lse, self_delta, self_allow
    )(
        self_carry,
        (
            lax.all_gather(keys, "ctx", axis=0, tiled=True),
            lax.all_gather(values, "ctx", axis=0, tiled=True),
        ),
        jnp.int32(0),
    )
    own_self_kv = lax.psum_scatter(
        self_dkv.astype(jnp.bfloat16), "ctx", scatter_dimension=0, tiled=True
    )
    grad_query = (self_dq * score_scale).reshape(rows, width).astype(jnp.bfloat16)
    grad_qkv = jnp.concatenate([grad_query, own_self_kv], axis=1)
    grad_w_qkv = inner_rows(normed_one, grad_qkv)
    grad_b_query = column_sums(grad_query)
    grad_b_value = column_sums(own_self_kv[:, width:])
    grad_ln_one, gain_one, shift_one = back_one(times_transposed(grad_qkv, w_qkv))
    grad_input = grad_one + grad_ln_one
    grad_gains = jnp.stack([gain_one, gain_two, gain_three])
    grad_shifts = jnp.stack([shift_one, shift_two, shift_three])
    grad_biases = jnp.stack(
        [
            jnp.stack([grad_b_query, grad_b_value, grad_b_out]),
            jnp.stack([grad_b_cq, grad_b_cv, grad_b_cout]),
        ]
    )
    qkv_own, out_own, gains_own, shifts_own, biases_own, bup_own, bdown_own = (
        lax.psum_scatter(grad_w_qkv, ("ctx", "fsdp"), scatter_dimension=0, tiled=True),
        lax.psum_scatter(grad_w_out, ("ctx", "fsdp"), scatter_dimension=0, tiled=True),
        lax.psum_scatter(grad_gains, ("ctx", "fsdp"), scatter_dimension=1, tiled=True),
        lax.psum_scatter(grad_shifts, ("ctx", "fsdp"), scatter_dimension=1, tiled=True),
        lax.psum_scatter(grad_biases, ("ctx", "fsdp"), scatter_dimension=2, tiled=True),
        lax.psum_scatter(grad_b_upper, ("ctx", "fsdp"), scatter_dimension=0, tiled=True),
        lax.psum_scatter(grad_b_lower, ("ctx", "fsdp"), scatter_dimension=0, tiled=True),
    )
    return (
        result.astype(jnp.bfloat16)[None],
        grad_input[None],
        grad_source[None],
        gains_own,
        shifts_own,
        biases_own,
        qkv_own,
        out_own,
        cq_own,
        ckv_own,
        cout_own,
        upper_own,
        bup_own,
        lower_own,
        bdown_own,
    )


def solution(mesh):
    placed = (
        P("fsdp", "ctx", None),
        P("fsdp", "ctx", None),
        P("fsdp", "ctx", None),
        P("fsdp", None),
        P("fsdp", None),
        P("fsdp", None),
        P("fsdp", None),
        P(None, "fsdp"),
        P(None, "fsdp"),
        P(None, None, "fsdp"),
        P("fsdp", None),
        P("fsdp", None),
        P("fsdp", None),
        P("fsdp", None),
        P("fsdp", None),
        P("fsdp", None),
        P("fsdp"),
        P("fsdp", None),
        P("fsdp"),
    )
    return jax.shard_map(
        per_device,
        mesh=mesh,
        in_specs=placed,
        out_specs=(
            P("fsdp", "ctx", None),
            P("fsdp", "ctx", None),
            P("fsdp", "ctx", None),
            P(None, ("ctx", "fsdp")),
            P(None, ("ctx", "fsdp")),
            P(None, None, ("ctx", "fsdp")),
            P(("ctx", "fsdp"), None),
            P(("ctx", "fsdp"), None),
            P(("ctx", "fsdp"), None),
            P(("ctx", "fsdp"), None),
            P(("ctx", "fsdp"), None),
            P(("ctx", "fsdp"), None),
            P(("ctx", "fsdp")),
            P(("ctx", "fsdp"), None),
            P(("ctx", "fsdp")),
        ),
        check_vma=False,
    )
```

profile of v0, /device:TPU:0, one launch (start us, length us, event | category | flops | bytes accessed | tf_op | source)
XLA Modules:
  0.0 3936.7 jit_solution(10387177272679630371)
XLA Ops:
  8.8 60.3 %all-gather.21.cloned.1.call-done = bf16[1024,2048]{1,0:T(8,128)(2,1)} async-done(((bf16[512,2048]{1,0:T(8,128)(2,1)}), bf16[1024,2048]{1,0:T(8,128)(2,1)}) %all-gather.21.cloned.1.call-update) | async-done | bytes 4194320 | tf_op jit(solution)/shard_map/all_gather | solution.py:225
  87.9 63.2 %all-gather.13.cloned.1.call-done = bf16[1024,3072]{1,0:T(8,128)(2,1)} async-done(((bf16[512,3072]{1,0:T(8,128)(2,1)}), bf16[1024,3072]{1,0:T(8,128)(2,1)}) %all-gather.13.cloned.1.call-update) | async-done | bytes 6291472 | tf_op jit(solution)/shard_map/all_gather | solution.py:187
  170.6 33.9 all-gather.23.cloned.1.call-done
  210.7 45.5 %all-gather.27.cloned.1.call-done = bf16[2048,1024]{1,0:T(8,128)(2,1)} async-done(((bf16[128,1024]{1,0:T(8,128)(2,1)}), bf16[2048,1024]{1,0:T(8,128)(2,1)}) %all-gather.27.cloned.1.call-update) | async-done | bytes 4194320 | tf_op jit(solution)/shard_map/all_gather | solution.py:241
  262.3 69.8 %all-gather.17.cloned.1.call-done = bf16[4096,1024]{1,0:T(8,128)(2,1)} async-done(((bf16[256,1024]{1,0:T(8,128)(2,1)}), bf16[4096,1024]{1,0:T(8,128)(2,1)}) %all-gather.17.cloned.1.call-update) | async-done | bytes 8388624 | tf_op jit(solution)/shard_map/all_gather | solution.py:216
  343.7 64.2 %all-gather.15.cloned.1.call-done = bf16[4096,1024]{1,0:T(8,128)(2,1)} async-done(((bf16[256,1024]{1,0:T(8,128)(2,1)}), bf16[4096,1024]{1,0:T(8,128)(2,1)}) %all-gather.15.cloned.1.call-update) | async-done | bytes 8388624 | tf_op jit(solution)/shard_map/all_gather | solution.py:215
  419.5 70.8 %while.56 = (s32[]{:T(128)}, f32[16,256]{1,0:T(8,128)S(1)}, f32[16,256]{1,0:T(8,128)S(1)}, f32[16,256,64]{1,2,0:T(8,128)S(1)}, s32[256]{0:T(256)S(1)}, /*index=5...) while((s32[]{:T(128)}, f32[16,256]{1,0:T(8,128)S(1)}, ...), condition=%wide.region_7.8_spmd.clone, body=%wide.region_4.7_spmd.clone.sunk | while | flops 561139712 | bytes 34879724 | solution.py:63
  497.2 39.5 %while.57 = (s32[]{:T(128)}, f32[16,256]{1,0:T(8,128)S(1)}, f32[16,256]{1,0:T(8,128)S(1)}, f32[16,256,64]{1,2,0:T(8,128)}, s32[256]{0:T(256)S(1)}, /*index=5*/s3...) while((s32[]{:T(128)}, f32[16,256]{1,0:T(8,128)S(1)}, ...), condition=%wide.region_15.16_spmd.clone, body=%wide.region_12.15_spmd.clone.sunk | while | flops 560877568 | bytes 43261200 | solution.py:63
  541.9 168.6 %all-gather.31.cloned.1.call-done = bf16[1024,8192]{1,0:T(8,128)(2,1)} async-done(((bf16[512,8192]{1,0:T(8,128)(2,1)}), bf16[1024,8192]{1,0:T(8,128)(2,1)}) %all-gather.31.cloned.1.call-update) | async-done | bytes 16777232 | tf_op jit(solution)/shard_map/all_gather | solution.py:251
  724.4 186.6 %all-gather.33.cloned.1.call-done = bf16[8192,1024]{1,0:T(8,128)(2,1)} async-done(((bf16[4096,1024]{1,0:T(8,128)(2,1)}), bf16[8192,1024]{1,0:T(8,128)(2,1)}) %all-gather.33.cloned.1.call-update) | async-done | bytes 16777232 | tf_op jit(solution)/shard_map/all_gather | solution.py:252
  911.0 17.8 convert_reduce_fusion
  957.5 52.9 %while.58 = (s32[]{:T(128)}, f32[256,16,64]{0,2,1:T(8,128)S(1)}, bf16[2048,2048]{0,1:T(8,128)(2,1)}, bf16[4,512,1024]{1,2,0:T(8,128)(2,1)}, s32[256]{0:T(256)S(1...) while((s32[]{:T(128)}, f32[256,16,64]{0,2,1:T(8,128)S(1)}, ...), condition=%wide.region_21.22_spmd.clone, body=%wide.region_20.21_spmd.clone.sunk | while | flops 1369047040 | bytes 58121480 | solution.py:63
  1041.2 117.5 %while.59 = (s32[]{:T(128)}, f32[256,16,64]{0,2,1:T(8,128)S(1)}, bf16[4096,2048]{0,1:T(8,128)(2,1)}, bf16[8,512,1024]{1,2,0:T(8,128)(2,1)}, s32[256]{0:T(256)S(1...) while((s32[]{:T(128)}, f32[256,16,64]{0,2,1:T(8,128)S(1)}, ...), condition=%wide.region_25.26_spmd.clone, body=%wide.region_24.25_spmd.clone.sunk | while | flops 1369309184 | bytes 58128668 | solution.py:63
  1161.1 176.6 %reduce-scatter.23.cloned.1.call-done = bf16[256,2048]{0,1:T(8,128)(2,1)} async-done(((bf16[4096,2048]{0,1:T(8,128)(2,1)}), bf16[256,2048]{0,1:T(8,128)(2,1)}) %reduce-scatter.23.cloned.1.call-update) | async-done | bytes 1048592 | tf_op jit(solution)/shard_map/reduce_scatter | solution.py:330
  1423.4 39.8 %all-reduce.2 = (f32[8192]{0:T(1024)S(1)}, f32[1024]{0:T(1024)S(1)}) all-reduce(f32[8192]{0:T(1024)S(1)} %copy-done.54, f32[1024]{0:T(1024)S(1)} %copy-done.58), channel_id=13, replica_groups=mesh['ctx'=16,'fsdp'=2] {'ctx','fsdp'}, use_global_device_ids=true, to_apply=%region_52.53.clone | all-reduce | flops 9216 | bytes 73728
  1483.9 127.0 %reduce-scatter.41.cloned.1.call-done = f32[32,3]{1,0:T(8,128)} async-done(((f32[1024,3]{1,0:T(8,128)}), f32[32,3]{1,0:T(8,128)}) %reduce-scatter.41.cloned.1.call-update) | async-done | bytes 400
  1612.3 130.7 %reduce-scatter.43.cloned.1.call-done = f32[32,6]{1,0:T(8,128)} async-done(((f32[1024,6]{1,0:T(8,128)}), f32[32,6]{1,0:T(8,128)}) %reduce-scatter.43.cloned.1.call-update) | async-done | bytes 784
  1744.5 138.6 %reduce-scatter.31.cloned.1.call-done = f32[32,1024]{1,0:T(8,128)} async-done(((f32[1024,1024]{1,0:T(8,128)}), f32[32,1024]{1,0:T(8,128)}) %reduce-scatter.31.cloned.1.call-update) | async-done | bytes 131088 | tf_op jit(solution)/shard_map/reduce_scatter | solution.py:308
  1883.1 141.2 %reduce-scatter.29.cloned.1.call-done = f32[32,1024]{1,0:T(8,128)} async-done(((f32[1024,1024]{1,0:T(8,128)}), f32[32,1024]{1,0:T(8,128)}) %reduce-scatter.29.cloned.1.call-update) | async-done | bytes 131088 | tf_op jit(solution)/shard_map/reduce_scatter | solution.py:306
  2024.3 141.1 %reduce-scatter.27.cloned.1.call-done = f32[32,1024]{1,0:T(8,128)} async-done(((f32[1024,1024]{1,0:T(8,128)}), f32[32,1024]{1,0:T(8,128)}) %reduce-scatter.27.cloned.1.call-update) | async-done | bytes 131088 | tf_op jit(solution)/shard_map/reduce_scatter | solution.py:350
  2165.5 182.9 %reduce-scatter.45.cloned.1.call-done = f32[32,2048]{1,0:T(8,128)} async-done(((f32[1024,2048]{1,0:T(8,128)}), f32[32,2048]{1,0:T(8,128)}) %reduce-scatter.45.cloned.1.call-update) | async-done | bytes 262160
  2348.3 163.4 %reduce-scatter.25.cloned.1.call-done = f32[32,3072]{1,0:T(8,128)} async-done(((f32[1024,3072]{1,0:T(8,128)}), f32[32,3072]{1,0:T(8,128)}) %reduce-scatter.25.cloned.1.call-update) | async-done | bytes 393232 | tf_op jit(solution)/shard_map/reduce_scatter | solution.py:349
  2511.8 707.9 %reduce-scatter.35.cloned.1.call-done = f32[256,1024]{1,0:T(8,128)} async-done(((f32[8192,1024]{1,0:T(8,128)}), f32[256,1024]{1,0:T(8,128)}) %reduce-scatter.35.cloned.1.call-update) | async-done | bytes 1048592 | tf_op jit(solution)/shard_map/reduce_scatter | solution.py:272
  3219.7 710.2 %reduce-scatter.33.cloned.1.call-done = f32[32,8192]{1,0:T(8,128)} async-done(((f32[1024,8192]{1,0:T(8,128)}), f32[32,8192]{1,0:T(8,128)}) %reduce-scatter.33.cloned.1.call-update) | async-done | bytes 1048592 | tf_op jit(solution)/shard_map/reduce_scatter | solution.py:271
  (621 shorter events, 534.0 us)
Async XLA Ops:
  7.2 61.9 %all-gather.21.cloned.1.call-start = ((), (), s32[]{:S(2)}) async-start(), calls=%async_computation.16 | async-start | bytes 6291456 | tf_op jit(solution)/shard_map/all_gather | solution.py:225
  8.0 143.1 %all-gather.13.cloned.1.call-start = ((), (), s32[]{:S(2)}) async-start(), calls=%async_computation.12 | async-start | bytes 9437184 | tf_op jit(solution)/shard_map/all_gather | solution.py:187
  8.7 195.7 %all-gather.23.cloned.1.call-start = ((), (), s32[]{:S(2)}) async-start(), calls=%async_computation.17 | async-start | bytes 4456448 | tf_op jit(solution)/shard_map/all_gather | solution.py:240
  72.8 183.3 %all-gather.27.cloned.1.call-start = ((), (), s32[]{:S(2)}) async-start(), calls=%async_computation.19 | async-start | bytes 4456448 | tf_op jit(solution)/shard_map/all_gather | solution.py:241
  78.0 254.1 %all-gather.17.cloned.1.call-start = ((), (), s32[]{:S(2)}) async-start(), calls=%async_computation.14 | async-start | bytes 8912896 | tf_op jit(solution)/shard_map/all_gather | solution.py:216
  87.8 854.3 %copy-start.34 = (f32[1,1024]{1,0:T(1,128)}, f32[1,1024]{1,0:T(1,128)S(1)}, u32[]{:S(2)}) copy-start(f32[1,1024]{1,0:T(1,128)S(1)} %get-tuple-element.832) | copy-start | bytes 12292
  158.5 249.4 %all-gather.15.cloned.1.call-start = ((), (), s32[]{:S(2)}) async-start(), calls=%async_computation.13 | async-start | bytes 8912896 | tf_op jit(solution)/shard_map/all_gather | solution.py:215
  160.7 329.8 %all-gather.19.cloned.1.call-start = ((), (), s32[]{:S(2)}) async-start(), calls=%async_computation.15 | async-start | bytes 3145728 | tf_op jit(solution)/shard_map/all_gather | solution.py:188
  161.5 332.6 %all-gather.25.cloned.1.call-start = ((), (), s32[]{:S(2)}) async-start(), calls=%async_computation.18 | async-start | bytes 3145728 | tf_op jit(solution)/shard_map/all_gather | solution.py:224
  162.2 376.0 %all-gather.29.cloned.1.call-start = ((), (), s32[]{:S(2)}) async-start(), calls=%async_computation.20 | async-start | bytes 3145728 | tf_op jit(solution)/shard_map/all_gather | solution.py:226
  163.0 547.6 %all-gather.31.cloned.1.call-start = ((), (), s32[]{:S(2)}) async-start(), calls=%async_computation.21 | async-start | bytes 25165824 | tf_op jit(solution)/shard_map/all_gather | solution.py:251
  163.6 747.4 %all-gather.33.cloned.1.call-start = ((), (), s32[]{:S(2)}) async-start(), calls=%async_computation.22 | async-start | bytes 25165824 | tf_op jit(solution)/shard_map/all_gather | solution.py:252
  164.3 995.5 %reduce-scatter.37.cloned.1.call-start = ((), (), s32[]{:S(2)}) async-start(), calls=%async_computation.30 | async-start | bytes 8912896
  1022.8 314.9 %reduce-scatter.23.cloned.1.call-start = ((), (), s32[]{:S(2)}) async-start(), calls=%async_computation.23 | async-start | bytes 17825792 | tf_op jit(solution)/shard_map/reduce_scatter | solution.py:330
  1158.7 323.8 %reduce-scatter.39.cloned.1.call-start = ((), (), s32[]{:S(2)}) async-start(), calls=%async_computation.31 | async-start | bytes 540672
  1345.7 265.2 %reduce-scatter.41.cloned.1.call-start = ((), (), s32[]{:S(2)}) async-start(), calls=%async_computation.32 | async-start | bytes 540672
  1346.8 396.2 %reduce-scatter.43.cloned.1.call-start = ((), (), s32[]{:S(2)}) async-start(), calls=%async_computation.33 | async-start | bytes 540672
  1352.2 530.9 %reduce-scatter.31.cloned.1.call-start = ((), (), s32[]{:S(2)}) async-start(), calls=%async_computation.27 | async-start | bytes 4325376 | tf_op jit(solution)/shard_map/reduce_scatter | solution.py:308
  1355.0 669.3 %reduce-scatter.29.cloned.1.call-start = ((), (), s32[]{:S(2)}) async-start(), calls=%async_computation.26 | async-start | bytes 4325376 | tf_op jit(solution)/shard_map/reduce_scatter | solution.py:306
  1359.3 806.2 %reduce-scatter.27.cloned.1.call-start = ((), (), s32[]{:S(2)}) async-start(), calls=%async_computation.25 | async-start | bytes 4325376 | tf_op jit(solution)/shard_map/reduce_scatter | solution.py:350
  1363.1 985.2 %reduce-scatter.45.cloned.1.call-start = ((), (), s32[]{:S(2)}) async-start(), calls=%async_computation.34 | async-start | bytes 8650752
  1376.9 1134.9 %reduce-scatter.25.cloned.1.call-start = ((), (), s32[]{:S(2)}) async-start(), calls=%async_computation.24 | async-start | bytes 12976128 | tf_op jit(solution)/shard_map/reduce_scatter | solution.py:349
  1385.7 1834.0 %reduce-scatter.35.cloned.1.call-start = ((), (), s32[]{:S(2)}) async-start(), calls=%async_computation.29 | async-start | bytes 34603008 | tf_op jit(solution)/shard_map/reduce_scatter | solution.py:272
  1401.7 2528.2 %reduce-scatter.33.cloned.1.call-start = ((), (), s32[]{:S(2)}) async-start(), calls=%async_computation.28 | async-start | bytes 34603008 | tf_op jit(solution)/shard_map/reduce_scatter | solution.py:271
  (96 other events, 5059.7 us)
Sparse Core Ops, SparseCore 0:
  9.6 59.4 all-gather.20
  70.6 80.4 all-gather.12
  153.8 50.5 all-gather.22
  207.0 49.0 all-gather.26
  258.7 73.3 all-gather.16
  334.7 73.1 all-gather.14
  409.4 31.3 all-gather.18
  442.4 33.1 all-gather.24
  477.1 33.0 all-gather.28
  511.7 198.8 all-gather.30
  712.1 198.8 all-gather.32
  1022.9 104.5 reduce-scatter.36
  1158.8 178.8 reduce-scatter.22
  1345.8 132.8 reduce-scatter.38
  1480.9 129.9 reduce-scatter.40
  1613.0 129.9 reduce-scatter.42
  1745.8 137.2 reduce-scatter.30
  1885.9 138.3 reduce-scatter.28
  2027.3 138.1 reduce-scatter.26
  2168.3 180.0 reduce-scatter.44
  2356.0 155.7 reduce-scatter.24
  2514.6 705.0 reduce-scatter.34
  3222.6 707.2 reduce-scatter.32
where the time goes:
time: 3940 us
  waiting for transfers between devices  3320 us (84%)
  matrix products  289 us (7%)
  local copies, waits for them, and re-layouts  174 us (4%)
  blocking collectives  62.1 us (2%)
  other arithmetic  60.2 us (2%)
    reduce_scatter x1, waiting for transfers between devices, per_device(): lax.psum_scatter(grad_w_upper, ('ctx', 'fsdp'), scatter_dimension=0, tile...  710 us
    reduce_scatter x1, waiting for transfers between devices, per_device(): lax.psum_scatter(grad_w_lower, ('ctx', 'fsdp'), scatter_dimension=0, tile...  708 us
    unnamed x28, waiting for transfers between devices  446 us
    all_gather x1, waiting for transfers between devices, per_device(): lax.all_gather(w_down, 'fsdp', axis=0, tiled=True)  187 us
    reduce_scatter x1, waiting for transfers between devices, per_device(): lax.psum_scatter(self_dkv.astype(jnp.bfloat16), 'ctx', scatter_dimension=...  177 us
    all_gather x1, waiting for transfers between devices, per_device(): lax.all_gather(w_up, 'fsdp', axis=0, tiled=True)  169 us
    reduce_scatter x1, waiting for transfers between devices, per_device(): lax.psum_scatter(grad_w_qkv, ('ctx', 'fsdp'), scatter_dimension=0, tiled=...  163 us
    reduce_scatter x1, waiting for transfers between devices, per_device(): lax.psum_scatter(grad_w_cq, ('ctx', 'fsdp'), scatter_dimension=0, tiled=T...  141 us
  transfers between devices with their start and end apart: 23, of which 18 were waited for; matrix products, arithmetic and copies ran while one was open for 10% of the time, Pallas kernels for 0%

commit v1 on v0

v1 whole, which is shorter than its diff:
```python
import functools

import jax
import jax.numpy as jnp
from jax import lax
from jax.experimental import pallas as pl
from jax.experimental.pallas import tpu as pltpu
from jax.sharding import Mesh
from jax.sharding import PartitionSpec as P

H = 16
BLOCK = 128

CHIP = ("part", "hc")
HEADS = ("hc", "core")
CTX = ("part", "hc", "core")
QUAD = ("core", "fsdp")
ALL = ("part", "hc", "core", "fsdp")

ln_eps = 1e-05
score_scale = 0.125
low = jnp.bfloat16
full = jnp.float32
VMEM_BYTES = 56 * 1024 * 1024


def layer_norm(v, gain, shift):
    centred = v - jnp.mean(v, axis=-1, keepdims=True)
    spread = jnp.mean(centred * centred, axis=-1, keepdims=True)
    return centred * lax.rsqrt(spread + ln_eps) * gain + shift


def gelu_tanh(v):
    return 0.5 * v * (1.0 + jnp.tanh(0.7978845608028654 * (v + 0.044715 * v * v * v)))


def contract(left, right, left_dim, right_dim):
    return lax.dot_general(
        left, right, (((left_dim,), (right_dim,)), ((), ())), preferred_element_type=full
    )


def column_sums(values):
    return jnp.sum(values.astype(full), axis=0)


def block_numbers(order, flip):
    upper = 2 * order.shape[0] - 1 - order
    first = jnp.where(flip == 1, upper, order)
    second = jnp.where(flip == 1, order, upper)
    return jnp.stack([first, second], axis=1).reshape(-1)


def sorted_slots(blocks):
    count = blocks.shape[0]
    rank = jnp.sum((blocks[None, :] < blocks[:, None]).astype(jnp.int32), axis=1)
    hit = rank[None, :] == jnp.arange(count, dtype=jnp.int32)[:, None]
    return jnp.sum(jnp.where(hit, jnp.arange(count, dtype=jnp.int32)[None, :], 0), axis=1)


def document_starts(places, lengths):
    ends = jnp.cumsum(lengths, dtype=jnp.int32)
    passed = ends[None, :] <= places[:, None]
    return jnp.max(jnp.where(passed, ends[None, :], 0), axis=1)


def source_range(places, lengths, source_lengths):
    ends = jnp.cumsum(lengths, dtype=jnp.int32)
    passed = ends[None, :] <= places[:, None]
    source_ends = jnp.cumsum(source_lengths, dtype=jnp.int32)
    start = jnp.max(jnp.where(passed, source_ends[None, :], 0), axis=1)
    stop = jnp.min(jnp.where(passed, source_ends[-1], source_ends[None, :]), axis=1)
    return start, stop


def tile_plan(start, stop, query_tile, key_tile):
    start = start.reshape(-1, query_tile)
    stop = stop.reshape(-1, query_tile)
    first = jnp.min(start, axis=1) // key_tile
    last = (jnp.max(stop, axis=1) + key_tile - 1) // key_tile
    inner = jnp.clip((jnp.max(start, axis=1) + key_tile - 1) // key_tile, first, last)
    outer = jnp.clip(jnp.min(stop, axis=1) // key_tile, inner, last)
    return jnp.stack([first, inner, outer, last]).astype(jnp.int32)


def over_tiles(plan, tile_number, step, carry):
    first, inner = plan[0, tile_number], plan[1, tile_number]
    outer, last = plan[2, tile_number], plan[3, tile_number]
    carry = lax.fori_loop(inner, outer, functools.partial(step, masked=False), carry)
    before = inner - first

    def edge(index, state):
        number = jnp.where(index < before, first + index, outer + index - before)
        return step(number, state, masked=True)

    return lax.fori_loop(0, before + last - outer, edge, carry)


def masked_scores(scores, number, tile, start, stop):
    keys = number * tile + lax.broadcasted_iota(jnp.int32, scores.shape, 0)
    return jnp.where((keys >= start) & (keys < stop), scores, -jnp.inf)


def forward_tiles(plan, number, query, start, stop, keys_of, values_of, tile, depth):
    width = query.shape[1]

    def step(j, carry, masked):
        top, total, accum = carry
        scores = contract(keys_of(j), query, 1, 0)
        if masked:
            scores = masked_scores(scores, j, tile, start, stop)
        newtop = jnp.maximum(top, jnp.max(scores, axis=0, keepdims=True))
        weights = jnp.exp(scores - newtop)
        factor = jnp.exp(top - newtop)
        total = total * factor + jnp.sum(weights, axis=0, keepdims=True)
        accum = accum * factor + contract(values_of(j), weights.astype(low), 1, 0)
        return newtop, total, accum

    carry = (
        jnp.full((1, width), -1e30, full),
        jnp.zeros((1, width), full),
        jnp.zeros((depth, width), full),
    )
    top, total, accum = over_tiles(plan, number, step, carry)
    return accum / total, top + jnp.log(total)


def tile_at(number, size):
    return pl.ds(pl.multiple_of(number * size, size), size)


def half_at(slot):
    return pl.ds(pl.multiple_of((slot & 1) * BLOCK, BLOCK), BLOCK)


def self_forward_kernel(
    tile, plan, query_slot, key_slot, range_ref, own_ref, all_ref,
    out_ref, exact_ref, lse_ref, query_s, key_s, value_s,
):
    depth, queries = query_s.shape
    count = value_s.shape[1]

    @pl.loop(0, queries // BLOCK)
    def _(b):
        slot = query_slot[b]
        query_s[:, tile_at(b, BLOCK)] = own_ref[slot >> 1, 0:depth, half_at(slot)] * low(score_scale)

    @pl.loop(0, count // BLOCK)
    def _(b):
        slot = key_slot[b]
        block = all_ref[slot >> 1, depth : 2 * depth, half_at(slot)]
        key_s[tile_at(b, BLOCK), :] = block.T
        value_s[:, tile_at(b, BLOCK)] = all_ref[slot >> 1, 2 * depth : 3 * depth, half_at(slot)]

    @pl.loop(0, queries // tile)
    def _(t):
        here = tile_at(t, tile)
        result, lse = forward_tiles(
            plan, t, query_s[:, here], range_ref[0:1, here], range_ref[1:2, here],
            lambda j: key_s[tile_at(j, tile), :], lambda j: value_s[:, tile_at(j, tile)],
            tile, depth,
        )
        exact_ref[:, here] = result
        lse_ref[0:1, here] = lse

    @pl.loop(0, queries // BLOCK)
    def _(b):
        slot = query_slot[b]
        out_ref[slot >> 1, :, half_at(slot)] = exact_ref[:, tile_at(b, BLOCK)].astype(low)


def self_backward_kernel(
    tile, plan, query_slot, key_slot, range_ref, own_ref, all_ref, grad_ref, exact_ref, lse_ref,
    dq_ref, dkv_ref, query_s, grad_s, key_s, keyt_s, value_s, dq_s, dk_s, dv_s,
):
    depth, queries = query_s.shape
    count = keyt_s.shape[1]

    @pl.loop(0, queries // BLOCK)
    def _(b):
        slot = query_slot[b]
        query_s[:, tile_at(b, BLOCK)] = own_ref[slot >> 1, 0:depth, half_at(slot)] * low(score_scale)
        grad_s[:, tile_at(b, BLOCK)] = grad_ref[slot >> 1, :, half_at(slot)]

    @pl.loop(0, count // BLOCK)
    def _(b):
        slot = key_slot[b]
        block = all_ref[slot >> 1, depth : 2 * depth, half_at(slot)]
        keyt_s[:, tile_at(b, BLOCK)] = block
        key_s[tile_at(b, BLOCK), :] = block.T
        value_s[tile_at(b, BLOCK), :] = all_ref[slot >> 1, 2 * depth : 3 * depth, half_at(slot)].T

    dk_s[...] = jnp.zeros_like(dk_s)
    dv_s[...] = jnp.zeros_like(dv_s)

    @pl.loop(0, queries // tile)
    def _(t):
        here = tile_at(t, tile)
        query, grad = query_s[:, here], grad_s[:, here]
        start, stop = range_ref[0:1, here], range_ref[1:2, here]
        lse = lse_ref[0:1, here]
        delta = jnp.sum(grad.astype(full) * exact_ref[:, here], axis=0, keepdims=True)

        def step(j, dq, masked):
            there = tile_at(j, tile)
            scores = contract(key_s[there, :], query, 1, 0)
            if masked:
                scores = masked_scores(scores, j, tile, start, stop)
            probs = jnp.exp(scores - lse)
            dprobs = contract(value_s[there, :], grad, 1, 0)
            dscores = (probs * (dprobs - delta)).astype(low)
            dv_s[:, there] += contract(grad, probs.astype(low), 1, 1)
            dk_s[:, there] += contract(query, dscores, 1, 1)
            return dq + contract(keyt_s[:, there], dscores, 1, 0)

        dq_s[:, here] = over_tiles(plan, t, step, jnp.zeros((depth, tile), full))

    @pl.loop(0, queries // BLOCK)
    def _(b):
        slot = query_slot[b]
        dq_ref[slot >> 1, :, half_at(slot)] = (dq_s[:, tile_at(b, BLOCK)] * score_scale).astype(low)

    @pl.loop(0, count // BLOCK)
    def _(b):
        slot = key_slot[b]
        dkv_ref[slot >> 1, 0:depth, half_at(slot)] = dk_s[:, tile_at(b, BLOCK)].astype(dkv_ref.dtype)
        dkv_ref[slot >> 1, depth : 2 * depth, half_at(slot)] = dv_s[:, tile_at(b, BLOCK)].astype(dkv_ref.dtype)


def one_head(values, head, depth):
    rows = lax.broadcasted_iota(jnp.int32, values.shape, 0)
    inside = (rows >= head * depth) & (rows < (head + 1) * depth)
    return jnp.where(inside, values, jnp.zeros_like(values))


def cross_forward_kernel(
    tile, plan, range_ref, query_ref, key_ref, value_ref, out_ref, exact_ref, lse_ref, value_s
):
    count = value_s.shape[1]
    depth = value_s.shape[0] // 2

    @pl.loop(0, count // BLOCK)
    def _(b):
        value_s[:, tile_at(b, BLOCK)] = value_ref[tile_at(b, BLOCK), :].T

    query = query_ref[...] * low(score_scale)
    for head in range(2):
        rows = pl.ds(head * depth, depth)
        result, lse = forward_tiles(
            plan, 0, one_head(query, head, depth), range_ref[0:1, :], range_ref[1:2, :],
            lambda j: key_ref[tile_at(j, tile), :],
            lambda j, rows=rows: value_s[rows, tile_at(j, tile)],
            tile, depth,
        )
        exact_ref[rows, :] = result
        out_ref[rows, :] = result.astype(low)
        lse_ref[0, head : head + 1, :] = lse


def cross_backward_kernel(
    tile, plan, range_ref, query_ref, key_ref, value_ref, grad_ref, exact_ref, lse_ref,
    dq_ref, dkv_ref, keyt_s, dk_s, dv_s,
):
    count = keyt_s.shape[1]
    depth = keyt_s.shape[0] // 2
    width = query_ref.shape[1]

    @pl.loop(0, count // BLOCK)
    def _(b):
        keyt_s[:, tile_at(b, BLOCK)] = key_ref[tile_at(b, BLOCK), :].T

    dk_s[...] = jnp.zeros_like(dk_s)
    dv_s[...] = jnp.zeros_like(dv_s)
    start, stop = range_ref[0:1, :], range_ref[1:2, :]
    all_query = query_ref[...] * low(score_scale)
    for head in range(2):
        rows = pl.ds(head * depth, depth)
        query = one_head(all_query, head, depth)
        grad = one_head(grad_ref[...], head, depth)
        lse = lse_ref[0, head : head + 1, :]
        delta = jnp.sum(grad_ref[rows, :].astype(full) * exact_ref[rows, :], axis=0, keepdims=True)

        def step(j, dq, masked, rows=rows, query=query, grad=grad, lse=lse, delta=delta):
            there = tile_at(j, tile)
            scores = contract(key_ref[there, :], query, 1, 0)
            if masked:
                scores = masked_scores(scores, j, tile, start, stop)
            probs = jnp.exp(scores - lse)
            dprobs = contract(value_ref[there, :], grad, 1, 0)
            dscores = (probs * (dprobs - delta)).astype(low)
            dv_s[there, :] += contract(probs.astype(low), grad, 1, 1)
            dk_s[there, :] += contract(dscores, query, 1, 1)
            return dq + contract(keyt_s[rows, there], dscores, 1, 0)

        dq = over_tiles(plan, 0, step, jnp.zeros((depth, width), full))
        dq_ref[rows, :] = (dq * score_scale).astype(low)
    parts, _, part_rows, _ = dkv_ref.shape
    dkv_ref[:, 0] = dk_s[...].astype(low).reshape(parts, part_rows, 2 * depth)
    dkv_ref[:, 1] = dv_s[...].astype(low).reshape(parts, part_rows, 2 * depth)


def smem():
    return pl.BlockSpec(memory_space=pltpu.SMEM)


def vmem():
    return pl.BlockSpec(memory_space=pltpu.VMEM)


def params():
    return pltpu.CompilerParams(vmem_limit_bytes=VMEM_BYTES)


def self_tile(queries):
    return min(512, queries)


def self_forward(plan, query_slot, key_slot, ranges, own, everyone):
    heads, three, rows = own.shape
    depth = three // 3
    queries, count = heads * rows, everyone.shape[0] * rows
    tile = self_tile(queries)
    return pl.pallas_call(
        functools.partial(self_forward_kernel, tile),
        out_shape=(
            jax.ShapeDtypeStruct((heads, depth, rows), low),
            jax.ShapeDtypeStruct((depth, queries), full),
            jax.ShapeDtypeStruct((8, queries), full),
        ),
        in_specs=[smem()] * 3 + [vmem()] * 3,
        out_specs=(vmem(),) * 3,
        scratch_shapes=[
            pltpu.VMEM((depth, queries), low),
            pltpu.VMEM((count, depth), low),
            pltpu.VMEM((depth, count), low),
        ],
        compiler_params=params(),
        cost_estimate=pl.CostEstimate(
            flops=queries * count * 400, bytes_accessed=queries * 3000, transcendentals=0
        ),
        name="self_forward",
    )(plan, query_slot, key_slot, ranges, own, everyone)


def self_backward(plan, query_slot, key_slot, ranges, own, everyone, grad, exact, lse, kv_type):
    heads, three, rows = own.shape
    depth = three // 3
    queries, count = heads * rows, everyone.shape[0] * rows
    tile = self_tile(queries)
    return pl.pallas_call(
        functools.partial(self_backward_kernel, tile),
        out_shape=(
            jax.ShapeDtypeStruct((heads, depth, rows), low),
            jax.ShapeDtypeStruct((everyone.shape[0], 2 * depth, rows), kv_type),
        ),
        in_specs=[smem()] * 3 + [vmem()] * 6,
        out_specs=(vmem(),) * 2,
        scratch_shapes=[
            pltpu.VMEM((depth, queries), low),
            pltpu.VMEM((depth, queries), low),
            pltpu.VMEM((count, depth), low),
            pltpu.VMEM((depth, count), low),
            pltpu.VMEM((count, depth), low),
            pltpu.VMEM((depth, queries), full),
            pltpu.VMEM((depth, count), full),
            pltpu.VMEM((depth, count), full),
        ],
        compiler_params=params(),
        cost_estimate=pl.CostEstimate(
            flops=queries * count * 1000, bytes_accessed=queries * 6000, transcendentals=0
        ),
        name="self_backward",
    )(plan, query_slot, key_slot, ranges, own, everyone, grad, exact, lse)


def cross_tile(count):
    return min(512, count)


def pair_spec(rows, cols):
    return pl.BlockSpec((rows, cols), lambda i: (i, 0))


def cross_forward(plan, ranges, query, keys_values):
    width, rows = query.shape
    count = keys_values.shape[0]
    pairs = H // 2
    wide = width // pairs
    return pl.pallas_call(
        functools.partial(cross_forward_kernel, cross_tile(count)),
        grid=(pairs,),
        out_shape=(
            jax.ShapeDtypeStruct((width, rows), low),
            jax.ShapeDtypeStruct((width, rows), full),
            jax.ShapeDtypeStruct((pairs, 8, rows), full),
        ),
        in_specs=[
            smem(),
            vmem(),
            pair_spec(wide, rows),
            pl.BlockSpec((count, wide), lambda i: (0, i)),
            pl.BlockSpec((count, wide), lambda i: (0, pairs + i)),
        ],
        out_specs=(
            pair_spec(wide, rows),
            pair_spec(wide, rows),
            pl.BlockSpec((1, 8, rows), lambda i: (i, 0, 0)),
        ),
        scratch_shapes=[pltpu.VMEM((wide, count), low)],
        compiler_params=params(),
        cost_estimate=pl.CostEstimate(
            flops=rows * count * width * 8, bytes_accessed=count * width * 4, transcendentals=0
        ),
        name="cross_forward",
    )(plan, ranges, query, keys_values, keys_values)


def cross_backward(plan, ranges, query, keys_values, grad, exact, lse, parts):
    width, rows = query.shape
    count = keys_values.shape[0]
    pairs = H // 2
    wide = width // pairs
    return pl.pallas_call(
        functools.partial(cross_backward_kernel, cross_tile(count)),
        grid=(pairs,),
        out_shape=(
            jax.ShapeDtypeStruct((width, rows), low),
            jax.ShapeDtypeStruct((parts, 2, count // parts, width), low),
        ),
        in_specs=[
            smem(),
            vmem(),
            pair_spec(wide, rows),
            pl.BlockSpec((count, wide), lambda i: (0, i)),
            pl.BlockSpec((count, wide), lambda i: (0, pairs + i)),
            pair_spec(wide, rows),
            pair_spec(wide, rows),
            pl.BlockSpec((1, 8, rows), lambda i: (i, 0, 0)),
        ],
        out_specs=(
            pair_spec(wide, rows),
            pl.BlockSpec((parts, 2, count // parts, wide), lambda i: (0, 0, 0, i)),
        ),
        scratch_shapes=[
            pltpu.VMEM((wide, count), low),
            pltpu.VMEM((count, wide), full),
            pltpu.VMEM((count, wide), full),
        ],
        compiler_params=params(),
        cost_estimate=pl.CostEstimate(
            flops=rows * count * width * 20, bytes_accessed=count * width * 8, transcendentals=0
        ),
        name="cross_backward",
    )(plan, ranges, query, keys_values, keys_values, grad, exact, lse)


class Exchange:
    def __init__(self):
        self.fsdp = lax.axis_size("fsdp")
        self.chips = lax.axis_size(CHIP)
        self.core = lax.axis_index("core")
        self.row = lax.axis_index("fsdp")
        self.chip = lax.axis_index(CHIP)
        self.paired = self.fsdp == 2
        self.cube = self.paired and self.chips == 8

    def swap(self, value, axis):
        return lax.ppermute(value, axis, [(0, 1), (1, 0)])

    def swap_chip(self, value, bit):
        return lax.ppermute(value, CHIP, [(i, i ^ bit) for i in range(self.chips)])

    def gather_weight(self, shard):
        piece = shard.shape[0] // 2
        mine = lax.dynamic_slice_in_dim(shard, self.core * piece, piece, 0)
        return lax.all_gather(mine, ("fsdp", "core"), axis=0, tiled=True)

    def gather_last(self, shard):
        if not self.paired:
            return lax.all_gather(shard, "fsdp", axis=shard.ndim - 1, tiled=True)
        other = self.swap(shard, "fsdp")
        return jnp.where(
            self.row == 0,
            jnp.concatenate([shard, other], axis=-1),
            jnp.concatenate([other, shard], axis=-1),
        )

    def up_slice(self, shard):
        rows, hidden = shard.shape
        wide = hidden // (2 * self.fsdp)
        if not self.paired:
            split = shard.reshape(rows, self.fsdp, 2, wide)
            mine = lax.dynamic_index_in_dim(split, self.core, 2, keepdims=False)
            return lax.all_to_all(mine, "fsdp", 1, 0, tiled=True).reshape(rows * self.fsdp, wide)
        sent = lax.dynamic_slice_in_dim(shard, (2 * (1 - self.row) + self.core) * wide, wide, 1)
        kept = lax.dynamic_slice_in_dim(shard, (2 * self.row + self.core) * wide, wide, 1)
        other = self.swap(sent, "fsdp")
        whole = jnp.concatenate([kept, kept], axis=0)
        return lax.dynamic_update_slice_in_dim(whole, other, (1 - self.row) * rows, 0)

    def quad_gather(self, value):
        if not self.paired:
            return lax.all_gather(value, QUAD, axis=0, tiled=True)
        across = self.swap(value, "fsdp")
        beside = self.swap(value, "core")
        corner = self.swap(across, "core")
        return jnp.concatenate([value, beside, across, corner], axis=0)

    def quad_sum(self, value):
        if not self.paired:
            return lax.psum_scatter(value, QUAD, scatter_dimension=0, tiled=True).astype(full)
        rows = value.shape[0] // 4
        parts = value.reshape(2, 2, rows, value.shape[1])
        theirs = self.swap(parts[:, 1], "core")
        both = parts[:, 0].astype(full) + theirs.astype(full)
        return both[0] + self.swap(both[1].astype(low), "fsdp").astype(full)

    def halve(self, value, axis, bit, swap):
        kept = lax.dynamic_index_in_dim(value, bit, axis, keepdims=False)
        sent = lax.dynamic_index_in_dim(value, 1 - bit, axis, keepdims=False)
        return kept.astype(full) + swap(sent).astype(full)

    def chip_sum(self, value):
        if not self.cube:
            return lax.psum_scatter(value, CHIP, scatter_dimension=0, tiled=True).astype(full)
        rows = value.shape[0] // 8
        value = value.reshape((2, 2, 2, rows) + value.shape[1:])
        value = self.halve(value, 2, self.chip & 1, lambda v: self.swap_chip(v, 1)).astype(low)
        value = self.halve(value, 1, (self.chip >> 1) & 1, lambda v: self.swap_chip(v, 2)).astype(low)
        return self.halve(value, 0, self.chip >> 2, lambda v: self.swap_chip(v, 4))

    def device_sum(self, values):
        count = len(values)
        rows, cols = values[0].shape
        share = rows // (self.chips * 2 * self.fsdp)
        shape = (self.chips, 2, self.fsdp, share, cols)
        if not self.cube:
            stacked = jnp.stack([v.reshape(shape) for v in values], axis=3)
            stacked = lax.psum_scatter(stacked, "core", scatter_dimension=1, tiled=True)
            stacked = lax.psum_scatter(stacked, "fsdp", scatter_dimension=2, tiled=True)
            stacked = lax.psum_scatter(stacked, CHIP, scatter_dimension=0, tiled=True)
            return [stacked[0, 0, 0, i].astype(full) for i in range(count)]
        halves = [
            self.halve(v.reshape(shape), 1, self.core, lambda u: self.swap(u, "core")).astype(low)
            for v in values
        ]
        stacked = jnp.stack(halves, axis=2)
        stacked = self.halve(stacked, 1, self.row, lambda u: self.swap(u, "fsdp")).astype(low)
        summed = self.chip_sum(stacked)[0]
        return [summed[i] for i in range(count)]

    def to_owner(self, value):
        chips, fsdp = self.chips, self.fsdp
        moves = []
        for chip in range(chips):
            for core in range(2):
                for row in range(fsdp):
                    moves.append(
                        ((chip * 2 + core) * fsdp + row, (row * 2 + core) * chips + chip)
                    )
        return lax.ppermute(value, ALL, moves)

    def quad_columns(self, value):
        quad = 2 * self.fsdp
        rows, wide = value.shape
        share = rows // quad
        if not self.paired:
            value = lax.all_to_all(value, QUAD, 0, 1, tiled=True)
            value = value.reshape(share, 2, self.fsdp, wide).transpose(0, 2, 1, 3)
            return value.reshape(share, quad * wide)
        value = value.reshape(2, 2, share, wide)
        core, row = self.core, self.row

        def block(c, f):
            part = lax.dynamic_index_in_dim(value, c, 0, keepdims=False)
            return lax.dynamic_index_in_dim(part, f, 0, keepdims=False)

        got = [
            block(core, row),
            self.swap(block(1 - core, row), "core"),
            self.swap(block(core, 1 - row), "fsdp"),
            lax.ppermute(block(1 - core, 1 - row), QUAD, [(i, 3 - i) for i in range(4)]),
        ]
        got = [jnp.where(core == 0, got[i], got[i ^ 1]) for i in range(4)]
        got = [jnp.where(row == 0, got[i], got[i ^ 2]) for i in range(4)]
        return jnp.concatenate(got, axis=1)


def per_device(
    tokens, encoder, cotangent, seq_lengths, source_lengths, pair_order, pair_flip,
    ln_gain, ln_bias, attn_bias, self_qkv, self_out, cross_q, cross_kv, cross_out,
    w_up, up_bias, w_down, down_bias,
):
    move = Exchange()
    resid = tokens[0].astype(full)
    source = encoder[0]
    grad_low = cotangent[0]
    rows, width = resid.shape
    src_rows = source.shape[0]
    depth = width // H
    ctx_count = lax.axis_size(CTX)
    parts = lax.axis_size("part")
    devices = ctx_count * move.fsdp
    here = lax.axis_index(CTX)
    part = lax.axis_index("part")

    blocks = block_numbers(pair_order[0], pair_flip[0])
    lengths, src_lengths = seq_lengths[0], source_lengths[0]
    offsets = jnp.arange(BLOCK, dtype=jnp.int32)
    part_blocks = lax.dynamic_slice_in_dim(blocks, part * (blocks.shape[0] // parts), blocks.shape[0] // parts)
    query_slot, key_slot = sorted_slots(part_blocks), sorted_slots(blocks)
    query_places = (jnp.sort(part_blocks) if parts > 1 else jnp.arange(part_blocks.shape[0], dtype=jnp.int32))
    query_places = (query_places[:, None] * BLOCK + offsets[None, :]).reshape(-1)
    self_start = document_starts(query_places, lengths)
    self_stop = query_places + 1
    tile = self_tile(query_places.shape[0])
    self_plan = tile_plan(self_start, self_stop, tile, tile)
    self_ranges = jnp.stack([self_start, self_stop])
    my_blocks = lax.dynamic_slice_in_dim(blocks, here * (rows // BLOCK), rows // BLOCK)
    my_places = (my_blocks[:, None] * BLOCK + offsets[None, :]).reshape(-1)
    cross_start, cross_stop = source_range(my_places, lengths, src_lengths)
    cross_plan = tile_plan(cross_start, cross_stop, rows, cross_tile(src_rows * ctx_count))
    cross_ranges = jnp.stack([cross_start, cross_stop])

    small = jnp.concatenate(
        [ln_gain, ln_bias, attn_bias.reshape(6, -1), down_bias[None]], axis=0
    )
    small = move.gather_last(small).astype(full)
    gains, shifts, biases, bias_down = small[0:3], small[3:6], small[6:12].reshape(2, 3, width), small[12]
    w_qkv = move.gather_weight(self_qkv)
    w_ckv = move.gather_weight(cross_kv)
    w_out = move.gather_weight(self_out)
    w_cq = move.gather_weight(cross_q)
    w_cout = move.gather_weight(cross_out)
    w_upper = move.up_slice(w_up)
    wide = w_upper.shape[1]
    w_lower = lax.dynamic_slice_in_dim(w_down, move.core * wide, wide, 0)
    bias_up = lax.dynamic_slice_in_dim(up_bias, move.core * wide, wide, 0).astype(full)

    norm_one, back_one = jax.vjp(layer_norm, resid, gains[0], shifts[0])
    normed_one = norm_one.astype(low)
    projected = contract(w_qkv, normed_one, 0, 1)
    shift_qkv = jnp.concatenate([biases[0, 0], jnp.zeros((width,), full), biases[0, 1]])
    projected = (projected + shift_qkv[:, None]).astype(low)
    projected = projected.reshape(3, H, depth, rows).transpose(1, 0, 2, 3).reshape(H, 3 * depth, rows)
    own_heads = lax.all_to_all(projected, HEADS, 0, 0, tiled=True)
    all_heads = own_heads if parts == 1 else lax.all_gather(own_heads, "part", axis=0, tiled=True)
    self_args = (self_plan, query_slot, key_slot, self_ranges, own_heads, all_heads)
    self_low, self_exact, self_lse = self_forward(*self_args)
    self_att = lax.all_to_all(self_low, HEADS, 0, 0, tiled=True).reshape(width, rows)
    mixed_one = resid + contract(self_att, w_out, 0, 0) + biases[0, 2]

    src_proj = jnp.dot(source, w_ckv, preferred_element_type=full)
    shift_ckv = jnp.concatenate([jnp.zeros((width,), full), biases[1, 1]])
    src_kv = lax.all_gather((src_proj + shift_ckv).astype(low), CTX, axis=0, tiled=True)

    norm_two, back_two = jax.vjp(layer_norm, mixed_one, gains[1], shifts[1])
    normed_two = norm_two.astype(low)
    cross_query = (contract(w_cq, normed_two, 0, 1) + biases[1, 0][:, None]).astype(low)
    cross_att, cross_exact, cross_lse = cross_forward(cross_plan, cross_ranges, cross_query, src_kv)
    mixed_two = mixed_one + contract(cross_att, w_cout, 0, 0) + biases[1, 2]

    norm_three, back_three = jax.vjp(layer_norm, mixed_two, gains[2], shifts[2])
    grad_quad = move.quad_gather(grad_low)
    quad_three = move.quad_gather(norm_three.astype(low))
    hidden_pre = jnp.dot(quad_three, w_upper, preferred_element_type=full) + bias_up
    activated, back_gelu = jax.vjp(gelu_tanh, hidden_pre)
    act_low = activated.astype(low)
    branch = jnp.dot(act_low, w_lower, preferred_element_type=full).astype(low)
    result = mixed_two + move.quad_sum(branch) + bias_down

    grad_out = grad_low.astype(full)
    grad_b_lower = column_sums(grad_low)
    grad_w_lower = contract(act_low, grad_quad, 0, 0).astype(low)
    lower_own = move.to_owner(move.chip_sum(grad_w_lower).astype(low)).astype(full)
    grad_act = contract(grad_quad, w_lower, 1, 1)
    grad_hidden = back_gelu(grad_act)[0].astype(low)
    grad_b_upper = column_sums(grad_hidden)
    grad_three = move.quad_sum(contract(grad_hidden, w_upper, 1, 1).astype(low))
    grad_w_upper = contract(quad_three, grad_hidden, 0, 0).astype(low)
    upper_own = move.quad_columns(move.chip_sum(grad_w_upper).astype(low)).astype(full)
    grad_ln_three, gain_three, shift_three = back_three(grad_three)
    grad_two = grad_out + grad_ln_three

    grad_two_low = grad_two.astype(low)
    grad_b_cout = column_sums(grad_two_low)
    grad_cross_att = contract(w_cout, grad_two_low, 1, 1).astype(low)
    grad_w_cout = contract(cross_att, grad_two_low, 1, 0).astype(low)
    grad_cq, cross_dkv = cross_backward(
        cross_plan, cross_ranges, cross_query, src_kv, grad_cross_att, cross_exact, cross_lse, ctx_count
    )
    own_dkv = lax.psum_scatter(cross_dkv, CTX, scatter_dimension=0, tiled=True)[0]
    grad_source = contract(own_dkv[0], w_ckv[:, :width], 1, 1) + contract(own_dkv[1], w_ckv[:, width:], 1, 1)
    grad_b_cv = column_sums(own_dkv[1])
    grad_b_cq = jnp.sum(grad_cq.astype(full), axis=1)
    grad_w_cq = contract(normed_two, grad_cq, 0, 1).astype(low)
    grad_ln_two, gain_two, shift_two = back_two(contract(grad_cq, w_cq, 0, 1))
    grad_one = grad_two + grad_ln_two

    grad_one_low = grad_one.astype(low)
    grad_b_out = column_sums(grad_one_low)
    grad_self_att = contract(w_out, grad_one_low, 1, 1).astype(low).reshape(H, depth, rows)
    grad_heads = lax.all_to_all(grad_self_att, HEADS, 0, 0, tiled=True)
    grad_w_out = contract(self_att, grad_one_low, 1, 0).astype(low)
    cout_own, cq_own, out_own = move.device_sum([grad_w_cout, grad_w_cq, grad_w_out])
    head_dq, head_dkv = self_backward(
        *self_args, grad_heads, self_exact, self_lse, low if parts == 1 else full
    )
    if parts > 1:
        head_dkv = lax.psum_scatter(head_dkv, "part", scatter_dimension=0, tiled=True).astype(low)
    head_grad = jnp.concatenate([head_dq, head_dkv], axis=1)
    grad_qkv = lax.all_to_all(head_grad, HEADS, 0, 0, tiled=True)
    grad_qkv = grad_qkv.reshape(H, 3, depth, rows).transpose(1, 0, 2, 3).reshape(3 * width, rows)
    sums = jnp.sum(grad_qkv.astype(full), axis=1).reshape(3, width)
    grad_ln_one, gain_one, shift_one = back_one(contract(grad_qkv, w_qkv, 0, 1))
    grad_input = grad_one + grad_ln_one

    group_one = lax.all_gather(normed_one, HEADS, axis=0, tiled=True)
    group_source = lax.all_gather(source, HEADS, axis=0, tiled=True)
    head_rows = head_grad.transpose(1, 0, 2).reshape(3 * depth, H * rows)
    head_w = contract(group_one, head_rows, 0, 1)
    pieces = own_dkv.reshape(2, src_rows, H, depth).transpose(2, 1, 0, 3).reshape(H, src_rows, 2 * depth)
    pieces = lax.all_to_all(pieces, HEADS, 0, 0, tiled=True).reshape(H * src_rows, 2 * depth)
    head_c = contract(group_source, pieces, 0, 0)
    head_all = jnp.concatenate([head_w, head_c], axis=1).astype(low)
    cols = head_all.shape[1]
    share = width // devices

    vectors = jnp.stack(
        [gain_one, gain_two, gain_three, shift_one, shift_two, shift_three,
         sums[0], sums[2], grad_b_out, grad_b_cq, grad_b_cv, grad_b_cout, grad_b_lower]
    )
    vectors = vectors.reshape(13, devices, share).transpose(1, 0, 2).reshape(devices, 13 * share)
    hidden = wide * 2 * move.fsdp
    upper_sums = lax.dynamic_update_slice_in_dim(
        jnp.zeros((hidden,), full), grad_b_upper, (move.row * 2 + move.core) * wide, 0
    ).reshape(devices, hidden // devices)
    vectors = jnp.concatenate([vectors, upper_sums], axis=1)
    used = vectors.shape[1]
    extra = -(-used // cols)
    vectors = jnp.pad(vectors, ((0, 0), (0, extra * cols - used))).reshape(devices, extra, cols)
    outgoing = jnp.concatenate([head_all.reshape(devices, share, cols), vectors.astype(low)], axis=1)
    incoming = lax.all_to_all(outgoing, ALL, 0, 0, tiled=True)
    heads_in = incoming[:, :share].reshape(parts, H, move.fsdp, share, cols)
    heads_in = jnp.sum(heads_in.astype(full), axis=(0, 2))
    qkv_own = heads_in[:, :, : 3 * depth].reshape(H, share, 3, depth).transpose(1, 2, 0, 3).reshape(share, 3 * width)
    ckv_own = heads_in[:, :, 3 * depth :].reshape(H, share, 2, depth).transpose(1, 2, 0, 3).reshape(share, 2 * width)
    tail = jnp.sum(incoming[:, share:].astype(full), axis=0).reshape(-1)
    vec = tail[: 13 * share].reshape(13, share)
    bup_own = tail[13 * share : used]
    return (
        result.astype(low)[None],
        grad_input[None],
        grad_source[None],
        vec[0:3],
        vec[3:6],
        vec[6:12].reshape(2, 3, share),
        qkv_own,
        out_own,
        cq_own,
        ckv_own,
        cout_own,
        upper_own,
        bup_own,
        lower_own,
        vec[12],
    )


def solution(mesh):
    ctx, fsdp = mesh.shape["ctx"], mesh.shape["fsdp"]
    inner = Mesh(mesh.devices.reshape(ctx // H, H // 2, 2, fsdp), ALL)
    tokens = P("fsdp", CTX, None)
    group = P("fsdp", None)
    owned = P(ALL, None)
    return jax.shard_map(
        per_device,
        mesh=inner,
        in_specs=(tokens,) * 3
        + (group,) * 4
        + (P(None, "fsdp"), P(None, "fsdp"), P(None, None, "fsdp"))
        + (group,) * 6
        + (P("fsdp"), group, P("fsdp")),
        out_specs=(tokens,) * 3
        + (P(None, ALL), P(None, ALL), P(None, None, ALL))
        + (owned,) * 6
        + (P(ALL), owned, P(ALL)),
        check_vma=False,
    )
```

time: 3940 us -> 843 us (0.21)
  waiting for transfers between devices: 3320 us -> 358 us
  matrix products: 289 us -> 102 us
  Pallas kernels: 0 us -> 140 us
  local copies, waits for them, and re-layouts: 174 us -> 108 us
  blocking collectives: 62.1 us -> 0 us
  starting transfers between devices: 1.14 us -> 60.2 us
    reduce_scatter x7 -> x1, waiting for transfers between devices: 2180 us -> 0.01 us  [per_device(): lax.psum_scatter(cross_dkv, CTX, scatter_dimension=0, tiled=True)[0]]
    all_gather x11 -> x8, waiting for transfers between devices: 692 us -> 102 us  [the longest x5 70.9 us: gather_weight(): return lax.all_gather(mine, ('fsdp', 'core'), axis=0, tiled=True)]
    unnamed x28 -> x9, waiting for transfers between devices: 446 us -> 0.81 us
    ppermute x0 -> x29, waiting for transfers between devices: none -> 205 us  [the longest x9 161 us: swap_chip(): return lax.ppermute(value, CHIP, [(i, i ^ bit) for i in range(self.chips)])]
    dot_general x105 -> x22, matrix products: 289 us -> 102 us  [the longest x19 80.8 us: contract(): lax.dot_general(left, right, (((left_dim,), (right_dim,)), ((), ())), pre...]
    pallas_call x0 -> x4, Pallas kernels: none -> 140 us  [the longest x1 47 us: cross_backward(): pl.pallas_call(functools.partial(cross_backward_kernel, cross_tile(count)...]
    unnamed x172 -> x137, local copies, waits for them, and re-layouts: 79.9 us -> 21.8 us
    all_to_all x0 -> x6, waiting for transfers between devices: none -> 50.1 us  [the longest x1 27.7 us: per_device(): own_heads = lax.all_to_all(projected, HEADS, 0, 0, tiled=True)]
  transfers between devices with their start and end apart: 23 -> 44, of which waited for: 18 -> 18; matrix products, arithmetic and copies ran while one was open for 10% -> 27% of each run, Pallas kernels for 0% -> 17%
where the time goes in v1:
time: 843 us; the launch traced here: 834 us
  waiting for transfers between devices  358 us (42%)
  Pallas kernels  140 us (17%)
  local copies, waits for them, and re-layouts  108 us (13%)
  matrix products  102 us (12%)
  starting transfers between devices  60.2 us (7%)
  other arithmetic  43.3 us (5%)
  between operations  22.1 us (3%)
    ppermute x9, waiting for transfers between devices, swap_chip(): return lax.ppermute(value, CHIP, [(i, i ^ bit) for i in range(self.chips)])  161 us
    dot_general x19, matrix products, contract(): lax.dot_general(left, right, (((left_dim,), (right_dim,)), ((), ())), pre...  80.8 us
    all_gather x5, waiting for transfers between devices, gather_weight(): return lax.all_gather(mine, ('fsdp', 'core'), axis=0, tiled=True)  70.9 us
    pallas_call x1, Pallas kernels, cross_backward(): pl.pallas_call(functools.partial(cross_backward_kernel, cross_tile(count)...  47 us
    ppermute x18, waiting for transfers between devices, swap(): return lax.ppermute(value, axis, [(0, 1), (1, 0)])  44.8 us
    pallas_call x1, Pallas kernels, cross_forward(): pl.pallas_call(functools.partial(cross_forward_kernel, cross_tile(count))...  44.2 us
    all_gather x1, waiting for transfers between devices, per_device(): lax.all_gather((src_proj + shift_ckv).astype(low), CTX, axis=0, tiled=True)  31 us
    all_to_all x1, waiting for transfers between devices, per_device(): own_heads = lax.all_to_all(projected, HEADS, 0, 0, tiled=True)  27.7 us
  transfers between devices with their start and end apart: 44, of which 18 were waited for; matrix products, arithmetic and copies ran while one was open for 27% of the time, Pallas kernels for 17%

profile of v1, /device:TPU:0, one launch (start us, length us, event | category | flops | bytes accessed | tf_op | source)
XLA Modules:
  0.0 834.0 jit_solution(5593528672743359767)
XLA Ops:
  19.1 28.3 %all-gather.16.cloned.1.call-done = bf16[1024,2048]{1,0:T(8,128)(2,1)} async-done(((bf16[256,2048]{1,0:T(8,128)(2,1)}), bf16[1024,2048]{1,0:T(8,128)(2,1)}) %all-gather.16.cloned.1.call-update) | async-done | bytes 4194320 | tf_op jit(solution)/shard_map/all_gather | solution.py:476
  52.8 42.6 %all-gather.10.cloned.1.call-done = bf16[1024,3072]{1,0:T(8,128)(2,1)} async-done(((bf16[256,3072]{1,0:T(8,128)(2,1)}), bf16[1024,3072]{1,0:T(8,128)(2,1)}) %all-gather.10.cloned.1.call-update) | async-done | bytes 6291472 | tf_op jit(solution)/shard_map/all_gather | solution.py:476
  111.8 27.7 %all-to-all-done.own_ref.all_ref = bf16[16,192,256]{2,1,0:T(8,128)(2,1)S(1)} async-done(((bf16[16,192,256]{2,1,0:T(8,128)(2,1)}), bf16[16,192,256]{2,1,0:T(8,128)(2,1)S(1)}, u32[]{:S(2)}, u32[]{:S(2)}) %all-to-all-start) | async-done | bytes 1572896 | tf_op jit(solution)/shard_map/all_to_all | solution.py:646
  140.6 21.9 %self_forward.1 = (bf16[16,64,256]{2,1,0:T(8,128)(2,1)}, f32[64,4096]{1,0:T(8,128)}, f32[8,4096]{1,0:T(8,128)}) custom-call(s32[4,8]{1,0:T(4,128)} %pad_add_fusion.1.plan, s32[32]{0:T(128)} %select_reduce_fusion.query_slot.key_slot, s32[32]{0:T(128)} %select_reduce_fusion.query_slot.key_slot, s32[2,4096]{1,0:T(2,128)} %pad_add_fusion.range_ref, ...), custom_call_target="tpu_custom_call" | custom-call | flops 6710886400 | bytes 12288000 | tf_op jit(solution)/shard_map/self_forward/pallas_call | solution.py:323
  162.5 9.1 %all-to-all-start.1 = ((bf16[16,64,256]{2,1,0:T(8,128)(2,1)}), bf16[16,64,256]{2,1,0:T(8,128)(2,1)S(1)}, u32[]{:S(2)}, u32[]{:S(2)}) async-start(bf16[16,64,256]{2,1,0:T(8,128)(2,1)} %get-tuple-element.25), calls=%async_computation.1 | async-start | bytes 1048576 | tf_op jit(solution)/shard_map/all_to_all | solution.py:650
  194.6 31.0 %all-gather.18.cloned.1.call-done.key_ref.value_ref = bf16[2048,2048]{1,0:T(8,128)(2,1)} async-done(((bf16[128,2048]{1,0:T(8,128)(2,1)}), bf16[2048,2048]{1,0:T(8,128)(2,1)}) %all-gather.18.cloned.1.call-update) | async-done | bytes 8388624 | tf_op jit(solution)/shard_map/all_gather | solution.py:655
  225.6 44.2 %cross_forward.1 = (bf16[1024,256]{1,0:T(8,128)(2,1)}, f32[1024,256]{1,0:T(8,128)}, f32[8,8,256]{2,1,0:T(8,128)}) custom-call(s32[4,1]{1,0:T(4,128)} %copy.127.plan, s32[2,256]{1,0:T(2,128)} %pad_add_fusion.2.range_ref, bf16[1024,256]{1,0:T(8,128)(2,1)} %fusion.40.query_ref, bf16[2048,2048]{1,0:T(8,128)(2,1)} %all-gather.18.cloned.1.call-done.key_ref.value_ref, ...), custom_call_target="tpu_custom_call" | custom-call | flops 4294967296 | bytes 8388608 | tf_op jit(solution)/shard_map/cross_forward/pallas_call | solution.py:389
  276.4 12.5 %collective-permute-done.2 = bf16[256,1024]{1,0:T(8,128)(2,1)} collective-permute-done((bf16[256,1024]{1,0:T(8,128)(2,1)}, bf16[256,1024]{1,0:T(8,128)(2,1)}, u32[]{:S(2)}, u32[]{:S(2)}) %collective-permute-start.2) | collective-permute-done | bytes 524320 | tf_op jit(solution)/shard_map/ppermute | solution.py:468
  291.5 8.0 collective-permute-done.8
  301.6 8.3 fusion.75
  310.0 16.0 %convert_reduce_fusion = (bf16[2048]{0:T(1024)(128)(2,1)S(1)}, bf16[1024,2048]{1,0:T(8,128)(2,1)}) fusion(bf16[4096,1024]{1,0:T(8,128)(2,1)S(1)} %bitcast.435, s32[]{:T(128)S(6)} %select_n.281, bf16[256,1024]{1,0:T(8,128)(2,1)S(1)} %collective-permute-done.9, bf16[256,1024]{1,0:T(8,128)(2,1)} %collective-permute-done.8, ...), kind=kOutput, calls=%fused_computation.10 | convolution fusion | flops 4359976960 | bytes 18886660 | tf_op jit(solution)/shard_map/dot_general | solution.py:38
  333.6 8.8 %fusion.29 = bf16[1024,1024]{1,0:T(8,128)(2,1)S(1)} fusion(bf16[4096,1024]{1,0:T(8,128)(2,1)S(1)} %bitcast.435, s32[]{:T(128)S(6)} %select_n.281, f32[1024,2048]{1,0:T(8,128)} %fusion.75, f32[2048]{0:T(1024)S(1)} %dynamic-slice_convert_fusion), kind=kOutput, calls=%fused_computation.54 | convolution fusion | flops 4316987392 | bytes 14688260 | tf_op jit(solution)/shard_map/dot_general | solution.py:669
  346.5 11.4 %collective-permute-done.11 = bf16[256,1024]{1,0:T(8,128)(2,1)S(1)} collective-permute-done((bf16[256,1024]{1,0:T(8,128)(2,1)S(1)}, bf16[256,1024]{1,0:T(8,128)(2,1)S(1)}, u32[]{:S(2)}, u32[]{:S(2)}) %collective-permute-start.11) | collective-permute-done | bytes 524320 | tf_op jit(solution)/shard_map/ppermute | solution.py:468
  358.4 10.2 %collective-permute-done.6 = bf16[256,1024]{1,0:T(8,128)(2,1)S(1)} collective-permute-done((bf16[256,1024]{1,0:T(8,128)(2,1)S(1)}, bf16[256,1024]{1,0:T(8,128)(2,1)S(1)}, u32[]{:S(2)}, u32[]{:S(2)}) %collective-permute-start.6) | collective-permute-done | bytes 524320 | tf_op jit(solution)/shard_map/ppermute | solution.py:468
  371.9 47.0 %cross_backward.1 = (bf16[1024,256]{1,0:T(8,128)(2,1)}, bf16[16,2,128,1024]{3,2,1,0:T(8,128)(2,1)}) custom-call(s32[4,1]{1,0:T(4,128)} %copy.127.plan, s32[2,256]{1,0:T(2,128)} %pad_add_fusion.2.range_ref, bf16[1024,256]{1,0:T(8,128)(2,1)} %fusion.40.query_ref, bf16[2048,2048]{1,0:T(8,128)(2,1)} %all-gather.18.cloned.1.call-done.key_ref.value_ref, ...), custom_call_target="tpu_custom_call" | custom-call | flops 10737418240 | bytes 16777216 | tf_op jit(solution)/shard_map/cross_backward/pallas_call | solution.py:423
  419.8 11.5 %copy.134 = bf16[1024,4096]{1,0:T(8,128)(2,1)} copy(bf16[1024,4096]{0,1:T(8,128)(2,1)} %bitcast.377) | data formatting | bytes 16777216 | tf_op jit(solution)/shard_map/dot_general | solution.py:38
  443.9 10.0 %convolution_convert_fusion = bf16[2048,1024]{1,0:T(8,128)(2,1)S(1)} fusion(bf16[256,1024]{1,0:T(8,128)(2,1)S(1)} %copy-done.55, bf16[256,1024]{1,0:T(8,128)(2,1)} %collective-permute-done.8, bf16[256,1024]{1,0:T(8,128)(2,1)} %collective-permute-done.7, bf16[256,1024]{1,0:T(8,128)(2,1)S(1)} %bitcast.386, f32[1024,2048]{1,0:T(8,128)} %fusion.75, ...), kind=kOutput, calls=%fused_computation.21 | convolution fusion | flops 4326424576 | bytes 14688256 | tf_op jit(solution)/shard_map/dot_general | solution.py:38
  484.6 34.7 %collective-permute-done.19 = bf16[2,2,128,2048]{3,2,1,0:T(8,128)(2,1)} collective-permute-done((bf16[2,2,128,2048]{3,2,1,0:T(8,128)(2,1)}, bf16[2,2,128,2048]{3,2,1,0:T(8,128)(2,1)}, u32[]{:S(2)}, u32[]{:S(2)}) %collective-permute-start.19) | collective-permute-done | bytes 2097184 | tf_op jit(solution)/shard_map/ppermute | solution.py:471
  522.9 47.0 %collective-permute-done.25 = bf16[2,2,256,1024]{3,2,0,1:T(8,128)(2,1)} collective-permute-done((bf16[2,2,256,1024]{3,2,0,1:T(8,128)(2,1)}, bf16[2,2,256,1024]{3,2,0,1:T(8,128)(2,1)}, u32[]{:S(2)}, u32[]{:S(2)}) %collective-permute-start.25) | collective-permute-done | bytes 2097184 | tf_op jit(solution)/shard_map/ppermute | solution.py:471
  574.9 27.0 %self_backward.1 = (bf16[16,64,256]{2,1,0:T(8,128)(2,1)}, bf16[16,128,256]{2,1,0:T(8,128)(2,1)}) custom-call(s32[4,8]{1,0:T(4,128)} %pad_add_fusion.1.plan, s32[32]{0:T(128)} %select_reduce_fusion.query_slot.key_slot, s32[32]{0:T(128)} %select_reduce_fusion.query_slot.key_slot, s32[2,4096]{1,0:T(2,128)} %pad_add_fusion.range_ref, ...), custom_call_target="tpu_custom_call" | custom-call | flops 16777216000 | bytes 24576000 | tf_op jit(solution)/shard_map/self_backward/pallas_call | solution.py:350
  638.9 49.7 %collective-permute-done.21 = bf16[128,2048]{1,0:T(8,128)(2,1)S(1)} collective-permute-done((bf16[128,2048]{1,0:T(8,128)(2,1)S(1)}, bf16[128,2048]{1,0:T(8,128)(2,1)S(1)}, u32[]{:S(2)}, u32[]{:S(2)}) %collective-permute-start.21) | collective-permute-done | bytes 524320 | tf_op jit(solution)/shard_map/ppermute | solution.py:471
  701.0 10.6 %collective-permute-done.16 = bf16[2,2,1,3,32,1024]{5,4,3,1,0,2:T(8,128)(2,1)S(1)} collective-permute-done((bf16[2,2,1,3,32,1024]{5,4,3,1,0,2:T(8,128)(2,1)S(1)}, bf16[2,2,1,3,32,1024]{5,4,3,1,0,2:T(8,128)(2,1)S(1)}, u32[]{:S(2)}, u32[]{:S(2)}) %collective-permute-start.16) | collective-permute-done | bytes 786464 | tf_op jit(solution)/shard_map/ppermute | solution.py:471
  717.3 13.1 %collective-permute-done.17 = bf16[2,1,3,32,1024]{4,3,2,0,1:T(8,128)(2,1)S(1)} collective-permute-done((bf16[2,1,3,32,1024]{4,3,2,0,1:T(8,128)(2,1)S(1)}, bf16[2,1,3,32,1024]{4,3,2,0,1:T(8,128)(2,1)S(1)}, u32[]{:S(2)}, u32[]{:S(2)}) %collective-permute-start.17) | collective-permute-done | bytes 393248 | tf_op jit(solution)/shard_map/ppermute | solution.py:471
  790.4 18.4 %all-to-all-done.5 = bf16[32,35,320]{2,1,0:T(8,128)(2,1)} async-done(((bf16[32,35,320]{2,1,0:T(8,128)(2,1)}), bf16[32,35,320]{2,1,0:T(8,128)(2,1)}, u32[]{:S(2)}, u32[]{:S(2)}) %all-to-all-start.5) | async-done | bytes 716832 | tf_op jit(solution)/shard_map/all_to_all | solution.py:743
  (406 shorter events, 262.9 us)
Async XLA Ops:
  7.2 40.2 %all-gather.16.cloned.1.call-start = ((), (), s32[]{:S(2)}) async-start(), calls=%async_computation.10 | async-start | bytes 5242880 | tf_op jit(solution)/shard_map/all_gather | solution.py:476
  9.7 85.6 %all-gather.10.cloned.1.call-start = ((), (), s32[]{:S(2)}) async-start(), calls=%async_computation.7 | async-start | bytes 7864320 | tf_op jit(solution)/shard_map/all_gather | solution.py:476
  11.1 177.5 %all-gather.12.cloned.1.call-start = ((), (), s32[]{:S(2)}) async-start(), calls=%async_computation.8 | async-start | bytes 2621440 | tf_op jit(solution)/shard_map/all_gather | solution.py:476
  13.2 178.2 %all-gather.14.cloned.1.call-start = ((), (), s32[]{:S(2)}) async-start(), calls=%async_computation.9 | async-start | bytes 2621440 | tf_op jit(solution)/shard_map/all_gather | solution.py:476
  14.1 211.6 %all-gather.18.cloned.1.call-start = ((), (), s32[]{:S(2)}) async-start(), calls=%async_computation.11 | async-start | bytes 8912896 | tf_op jit(solution)/shard_map/all_gather | solution.py:655
  101.7 37.7 %all-to-all-start = ((bf16[16,192,256]{2,1,0:T(8,128)(2,1)}), bf16[16,192,256]{2,1,0:T(8,128)(2,1)S(1)}, u32[]{:S(2)}, u32[]{:S(2)}) async-start(bf16[16,192,256]{2,1,0:T(8,128)(2,1)} %bitcast.18), calls=%async_computation | async-start | bytes 3145728 | tf_op jit(solution)/shard_map/all_to_all | solution.py:646
  107.5 162.4 %all-gather.20.cloned.1.call-start = ((), (), s32[]{:S(2)}) async-start(), calls=%async_computation.12 | async-start | bytes 2621440 | tf_op jit(solution)/shard_map/all_gather | solution.py:476
  171.6 248.2 %all-gather.22.cloned.1.call-start = ((), (), s32[]{:S(2)}) async-start(), calls=%async_computation.14 | async-start | bytes 8912896 | tf_op jit(solution)/shard_map/all_gather | solution.py:718
  176.5 123.1 %collective-permute-start.4 = (bf16[512,2048]{1,0:T(8,128)(2,1)}, bf16[512,2048]{1,0:T(8,128)(2,1)}, u32[]{:S(2)}, u32[]{:S(2)}) collective-permute-start(bf16[512,2048]{1,0:T(8,128)(2,1)} %get-tuple-element.123), channel_id=1, source_target_pairs={{0,1},{1,0},{2,3},{3,2},{4,5},{5,4},{6,7},{7,6},{8,9},{9,8},{10,11... | collective-permute-start | bytes 6291464 | tf_op jit(solution)/shard_map/ppermute | solution.py:468
  188.5 559.8 %reduce-scatter.2.cloned.1.call-start = ((), (), s32[]{:S(2)}) async-start(), calls=%async_computation.13 | async-start | bytes 8912896 | tf_op jit(solution)/shard_map/reduce_scatter | solution.py:692
  418.9 353.7 %all-gather.24.cloned.1.call-start = ((), (), s32[]{:S(2)}) async-start(), calls=%async_computation.15 | async-start | bytes 4456448 | tf_op jit(solution)/shard_map/all_gather | solution.py:719
  443.9 75.5 %collective-permute-start.19 = (bf16[2,2,128,2048]{3,2,1,0:T(8,128)(2,1)}, bf16[2,2,128,2048]{3,2,1,0:T(8,128)(2,1)}, u32[]{:S(2)}, u32[]{:S(2)}) collective-permute-start(bf16[2,2,128,2048]{3,2,1,0:T(8,128)(2,1)} %dynamic-slice_bitcast_fusion), channel_id=1, source_target_pairs={{0,4},{4,0},{8,12},{12,8},{16,20},{20,16},{24,28},{28,24},{1,5},{5... | collective-permute-start | bytes 6291464 | tf_op jit(solution)/shard_map/ppermute | solution.py:471
  457.4 112.5 %collective-permute-start.25 = (bf16[2,2,256,1024]{3,2,0,1:T(8,128)(2,1)}, bf16[2,2,256,1024]{3,2,0,1:T(8,128)(2,1)}, u32[]{:S(2)}, u32[]{:S(2)}) collective-permute-start(bf16[2,2,256,1024]{3,2,0,1:T(8,128)(2,1)} %bitcast.368), channel_id=1, source_target_pairs={{0,4},{4,0},{8,12},{12,8},{16,20},{20,16},{24,28},{28,24},{1,5},{5... | collective-permute-start | bytes 6291464 | tf_op jit(solution)/shard_map/ppermute | solution.py:471
  465.6 109.3 %all-to-all-start.2 = ((bf16[16,64,256]{2,1,0:T(8,128)(2,1)}), bf16[16,64,256]{2,1,0:T(8,128)(2,1)}, u32[]{:S(2)}, u32[]{:S(2)}) async-start(bf16[16,64,256]{2,1,0:T(8,128)(2,1)} %bitcast.403), calls=%async_computation.2 | async-start | bytes 1048576 | tf_op jit(solution)/shard_map/all_to_all | solution.py:703
  479.6 137.7 %collective-permute-start.14 = (bf16[8,2,32,1024]{3,2,0,1:T(8,128)(2,1)}, bf16[8,2,32,1024]{3,2,0,1:T(8,128)(2,1)}, u32[]{:S(2)}, u32[]{:S(2)}) collective-permute-start(bf16[8,2,32,1024]{3,2,0,1:T(8,128)(2,1)} %bitcast.369), channel_id=1, source_target_pairs={{0,2},{2,0},{1,3},{3,1},{4,6},{6,4},{5,7},{7,5},{8,10},{10,8},{9,1... | collective-permute-start | bytes 3145736 | tf_op jit(solution)/shard_map/ppermute | solution.py:468
  481.1 138.4 %collective-permute-start.13 = (bf16[8,2,32,1024]{3,2,0,1:T(8,128)(2,1)}, bf16[8,2,32,1024]{3,2,0,1:T(8,128)(2,1)}, u32[]{:S(2)}, u32[]{:S(2)}) collective-permute-start(bf16[8,2,32,1024]{3,2,0,1:T(8,128)(2,1)} %bitcast.370), channel_id=1, source_target_pairs={{0,2},{2,0},{1,3},{3,1},{4,6},{6,4},{5,7},{7,5},{8,10},{10,8},{9,1... | collective-permute-start | bytes 3145736 | tf_op jit(solution)/shard_map/ppermute | solution.py:468
  484.2 136.9 %collective-permute-start.12 = (bf16[8,2,32,1024]{3,2,0,1:T(8,128)(2,1)}, bf16[8,2,32,1024]{3,2,0,1:T(8,128)(2,1)}, u32[]{:S(2)}, u32[]{:S(2)}) collective-permute-start(bf16[8,2,32,1024]{3,2,0,1:T(8,128)(2,1)} %bitcast.371), channel_id=1, source_target_pairs={{0,2},{2,0},{1,3},{3,1},{4,6},{6,4},{5,7},{7,5},{8,10},{10,8},{9,1... | collective-permute-start | bytes 3145736 | tf_op jit(solution)/shard_map/ppermute | solution.py:468
  522.9 102.8 %collective-permute-start.20 = (bf16[2,128,2048]{2,1,0:T(8,128)(2,1)}, bf16[2,128,2048]{2,1,0:T(8,128)(2,1)}, u32[]{:S(2)}, u32[]{:S(2)}) collective-permute-start(bf16[2,128,2048]{2,1,0:T(8,128)(2,1)} %dynamic-slice_bitcast_fusion.3), channel_id=1, source_target_pairs={{0,8},{4,12},{8,0},{12,4},{16,24},{20,28},{24,16},{28,20},{1,9},{5... | collective-permute-start | bytes 3145736 | tf_op jit(solution)/shard_map/ppermute | solution.py:471
  574.9 62.2 %collective-permute-start.26 = (bf16[2,256,1024]{2,1,0:T(8,128)(2,1)}, bf16[2,256,1024]{2,1,0:T(8,128)(2,1)}, u32[]{:S(2)}, u32[]{:S(2)}) collective-permute-start(bf16[2,256,1024]{2,1,0:T(8,128)(2,1)} %dynamic-slice_bitcast_fusion.2), channel_id=1, source_target_pairs={{0,8},{4,12},{8,0},{12,4},{16,24},{20,28},{24,16},{28,20},{1,9},{5... | collective-permute-start | bytes 3145736 | tf_op jit(solution)/shard_map/ppermute | solution.py:471
  606.1 125.2 %all-to-all-start.3 = ((bf16[16,192,256]{2,1,0:T(8,128)(2,1)}), bf16[16,192,256]{2,1,0:T(8,128)(2,1)S(1)}, u32[]{:S(2)}, u32[]{:S(2)}) async-start(bf16[16,192,256]{2,1,0:T(8,128)(2,1)} %constant_dynamic-update-slice_fusion), calls=%async_computation.3 | async-start | bytes 3145728 | tf_op jit(solution)/shard_map/all_to_all | solution.py:712
  623.4 65.4 %collective-permute-start.15 = (bf16[8,3,32,1024]{3,2,1,0:T(8,128)(2,1)S(1)}, bf16[8,3,32,1024]{3,2,1,0:T(8,128)(2,1)S(1)}, u32[]{:S(2)}, u32[]{:S(2)}) collective-permute-start(bf16[8,3,32,1024]{3,2,1,0:T(8,128)(2,1)S(1)} %dynamic-slice_bitcast_fusion.1), channel_id=1, source_target_pairs={{0,1},{1,0},{2,3},{3,2},{4,5},{5,4},{6,7},{7,6},{8,9},{9,8},{10,11... | collective-permute-start | bytes 4718600 | tf_op jit(solution)/shard_map/ppermute | solution.py:468
  627.4 61.2 %collective-permute-start.21 = (bf16[128,2048]{1,0:T(8,128)(2,1)S(1)}, bf16[128,2048]{1,0:T(8,128)(2,1)S(1)}, u32[]{:S(2)}, u32[]{:S(2)}) collective-permute-start(bf16[128,2048]{1,0:T(8,128)(2,1)S(1)} %dynamic-slice_bitcast_fusion.6), channel_id=1, source_target_pairs={{0,16},{4,20},{8,24},{12,28},{16,0},{20,4},{24,8},{28,12},{1,17},{... | collective-permute-start | bytes 1572872 | tf_op jit(solution)/shard_map/ppermute | solution.py:471
  638.8 61.0 %collective-permute-start.27 = (bf16[256,1024]{1,0:T(8,128)(2,1)S(1)}, bf16[256,1024]{1,0:T(8,128)(2,1)S(1)}, u32[]{:S(2)}, u32[]{:S(2)}) collective-permute-start(bf16[256,1024]{1,0:T(8,128)(2,1)S(1)} %dynamic-slice_bitcast_fusion.5), channel_id=1, source_target_pairs={{0,16},{4,20},{8,24},{12,28},{16,0},{20,4},{24,8},{28,12},{1,17},{... | collective-permute-start | bytes 1572872 | tf_op jit(solution)/shard_map/ppermute | solution.py:471
  731.2 54.9 %collective-permute-start.18 = (bf16[1,3,32,1024]{3,2,1,0:T(8,128)(2,1)}, bf16[1,3,32,1024]{3,2,1,0:T(8,128)(2,1)}, u32[]{:S(2)}, u32[]{:S(2)}) collective-permute-start(bf16[1,3,32,1024]{3,2,1,0:T(8,128)(2,1)} %dynamic-slice_bitcast_fusion.8), channel_id=1, source_target_pairs={{0,16},{4,20},{8,24},{12,28},{16,0},{20,4},{24,8},{28,12},{1,17},{... | collective-permute-start | bytes 589832 | tf_op jit(solution)/shard_map/ppermute | solution.py:471
  (81 other events, 1074.1 us)
Sparse Core Ops, SparseCore 0:
  10.2 37.1 all-gather.15
  48.9 46.3 all-gather.9
  97.5 22.5 all-gather.11
  122.1 22.6 all-gather.13
  147.3 78.2 all-gather.17
  227.1 21.6 all-gather.19
  250.9 75.0 all-gather.21
  419.0 142.4 reduce-scatter.1
  563.7 70.4 all-gather.23

commit v2 on v1

v2 whole, which is shorter than its diff:
```python
import functools

import jax
import jax.numpy as jnp
from jax import lax
from jax.experimental import pallas as pl
from jax.experimental.pallas import tpu as pltpu
from jax.sharding import Mesh
from jax.sharding import PartitionSpec as P

H = 16
BLOCK = 128

CHIP = ("part", "hc")
HEADS = ("hc", "core")
CTX = ("part", "hc", "core")
QUAD = ("core", "fsdp")
ALL = ("part", "hc", "core", "fsdp")

ln_eps = 1e-05
score_scale = 0.125
low = jnp.bfloat16
full = jnp.float32
SELF_TILES = (512, 512)
SELF_CHAINS = 1
CROSS_TILE = 1024
VMEM_BYTES = 56 * 1024 * 1024


def layer_norm(v, gain, shift):
    centred = v - jnp.mean(v, axis=-1, keepdims=True)
    spread = jnp.mean(centred * centred, axis=-1, keepdims=True)
    return centred * lax.rsqrt(spread + ln_eps) * gain + shift


def gelu_tanh(v):
    return 0.5 * v * (1.0 + jnp.tanh(0.7978845608028654 * (v + 0.044715 * v * v * v)))


def contract(left, right, left_dim, right_dim):
    return lax.dot_general(
        left, right, (((left_dim,), (right_dim,)), ((), ())), preferred_element_type=full
    )


def column_sums(values):
    return jnp.sum(values.astype(full), axis=0)


def plan_kernel(
    query_tile, self_key_tile, cross_key_tile, group_key_tile, cross_rows,
    order, flip, lengths, source_lengths, where,
    query_slot, key_slot, self_plan, cross_plan, group_plan, self_ranges, cross_ranges, group_ranges,
    block_of,
):
    pairs, documents = order.shape[0], lengths.shape[0]
    here, part = where[0], where[1]
    ends, source_ends = [], []
    for d in range(documents):
        ends.append(lengths[d] + (ends[-1] if d else 0))
        source_ends.append(source_lengths[d] + (source_ends[-1] if d else 0))

    def start_of(places):
        start = jnp.zeros_like(places)
        for end in ends:
            start = jnp.where(places >= end, end, start)
        return start

    def source_of(places):
        start, stop = jnp.zeros_like(places), jnp.zeros_like(places) + source_ends[0]
        for d in range(documents - 1):
            start = jnp.where(places >= ends[d], source_ends[d], start)
            stop = jnp.where(places >= ends[d], source_ends[d + 1], stop)
        return start, stop

    def stored(i):
        number = order[i >> 1]
        upper = (flip[i >> 1] + i) & 1 == 1
        return jnp.where(upper, 2 * pairs - 1 - number, number)

    @pl.loop(0, 2 * pairs)
    def _(i):
        key_slot[stored(i)] = i

    blocks = query_slot.shape[0]
    lanes = lax.broadcasted_iota(jnp.int32, (1, BLOCK), 1)

    def take(b, count):
        slot = key_slot[b] - part * blocks
        inside = (slot >= 0) & (slot < blocks)

        @pl.when(inside)
        def _():
            query_slot[count] = slot
            block_of[count] = b
            places = lanes + b * BLOCK
            self_ranges[0:1, tile_at(count, BLOCK)] = start_of(places)
            self_ranges[1:2, tile_at(count, BLOCK)] = places + 1
            start, stop = source_of(places)
            group_ranges[0:1, tile_at(count, BLOCK)] = start
            group_ranges[1:2, tile_at(count, BLOCK)] = stop

        return count + jnp.where(inside, 1, 0)

    lax.fori_loop(0, 2 * pairs, take, jnp.int32(0))

    def write(plan, t, low_start, high_start, low_stop, high_stop, key_tile):
        first = lax.div(low_start, key_tile)
        last = lax.div(high_stop + key_tile - 1, key_tile)
        inner = jnp.clip(lax.div(high_start + key_tile - 1, key_tile), first, last)
        plan[0, t] = first
        plan[1, t] = inner
        plan[2, t] = jnp.clip(lax.div(low_stop, key_tile), inner, last)
        plan[3, t] = last

    step = query_tile // BLOCK

    @pl.loop(0, blocks // step)
    def _(t):
        begin = block_of[t * step] * BLOCK
        end = block_of[t * step + step - 1] * BLOCK + BLOCK - 1
        write(self_plan, t, start_of(begin), start_of(end), begin + 1, end + 1, self_key_tile)
        first, last = source_of(begin), source_of(end)
        write(group_plan, t, first[0], last[0], first[1], last[1], group_key_tile)

    edges = []
    for k in range(cross_rows // BLOCK):
        begin = stored(here * (cross_rows // BLOCK) + k) * BLOCK
        low_edge, high_edge = source_of(begin), source_of(begin + BLOCK - 1)
        if k:
            edges = [
                jnp.minimum(edges[0], low_edge[0]), jnp.maximum(edges[1], high_edge[0]),
                jnp.minimum(edges[2], low_edge[1]), jnp.maximum(edges[3], high_edge[1]),
            ]
        else:
            edges = [low_edge[0], high_edge[0], low_edge[1], high_edge[1]]
        start, stop = source_of(lanes + begin)
        cross_ranges[0:1, k * BLOCK : (k + 1) * BLOCK] = start
        cross_ranges[1:2, k * BLOCK : (k + 1) * BLOCK] = stop
    write(cross_plan, 0, *edges, cross_key_tile)


def attention_plan(order, flip, lengths, source_lengths, here, part, parts, rows, sources):
    blocks = 2 * order.shape[0]
    mine = blocks // parts
    query_tile, key_tile = self_tiles(mine * BLOCK)
    group_key_tile = cross_tiles(mine * BLOCK, sources)[1]
    tiles = mine * BLOCK // query_tile
    shapes = ((mine,), (blocks,), (4, tiles), (4, 1), (4, tiles), (2, mine * BLOCK), (2, rows), (2, mine * BLOCK))
    return pl.pallas_call(
        functools.partial(plan_kernel, query_tile, key_tile, cross_tile(sources), group_key_tile, rows),
        out_shape=tuple(jax.ShapeDtypeStruct(shape, jnp.int32) for shape in shapes),
        in_specs=[smem()] * 5,
        out_specs=(smem(),) * 5 + (vmem(),) * 3,
        scratch_shapes=[pltpu.SMEM((mine,), jnp.int32)],
        compiler_params=params(),
        name="attention_plan",
    )(order, flip, lengths, source_lengths, jnp.stack([here, part]).astype(jnp.int32))


def over_tiles(plan, tile_number, step, carry):
    first, inner = plan[0, tile_number], plan[1, tile_number]
    outer, last = plan[2, tile_number], plan[3, tile_number]
    carry = lax.fori_loop(inner, outer, functools.partial(step, masked=False), carry)
    before = inner - first

    def edge(index, state):
        number = jnp.where(index < before, first + index, outer + index - before)
        return step(number, state, masked=True)

    return lax.fori_loop(0, before + last - outer, edge, carry)


def masked_scores(scores, number, tile, start, stop):
    keys = number * tile + lax.broadcasted_iota(jnp.int32, scores.shape, 0)
    return jnp.where((keys >= start) & (keys < stop), scores, -jnp.inf)


def forward_tiles(plan, number, queries, start, stop, keys_of, values_of, tile, depth):
    chains = range(len(queries))
    width = queries[0].shape[1]
    start, stop = as_list(start, len(queries)), as_list(stop, len(queries))

    def step(j, carry, masked):
        top, total, accum = carry
        scores = [contract(keys_of(j), queries[i], 1, 0) for i in chains]
        if masked:
            scores = [masked_scores(scores[i], j, tile, start[i], stop[i]) for i in chains]
        newtop = [jnp.maximum(top[i], jnp.max(scores[i], axis=0, keepdims=True)) for i in chains]
        weights = [jnp.exp(scores[i] - newtop[i]) for i in chains]
        factor = [jnp.exp(top[i] - newtop[i]) for i in chains]
        total = [total[i] * factor[i] + jnp.sum(weights[i], axis=0, keepdims=True) for i in chains]
        accum = [
            accum[i] * factor[i] + contract(values_of(j, i), weights[i].astype(low), 1, 0)
            for i in chains
        ]
        return newtop, total, accum

    carry = (
        [jnp.full((1, width), -1e30, full) for _ in chains],
        [jnp.zeros((1, width), full) for _ in chains],
        [jnp.zeros((depth, width), full) for _ in chains],
    )
    top, total, accum = over_tiles(plan, number, step, carry)
    return [accum[i] / total[i] for i in chains], [top[i] + jnp.log(total[i]) for i in chains]


def as_list(value, count):
    return value if isinstance(value, list) else [value] * count


def identity(size):
    rows = lax.broadcasted_iota(jnp.int32, (size, size), 0)
    cols = lax.broadcasted_iota(jnp.int32, (size, size), 1)
    return jnp.where(rows == cols, 1.0, 0.0).astype(low)


def flipped(eye, block):
    return contract(eye, block, 1, 1).astype(low)


def tile_at(number, size):
    return pl.ds(pl.multiple_of(number * size, size), size)


def half_at(slot):
    return pl.ds(pl.multiple_of((slot & 1) * BLOCK, BLOCK), BLOCK)


def self_forward_kernel(
    tiles, plan, query_slot, key_slot, range_ref, own_ref, all_ref,
    out_ref, exact_ref, lse_ref, query_s, key_s, value_s,
):
    query_tile, tile = tiles
    depth, queries = query_s.shape
    count = value_s.shape[1]

    @pl.loop(0, queries // BLOCK)
    def _(b):
        slot = query_slot[b]
        query_s[:, tile_at(b, BLOCK)] = own_ref[slot >> 1, 0:depth, half_at(slot)] * low(score_scale)

    @pl.loop(0, count // BLOCK)
    def _(b):
        slot = key_slot[b]
        block = all_ref[slot >> 1, depth : 2 * depth, half_at(slot)]
        key_s[tile_at(b, BLOCK), :] = block.T
        value_s[:, tile_at(b, BLOCK)] = all_ref[slot >> 1, 2 * depth : 3 * depth, half_at(slot)]

    chains = SELF_CHAINS
    lanes = query_tile // chains

    @pl.loop(0, queries // query_tile)
    def _(t):
        here = [pl.ds(pl.multiple_of(t * query_tile + i * lanes, lanes), lanes) for i in range(chains)]
        result, lse = forward_tiles(
            plan, t, [query_s[:, at] for at in here], [range_ref[0:1, at] for at in here],
            [range_ref[1:2, at] for at in here],
            lambda j: key_s[tile_at(j, tile), :], lambda j, i: value_s[:, tile_at(j, tile)],
            tile, depth,
        )
        for i in range(chains):
            exact_ref[:, here[i]] = result[i]
            lse_ref[0:1, here[i]] = lse[i]

    @pl.loop(0, queries // BLOCK)
    def _(b):
        slot = query_slot[b]
        out_ref[slot >> 1, :, half_at(slot)] = exact_ref[:, tile_at(b, BLOCK)].astype(low)


def self_backward_kernel(
    tiles, plan, query_slot, key_slot, range_ref, own_ref, all_ref, grad_ref, exact_ref, lse_ref,
    dq_ref, dkv_ref, rows_ref, query_s, grad_s, key_s, keyt_s, value_s, dq_s, dk_s, dv_s,
):
    query_tile, tile = tiles
    depth, queries = query_s.shape
    count = keyt_s.shape[1]

    @pl.loop(0, queries // BLOCK)
    def _(b):
        slot = query_slot[b]
        query_s[:, tile_at(b, BLOCK)] = own_ref[slot >> 1, 0:depth, half_at(slot)] * low(score_scale)
        grad_s[:, tile_at(b, BLOCK)] = grad_ref[slot >> 1, :, half_at(slot)]

    @pl.loop(0, count // BLOCK)
    def _(b):
        slot = key_slot[b]
        block = all_ref[slot >> 1, depth : 2 * depth, half_at(slot)]
        keyt_s[:, tile_at(b, BLOCK)] = block
        key_s[tile_at(b, BLOCK), :] = block.T
        value_s[tile_at(b, BLOCK), :] = all_ref[slot >> 1, 2 * depth : 3 * depth, half_at(slot)].T

    dk_s[...] = jnp.zeros_like(dk_s)
    dv_s[...] = jnp.zeros_like(dv_s)

    @pl.loop(0, queries // query_tile)
    def _(t):
        here = tile_at(t, query_tile)
        query, grad = query_s[:, here], grad_s[:, here]
        start, stop = range_ref[0:1, here], range_ref[1:2, here]
        lse = lse_ref[0:1, here]
        delta = jnp.sum(grad.astype(full) * exact_ref[:, here], axis=0, keepdims=True)

        def step(j, dq, masked):
            there = tile_at(j, tile)
            scores = contract(key_s[there, :], query, 1, 0)
            if masked:
                scores = masked_scores(scores, j, tile, start, stop)
            probs = jnp.exp(scores - lse)
            dprobs = contract(value_s[there, :], grad, 1, 0)
            dscores = (probs * (dprobs - delta)).astype(low)
            dv_s[:, there] += contract(grad, probs.astype(low), 1, 1)
            dk_s[:, there] += contract(query, dscores, 1, 1)
            return dq + contract(keyt_s[:, there], dscores, 1, 0)

        dq_s[:, here] = over_tiles(plan, t, step, jnp.zeros((depth, query_tile), full))

    @pl.loop(0, queries // BLOCK)
    def _(b):
        slot = query_slot[b]
        dq = (dq_s[:, tile_at(b, BLOCK)] * score_scale).astype(low)
        dq_ref[slot >> 1, :, half_at(slot)] = dq
        rows_ref[0:depth, tile_at(slot, BLOCK)] = dq

    @pl.loop(0, count // BLOCK)
    def _(b):
        slot = key_slot[b]
        dk = dk_s[:, tile_at(b, BLOCK)].astype(dkv_ref.dtype)
        dv = dv_s[:, tile_at(b, BLOCK)].astype(dkv_ref.dtype)
        dkv_ref[slot >> 1, 0:depth, half_at(slot)] = dk
        dkv_ref[slot >> 1, depth : 2 * depth, half_at(slot)] = dv
        if count == queries:
            rows_ref[depth : 2 * depth, tile_at(slot, BLOCK)] = dk.astype(low)
            rows_ref[2 * depth : 3 * depth, tile_at(slot, BLOCK)] = dv.astype(low)


def one_head(values, head, depth):
    rows = lax.broadcasted_iota(jnp.int32, values.shape, 0)
    inside = (rows >= head * depth) & (rows < (head + 1) * depth)
    return jnp.where(inside, values, jnp.zeros_like(values))


def cross_forward_kernel(
    tile, plan, range_ref, query_ref, key_ref, value_ref, out_ref, exact_ref, lse_ref, value_s
):
    depth = value_s.shape[0] // 2

    eye = identity(2 * depth)

    def turn(j, _):
        value_s[:, tile_at(j, tile)] = flipped(eye, value_ref[tile_at(j, tile), :])
        return 0

    lax.fori_loop(plan[0, 0], plan[3, 0], turn, 0)
    query = query_ref[...] * low(score_scale)
    rows = [pl.ds(head * depth, depth) for head in range(2)]
    result, lse = forward_tiles(
        plan, 0, [one_head(query, head, depth) for head in range(2)],
        range_ref[0:1, :], range_ref[1:2, :],
        lambda j: key_ref[tile_at(j, tile), :],
        lambda j, i: value_s[rows[i], tile_at(j, tile)],
        tile, depth,
    )
    for head in range(2):
        exact_ref[rows[head], :] = result[head]
        out_ref[rows[head], :] = result[head].astype(low)
        lse_ref[0, head : head + 1, :] = lse[head]


def cross_backward_kernel(
    tiles, plan, query_slot, range_ref, query_ref, keys_values_ref, grad_ref, exact_ref,
    dq_ref, dkv_ref, query_s, grad_s, exact_s, keyt_s, dkv_s,
):
    query_tile, tile = tiles
    depth = query_ref.shape[1]
    queries = query_s.shape[1]
    eye = identity(2 * depth)

    @pl.loop(0, queries // BLOCK)
    def _(b):
        slot = query_slot[b]
        at, there = tile_at(b, BLOCK), half_at(slot)
        query_s[:, at] = query_ref[slot >> 1, :, there] * low(score_scale)
        grad_s[:, at] = grad_ref[slot >> 1, :, there]
        exact_s[:, at] = exact_ref[slot >> 1, :, there]

    @pl.loop(0, keyt_s.shape[1] // tile)
    def _(j):
        at = tile_at(j, tile)
        keyt_s[:, at] = flipped(eye, keys_values_ref[at, :])[0:depth]

    dkv_s[...] = jnp.zeros_like(dkv_s)
    blank = jnp.zeros((depth, query_tile), low)

    @pl.loop(0, queries // query_tile)
    def _(t):
        here = tile_at(t, query_tile)
        grad = grad_s[:, here]
        start, stop = range_ref[0:1, here], range_ref[1:2, here]
        lse = exact_s[depth : depth + 1, here]
        delta = jnp.sum(grad.astype(full) * exact_s[0:depth, here], axis=0, keepdims=True)
        wide_query = jnp.concatenate([query_s[:, here], blank], axis=0)
        wide_grad = jnp.concatenate([blank, grad], axis=0)
        sides = jnp.concatenate([wide_query, wide_grad], axis=1)

        def step(j, dq, masked):
            there = tile_at(j, tile)
            keys_values = keys_values_ref[there, :]
            scores = contract(keys_values, wide_query, 1, 0)
            if masked:
                scores = masked_scores(scores, j, tile, start, stop)
            probs = jnp.exp(scores - lse)
            dprobs = contract(keys_values, wide_grad, 1, 0)
            dscores = (probs * (dprobs - delta)).astype(low)
            both = jnp.concatenate([dscores, probs.astype(low)], axis=1)
            dkv_s[there, :] += contract(both, sides, 1, 1)
            return dq + contract(keyt_s[:, there], dscores, 1, 0)

        dq = over_tiles(plan, t, step, jnp.zeros((depth, query_tile), full))
        query_s[:, here] = (dq * score_scale).astype(low)

    @pl.loop(0, queries // BLOCK)
    def _(b):
        slot = query_slot[b]
        dq_ref[slot >> 1, :, half_at(slot)] = query_s[:, tile_at(b, BLOCK)]

    dkv_ref[...] = dkv_s[...].astype(dkv_ref.dtype)


def smem():
    return pl.BlockSpec(memory_space=pltpu.SMEM)


def vmem():
    return pl.BlockSpec(memory_space=pltpu.VMEM)


def params():
    return pltpu.CompilerParams(vmem_limit_bytes=VMEM_BYTES)


def self_tiles(queries):
    return min(SELF_TILES[0], queries), min(SELF_TILES[1], queries)


def self_forward(plan, query_slot, key_slot, ranges, own, everyone):
    heads, three, rows = own.shape
    depth = three // 3
    queries, count = heads * rows, everyone.shape[0] * rows
    tile = self_tiles(queries)
    return pl.pallas_call(
        functools.partial(self_forward_kernel, tile),
        out_shape=(
            jax.ShapeDtypeStruct((heads, depth, rows), low),
            jax.ShapeDtypeStruct((depth, queries), full),
            jax.ShapeDtypeStruct((8, queries), full),
        ),
        in_specs=[smem()] * 3 + [vmem()] * 3,
        out_specs=(vmem(),) * 3,
        scratch_shapes=[
            pltpu.VMEM((depth, queries), low),
            pltpu.VMEM((count, depth), low),
            pltpu.VMEM((depth, count), low),
        ],
        compiler_params=params(),
        cost_estimate=pl.CostEstimate(flops=1, bytes_accessed=1, transcendentals=0),
        name="self_forward",
    )(plan, query_slot, key_slot, ranges, own, everyone)


def self_backward(plan, query_slot, key_slot, ranges, own, everyone, grad, exact, lse, kv_type):
    heads, three, rows = own.shape
    depth = three // 3
    queries, count = heads * rows, everyone.shape[0] * rows
    tile = self_tiles(queries)
    return pl.pallas_call(
        functools.partial(self_backward_kernel, tile),
        out_shape=(
            jax.ShapeDtypeStruct((heads, depth, rows), low),
            jax.ShapeDtypeStruct((everyone.shape[0], 2 * depth, rows), kv_type),
            jax.ShapeDtypeStruct((3 * depth, queries), low),
        ),
        in_specs=[smem()] * 3 + [vmem()] * 6,
        out_specs=(vmem(),) * 3,
        scratch_shapes=[
            pltpu.VMEM((depth, queries), low),
            pltpu.VMEM((depth, queries), low),
            pltpu.VMEM((count, depth), low),
            pltpu.VMEM((depth, count), low),
            pltpu.VMEM((count, depth), low),
            pltpu.VMEM((depth, queries), full),
            pltpu.VMEM((depth, count), full),
            pltpu.VMEM((depth, count), full),
        ],
        compiler_params=params(),
        cost_estimate=pl.CostEstimate(flops=1, bytes_accessed=1, transcendentals=0),
        name="self_backward",
    )(plan, query_slot, key_slot, ranges, own, everyone, grad, exact, lse)


def cross_tiles(queries, count):
    return min(512, queries), min(512, count)


def cross_tile(count):
    return min(CROSS_TILE, count)


def pair_spec(rows, cols):
    return pl.BlockSpec((rows, cols), lambda i: (i, 0))


def cross_forward(plan, ranges, query, keys_values):
    width, rows = query.shape
    count = keys_values.shape[0]
    pairs = H // 2
    wide = width // pairs
    return pl.pallas_call(
        functools.partial(cross_forward_kernel, cross_tile(count)),
        grid=(pairs,),
        out_shape=(
            jax.ShapeDtypeStruct((width, rows), low),
            jax.ShapeDtypeStruct((width, rows), full),
            jax.ShapeDtypeStruct((pairs, 8, rows), full),
        ),
        in_specs=[
            smem(),
            vmem(),
            pair_spec(wide, rows),
            pl.BlockSpec((count, wide), lambda i: (0, i)),
            pl.BlockSpec((count, wide), lambda i: (0, pairs + i)),
        ],
        out_specs=(
            pair_spec(wide, rows),
            pair_spec(wide, rows),
            pl.BlockSpec((1, 8, rows), lambda i: (i, 0, 0)),
        ),
        scratch_shapes=[pltpu.VMEM((wide, count), low)],
        compiler_params=params(),
        cost_estimate=pl.CostEstimate(flops=1, bytes_accessed=1, transcendentals=0),
        name="cross_forward",
    )(plan, ranges, query, keys_values, keys_values)


def cross_backward(plan, query_slot, ranges, query, keys_values, grad, exact, kv_type):
    heads, depth, rows = query.shape
    queries, count = heads * rows, keys_values.shape[0]
    return pl.pallas_call(
        functools.partial(cross_backward_kernel, cross_tiles(queries, count)),
        out_shape=(
            jax.ShapeDtypeStruct((heads, depth, rows), low),
            jax.ShapeDtypeStruct((count, 2 * depth), kv_type),
        ),
        in_specs=[smem()] * 2 + [vmem()] * 5,
        out_specs=(vmem(),) * 2,
        scratch_shapes=[
            pltpu.VMEM((depth, queries), low),
            pltpu.VMEM((depth, queries), low),
            pltpu.VMEM((exact.shape[1], queries), full),
            pltpu.VMEM((depth, count), low),
            pltpu.VMEM((count, 2 * depth), full),
        ],
        compiler_params=params(),
        cost_estimate=pl.CostEstimate(flops=1, bytes_accessed=1, transcendentals=0),
        name="cross_backward",
    )(plan, query_slot, ranges, query, keys_values, grad, exact)


def copy_kernel(_, value_ref, out_ref):
    out_ref[...] = value_ref[...]


def strided_columns(value, first, step, wide):
    rows, cols = value.shape
    count = cols // (step * wide)
    return pl.pallas_call(
        copy_kernel,
        out_shape=jax.ShapeDtypeStruct((rows, count * wide), value.dtype),
        grid_spec=pltpu.PrefetchScalarGridSpec(
            num_scalar_prefetch=1,
            grid=(count,),
            in_specs=[pl.BlockSpec((rows, wide), lambda i, at: (0, i * step + at[0]))],
            out_specs=pl.BlockSpec((rows, wide), lambda i, at: (0, i)),
        ),
        compiler_params=params(),
        name="strided_columns",
    )(first.astype(jnp.int32).reshape(1), value)


def owned_kernel(depth, pieces_ref, qkv_ref, ckv_ref):
    _, heads, groups, share, _ = pieces_ref.shape
    width = heads * depth
    for head in range(heads):
        total = 0.0
        for p in range(pieces_ref.shape[0]):
            for g in range(groups):
                total = total + pieces_ref[p, head, g].astype(full)
        at = head * depth
        for i in range(3):
            qkv_ref[:, i * width + at : i * width + at + depth] = total[:, i * depth : (i + 1) * depth]
        for i in range(2):
            ckv_ref[:, i * width + at : i * width + at + depth] = total[:, (3 + i) * depth : (4 + i) * depth]


def owned_columns(pieces, depth):
    _, heads, _, share, _ = pieces.shape
    width = heads * depth
    return pl.pallas_call(
        functools.partial(owned_kernel, depth),
        out_shape=(
            jax.ShapeDtypeStruct((share, 3 * width), full),
            jax.ShapeDtypeStruct((share, 2 * width), full),
        ),
        in_specs=[vmem()],
        out_specs=(vmem(),) * 2,
        compiler_params=params(),
        name="owned_columns",
    )(pieces)


def after(value, *others):
    return lax.optimization_barrier((value,) + others)[0]


class Exchange:
    def __init__(self):
        self.fsdp = lax.axis_size("fsdp")
        self.chips = lax.axis_size(CHIP)
        self.core = lax.axis_index("core")
        self.row = lax.axis_index("fsdp")
        self.chip = lax.axis_index(CHIP)
        self.paired = self.fsdp == 2
        self.cube = self.paired and self.chips == 8
        self.near, self.far = (self.chip >> 1) & 1, self.chip >> 2
        self.corner = 2 * (self.chip & 1) + self.core

    def swap(self, value, axis):
        return lax.ppermute(value, axis, [(0, 1), (1, 0)])

    def swap_chip(self, value, bit):
        return lax.ppermute(value, CHIP, [(i, i ^ bit) for i in range(self.chips)])

    def own_piece(self, shard):
        piece = shard.shape[0] // 2
        return lax.dynamic_slice_in_dim(shard, self.core * piece, piece, 0)

    def fetch(self, mine, begin=()):
        if not self.paired:
            return lax.all_gather(mine, ("fsdp", "core"), axis=0, tiled=True)
        return self.swap(after(mine, *begin) if begin else mine, "fsdp")

    def place(self, base, across, hold=()):
        if not self.paired:
            return across
        piece = across.shape[0]
        held = after(across, *hold) if hold else across
        corner = self.swap(held, "core")
        start = (1 - self.row) * 2 * piece
        whole = lax.dynamic_update_slice_in_dim(base, held, start + self.core * piece, 0)
        return lax.dynamic_update_slice_in_dim(whole, corner, start + (1 - self.core) * piece, 0)

    def gather_last(self, shard):
        if not self.paired:
            return lax.all_gather(shard, "fsdp", axis=shard.ndim - 1, tiled=True)
        other = self.swap(shard, "fsdp")
        return jnp.where(
            self.row == 0,
            jnp.concatenate([shard, other], axis=-1),
            jnp.concatenate([other, shard], axis=-1),
        )


    def hidden_parts(self, shard, axis):
        size = shard.shape[axis]
        if not self.cube:
            wide = size // 2
            return lax.dynamic_slice_in_dim(shard, self.core * wide, wide, axis)
        wide = size // 8
        parts = [
            lax.dynamic_slice_in_dim(shard, (4 * z + self.corner) * wide, wide, axis) for z in range(2)
        ]
        return jnp.concatenate(parts, axis=axis)

    def up_part(self, shard):
        rows, hidden = shard.shape
        if self.cube:
            return strided_columns(shard, self.corner, 4, hidden // 16)
        split = shard.reshape(rows, self.fsdp, 2, hidden // (2 * self.fsdp))
        return lax.dynamic_index_in_dim(split, self.core, 2, keepdims=False)

    def trade(self, mine, begin):
        half = mine.shape[0] // 2
        return [
            self.swap(after(mine[i * half : (i + 1) * half], *begin[i]), "fsdp") for i in range(2)
        ]

    def joined(self, base, theirs, hold):
        half = theirs[0].shape[0]
        start = (1 - self.row) * 2 * half
        for i in range(2):
            base = lax.dynamic_update_slice_in_dim(base, after(theirs[i], *hold[i]), start + i * half, 0)
        return base

    def swap_beside(self, value):
        return self.swap_chip(value, 1) if self.cube else self.swap(value, "fsdp")

    def quad_gather(self, value, hold=()):
        if not self.paired:
            return lax.all_gather(value, QUAD, axis=0, tiled=True), ()
        across = self.swap_beside(value)
        held = after(across, *hold)
        beside = self.swap(value, "core")
        corner = self.swap(held, "core")
        return jnp.concatenate([value, beside, held, corner], axis=0), (across,)

    def quad_sum(self, value):
        if not self.paired:
            total = lax.psum_scatter(value, QUAD, scatter_dimension=0, tiled=True)
            return total.astype(full), total
        rows = value.shape[0] // 4
        parts = value.reshape(2, 2, rows, value.shape[1])
        theirs = self.swap(parts[:, 1], "core")
        both = parts[:, 0].astype(full) + theirs.astype(full)
        got = self.swap_beside(both[1].astype(low))
        return (both[0], got), theirs

    def quad_end(self, pending, hold=()):
        if not self.paired:
            return pending
        mine, got = pending
        return (after(mine, *hold) if hold else mine) + got.astype(full)

    def send_half(self, value, axis, bit, swap, *others):
        if others:
            value = after(value, *others)
        sent = lax.dynamic_index_in_dim(value, 1 - bit, axis, keepdims=False)
        kept = lax.dynamic_index_in_dim(value, bit, axis, keepdims=False)
        return sent, (kept, swap(sent))

    def add(self, halves, *others):
        kept, got = halves
        if others:
            kept = after(kept, *others)
        return kept.astype(full) + got.astype(full)

    def chip_step(self, value, number, *others):
        bit = (self.chip >> number) & 1
        return self.send_half(value, 2 - number, bit, lambda v: self.swap_chip(v, 1 << number), *others)

    def chip_shape(self, value):
        return value.reshape((2, 2, 2, value.shape[0] // 8) + value.shape[1:])

    def chip_scatter(self, value):
        return lax.psum_scatter(value, CHIP, scatter_dimension=0, tiled=True).astype(full)

    def device_shape(self, value):
        rows, cols = value.shape
        return value.reshape(self.chips, 2, self.fsdp, rows // (self.chips * 2 * self.fsdp), cols)

    def device_scatter(self, values):
        stacked = jnp.stack([self.device_shape(v) for v in values], axis=3)
        stacked = lax.psum_scatter(stacked, "core", scatter_dimension=1, tiled=True)
        stacked = lax.psum_scatter(stacked, "fsdp", scatter_dimension=2, tiled=True)
        stacked = lax.psum_scatter(stacked, CHIP, scatter_dimension=0, tiled=True)
        return [stacked[0, 0, 0, i].astype(full) for i in range(len(values))]

    def to_owner(self, value):
        chips, fsdp = self.chips, self.fsdp
        moves = []
        for chip in range(chips):
            for core in range(2):
                for row in range(fsdp):
                    moves.append(
                        ((chip * 2 + core) * fsdp + row, (row * 2 + core) * chips + chip)
                    )
        return lax.ppermute(value, ALL, moves)

    def quad_columns(self, value):
        quad = 2 * self.fsdp
        rows, wide = value.shape
        share = rows // quad
        value = lax.all_to_all(value, QUAD, 0, 1, tiled=True)
        value = value.reshape(share, 2, self.fsdp, wide).transpose(0, 2, 1, 3)
        return value.reshape(share, quad * wide)

    def corner_columns(self, value):
        _, share, wide = value.shape

        def block(bits):
            return lax.dynamic_index_in_dim(value, self.corner ^ bits, 0, keepdims=False)

        got = [
            block(0),
            self.swap(block(1), "core"),
            self.swap_chip(block(2), 1),
            lax.ppermute(block(3), CTX, [(i, i ^ 3) for i in range(2 * self.chips)]),
        ]
        got = [jnp.where(self.core == 0, got[i], got[i ^ 1]) for i in range(4)]
        got = [jnp.where(self.chip & 1 == 0, got[i], got[i ^ 2]) for i in range(4)]
        got = [piece.astype(full) for piece in got]
        step = wide // 4
        return jnp.concatenate(
            [got[i][:, z * step : (z + 1) * step] for z in range(4) for i in range(4)], axis=1
        )

    def hidden_vector(self, value, hidden):
        devices = self.chips * 2 * self.fsdp
        if not self.cube:
            spread = jnp.zeros((hidden,), full)
            at = (self.row * 2 + self.core) * value.shape[0]
            return lax.dynamic_update_slice_in_dim(spread, value, at, 0).reshape(devices, -1)
        spread = jnp.zeros((4, 4, hidden // 16), full)
        spread = lax.dynamic_update_slice_in_dim(spread, value.reshape(4, 1, -1), self.corner, 1)
        return spread.reshape(devices, -1)


def per_device(
    tokens, encoder, cotangent, seq_lengths, source_lengths, pair_order, pair_flip,
    ln_gain, ln_bias, attn_bias, self_qkv, self_out, cross_q, cross_kv, cross_out,
    w_up, up_bias, w_down, down_bias,
):
    move = Exchange()
    resid = tokens[0].astype(full)
    source = encoder[0]
    grad_low = cotangent[0]
    rows, width = resid.shape
    src_rows = source.shape[0]
    depth = width // H
    ctx_count = lax.axis_size(CTX)
    parts = lax.axis_size("part")
    devices = ctx_count * move.fsdp
    here = lax.axis_index(CTX)
    part = lax.axis_index("part")

    plan = attention_plan(
        pair_order[0], pair_flip[0], seq_lengths[0], source_lengths[0],
        here, part, parts, rows, src_rows * ctx_count,
    )
    query_slot, key_slot, self_plan, cross_plan, group_plan, self_ranges, cross_ranges, group_ranges = plan

    small = [ln_gain, ln_bias, attn_bias.reshape(6, -1), down_bias[None]]
    bias_up = move.hidden_parts(up_bias, 0)
    if move.cube:
        small.append(bias_up.reshape(2, -1))
    small = move.gather_last(jnp.concatenate(small, axis=0)).astype(full)
    if move.cube:
        half = small.shape[1] // 2
        bias_up = jnp.concatenate([small[13, :half], small[14, :half], small[13, half:], small[14, half:]])
    bias_up = bias_up.astype(full)
    gains, shifts, biases, bias_down = small[0:3], small[3:6], small[6:12].reshape(2, 3, width), small[12]
    shards = (cross_kv, self_qkv, self_out, cross_q, cross_out)
    ckv_piece, qkv_piece, out_piece, cq_piece, cout_piece = [move.own_piece(w) for w in shards]
    bases = [jnp.concatenate([w, w], axis=0) if move.paired else w for w in shards]
    up_mine = move.up_part(w_up)
    down_mine = move.hidden_parts(w_down, 0)
    up_base = jnp.concatenate([up_mine, up_mine], axis=0)
    down_base = jnp.concatenate([down_mine, down_mine], axis=0)

    got_qkv = move.fetch(qkv_piece)
    group_source = lax.all_gather(source, HEADS, axis=0, tiled=True)

    norm_one, back_one = jax.vjp(layer_norm, resid, gains[0], shifts[0])
    normed_one = norm_one.astype(low)
    w_qkv = move.place(bases[1], got_qkv)
    ready = after(
        normed_one, *plan, bases[1], ckv_piece, out_piece, cq_piece, cout_piece, up_mine
    )
    projected = contract(w_qkv, ready, 0, 1)
    shift_qkv = jnp.concatenate([biases[0, 0], jnp.zeros((width,), full), biases[0, 1]])
    projected = (projected + shift_qkv[:, None]).astype(low)
    projected = projected.reshape(3, H, depth, rows).transpose(1, 0, 2, 3).reshape(H, 3 * depth, rows)
    own_heads = lax.all_to_all(projected, HEADS, 0, 0, tiled=True)

    got_out = move.fetch(out_piece, (got_qkv,))
    got_cq = move.fetch(cq_piece, (got_qkv,))
    got_cout = move.fetch(cout_piece, (own_heads,))
    got_ckv = move.fetch(ckv_piece, (got_qkv,))
    self_in = after(own_heads, got_ckv, bases[0], *bases[2:], up_base, down_base)
    all_heads = self_in if parts == 1 else lax.all_gather(self_in, "part", axis=0, tiled=True)
    self_args = (self_plan, query_slot, key_slot, self_ranges, self_in, all_heads)
    self_low, self_exact, self_lse = self_forward(*self_args)
    grad_quad, got_quad = move.quad_gather(after(grad_low, own_heads), (self_low,))
    out_low = after(self_low, got_out, got_cq, *got_quad)
    self_att = lax.all_to_all(out_low, HEADS, 0, 0, tiled=True).reshape(width, rows)
    w_ckv = move.place(bases[0], got_ckv, (own_heads,))
    w_out = move.place(bases[2], got_out, (self_low,))
    w_cq = move.place(bases[3], got_cq, (self_low,))
    w_cout = move.place(bases[4], got_cout, (self_att,))

    every_source = group_source
    if parts > 1:
        every_source = lax.all_gather(group_source, "part", axis=0, tiled=True)
    shift_ckv = jnp.concatenate([jnp.zeros((width,), full), biases[1, 1]])
    src_kv = (jnp.dot(every_source, w_ckv, preferred_element_type=full) + shift_ckv).astype(low)
    mixed_one = resid + contract(self_att, w_out, 0, 0) + biases[0, 2]

    norm_two, back_two = jax.vjp(layer_norm, mixed_one, gains[1], shifts[1])
    normed_two = norm_two.astype(low)
    cross_query = (contract(w_cq, normed_two, 0, 1) + biases[1, 0][:, None]).astype(low)
    if move.cube:
        got_up = move.trade(up_mine, ((self_low,), (self_att,)))
        cross_query = after(cross_query, got_up[0], got_cout)
    group_one = lax.all_gather(normed_one, HEADS, axis=0, tiled=True)
    cross_att, cross_exact, cross_lse = cross_forward(cross_plan, cross_ranges, cross_query, src_kv)
    mixed_two = mixed_one + contract(cross_att, w_cout, 0, 0) + biases[1, 2]

    head = lax.axis_index(HEADS)
    lse_rows = cross_lse[:, 0:2].reshape(H, 1, rows)
    kept = jnp.concatenate(
        [cross_exact.reshape(H, depth, rows), jnp.broadcast_to(lse_rows, (H, 8, rows))], axis=1
    )
    head_exact = lax.all_to_all(kept, HEADS, 0, 0, tiled=True)
    head_query = lax.all_to_all(cross_query.reshape(H, depth, rows), HEADS, 0, 0, tiled=True)
    head_cols = [
        lax.dynamic_slice_in_dim(w_ckv, i * width + head * depth, depth, 1) for i in range(2)
    ]
    head_shift = jnp.concatenate(
        [jnp.zeros((depth,), full), lax.dynamic_slice_in_dim(biases[1, 1], head * depth, depth, 0)]
    )
    head_kv = jnp.dot(every_source, jnp.concatenate(head_cols, axis=1), preferred_element_type=full)
    head_kv = (head_kv + head_shift).astype(low)

    norm_three, back_three = jax.vjp(layer_norm, mixed_two, gains[2], shifts[2])
    three_low = norm_three.astype(low)
    if move.cube:
        got_down = move.trade(down_mine, ((self_att,), (cross_att,)))
        three_low = after(three_low, got_up[1], got_down[0])
        w_upper = move.joined(up_base, got_up, ((self_att,), (cross_att,)))
    else:
        w_upper = lax.all_to_all(up_mine, "fsdp", 1, 0, tiled=True).reshape(width, -1)
        w_lower = down_mine
    wide = w_upper.shape[1]
    quad_three, _ = move.quad_gather(three_low)
    hidden_pre = jnp.dot(quad_three, w_upper, preferred_element_type=full) + bias_up
    if move.cube:
        w_lower = move.joined(down_base, got_down, ((cross_att,), (cross_att,)))
    activated, back_gelu = jax.vjp(gelu_tanh, hidden_pre)
    act_low = activated.astype(low)
    grad_act = contract(grad_quad, w_lower, 1, 1)
    grad_hidden = back_gelu(grad_act)[0].astype(low)
    grad_three, met = move.quad_sum(contract(grad_hidden, w_upper, 1, 1).astype(low))

    grad_out = grad_low.astype(full)
    grad_b_lower = column_sums(grad_low)
    grad_w_lower = contract(after(act_low, met), grad_quad, 0, 0).astype(low)
    grad_b_upper = column_sums(grad_hidden)
    sent = ()
    if move.cube:
        lower = grad_w_lower.reshape(2, 2, 2, -1, width)
        sent_a, lower = move.send_half(lower, 2, move.row, lambda v: move.swap(v, "fsdp"))
        sent = (sent_a,)
    grad_three = move.quad_end(grad_three, sent)
    grad_ln_three, gain_three, shift_three = back_three(grad_three)
    grad_two = grad_out + grad_ln_three

    grad_two_low = grad_two.astype(low)
    grad_b_cout = column_sums(grad_two_low)
    grad_cross_att = contract(w_cout, grad_two_low, 1, 1).astype(low)
    sent_cross = after(grad_cross_att.reshape(H, depth, rows), *sent) if sent else grad_cross_att.reshape(H, depth, rows)
    grad_head = lax.all_to_all(sent_cross, HEADS, 0, 0, tiled=True)
    grad_w_upper = contract(after(quad_three, grad_cross_att), grad_hidden, 0, 0).astype(low)
    got_lower = lower[1] if move.cube else grad_head
    head_in = after(grad_head, head_exact, head_query, head_kv, grad_w_upper, group_one)
    head_cq, head_dkv_rows = cross_backward(
        group_plan, query_slot, group_ranges, head_query, head_kv, head_in, head_exact,
        low if parts == 1 else full,
    )
    if parts > 1:
        head_dkv_rows = lax.psum_scatter(head_dkv_rows, "part", scatter_dimension=0, tiled=True).astype(low)
    head_cq_sent = after(head_cq, got_lower) if move.cube else head_cq
    grad_cq = lax.all_to_all(head_cq_sent, HEADS, 0, 0, tiled=True).reshape(width, rows)
    branch = jnp.dot(after(act_low, head_cq), w_lower, preferred_element_type=full).astype(low)
    result = mixed_two + move.quad_end(move.quad_sum(branch)[0]) + bias_down
    if move.cube:
        lower = move.add(lower, head_cq).astype(low)
        _, lower = move.send_half(lower, 1, move.near, lambda v: move.swap_chip(v, 2))
        upper = grad_w_upper.reshape(2, 2, 4, 2, -1, wide)
        sent_b, upper = move.send_half(upper, 3, move.row, lambda v: move.swap(v, "fsdp"))
    grad_b_cq = jnp.sum(grad_cq.astype(full), axis=1)
    grad_ln_two, gain_two, shift_two = back_two(contract(grad_cq, w_cq, 0, 1))
    grad_one = grad_two + grad_ln_two

    grad_one_low = grad_one.astype(low)
    grad_b_out = column_sums(grad_one_low)
    grad_self_att = contract(w_out, grad_one_low, 1, 1).astype(low).reshape(H, depth, rows)
    grad_heads = lax.all_to_all(grad_self_att, HEADS, 0, 0, tiled=True)
    grad_w_cout = contract(cross_att, grad_two_low, 1, 0).astype(low)
    grad_w_cq = contract(normed_two, grad_cq, 0, 1).astype(low)
    grad_w_out = contract(self_att, grad_one_low, 1, 0).astype(low)
    if move.cube:
        square = []
        for one in (grad_w_cout, grad_w_cq, grad_w_out):
            _, both = move.send_half(move.device_shape(one), 1, move.core, lambda v: move.swap(v, "core"))
            square.append(move.add(both).astype(low))
        square = jnp.stack(square, axis=1)
        square = square.reshape((2, 2, 2) + square.shape[1:])
        _, square = move.send_half(square, 2, move.chip & 1, lambda v: move.swap_chip(v, 1))
        grad_heads = after(grad_heads, square[0], upper[1])
        upper = move.add(upper, grad_self_att).astype(low)
        _, upper = move.send_half(upper, 1, move.near, lambda v: move.swap_chip(v, 2))
    head_dq, head_dkv, head_rows = self_backward(
        *self_args, grad_heads, self_exact, self_lse, low if parts == 1 else full
    )
    if parts > 1:
        head_dkv = lax.psum_scatter(head_dkv, "part", scatter_dimension=0, tiled=True).astype(low)
    head_grad = jnp.concatenate([head_dq, head_dkv], axis=1)
    if parts > 1:
        head_rows = head_grad.transpose(1, 0, 2).reshape(3 * depth, H * rows)
    if move.cube:
        head_grad = after(head_grad, lower[1], upper[1], square[1])
    grad_qkv = lax.all_to_all(head_grad, HEADS, 0, 0, tiled=True)
    if move.cube:
        lower = move.add(lower, head_rows).astype(low)
        _, lower = move.send_half(lower, 0, move.far, lambda v: move.swap_chip(v, 4))
        upper = move.add(upper, head_rows).astype(low)
        _, upper = move.send_half(upper, 0, move.far, lambda v: move.swap_chip(v, 4))
        square = move.add(square, head_rows).astype(low)
        _, square = move.send_half(square, 1, move.near, lambda v: move.swap_chip(v, 2))
    grad_qkv = grad_qkv.reshape(H, 3, depth, rows).transpose(1, 0, 2, 3).reshape(3 * width, rows)
    sums = jnp.sum(grad_qkv.astype(full), axis=1).reshape(3, width)
    grad_ln_one, gain_one, shift_one = back_one(contract(grad_qkv, w_qkv, 0, 1))
    grad_input = grad_one + grad_ln_one

    head_w = contract(head_rows, group_one, 1, 0).astype(low)
    head_c = contract(group_source, head_dkv_rows, 0, 0).astype(low)
    own_dkv = lax.all_to_all(head_dkv_rows.reshape(H, src_rows, 2 * depth), HEADS, 0, 0, tiled=True)
    own_dk = own_dkv[:, :, :depth].transpose(1, 0, 2).reshape(src_rows, width)
    own_dv = own_dkv[:, :, depth:].transpose(1, 0, 2).reshape(src_rows, width)
    head_all = jnp.concatenate([head_w.T, head_c], axis=1)
    grad_source = contract(jnp.concatenate([own_dk, own_dv], axis=1), w_ckv, 1, 1)
    grad_b_cv = column_sums(own_dv)
    cols = head_all.shape[1]
    share = width // devices

    if move.cube:
        lower_own = move.add(lower, grad_qkv)
        square = move.add(square, grad_qkv).astype(low)
        _, square = move.send_half(square, 0, move.far, lambda v: move.swap_chip(v, 4))
        square = move.add(square).astype(low)
        _, square = move.send_half(square, 1, move.row, lambda v: move.swap(v, "fsdp"))
        cout_own, cq_own, out_own = tuple(move.add(square))
        upper_own = move.corner_columns(move.add(upper, grad_qkv).astype(low))
    else:
        lower_own = move.to_owner(move.chip_scatter(grad_w_lower).astype(low)).astype(full)
        upper_own = move.quad_columns(move.chip_scatter(grad_w_upper).astype(low)).astype(full)
        cout_own, cq_own, out_own = move.device_scatter([grad_w_cout, grad_w_cq, grad_w_out])

    vectors = jnp.stack(
        [gain_one, gain_two, gain_three, shift_one, shift_two, shift_three,
         sums[0], sums[2], grad_b_out, grad_b_cq, grad_b_cv, grad_b_cout, grad_b_lower]
    )
    vectors = vectors.reshape(13, devices, share).transpose(1, 0, 2).reshape(devices, 13 * share)
    hidden = wide * 2 * move.fsdp
    upper_sums = move.hidden_vector(grad_b_upper, hidden)
    vectors = jnp.concatenate([vectors, upper_sums], axis=1)
    used = vectors.shape[1]
    extra = -(-used // cols)
    vectors = jnp.pad(vectors, ((0, 0), (0, extra * cols - used))).reshape(devices, extra, cols)
    outgoing = jnp.concatenate([head_all.reshape(devices, share, cols), vectors.astype(low)], axis=1)
    incoming = lax.all_to_all(outgoing, ALL, 0, 0, tiled=True)
    heads_in = incoming[:, :share].reshape(parts, H, move.fsdp, share, cols)
    qkv_own, ckv_own = owned_columns(heads_in, depth)
    tail = jnp.sum(incoming[:, share:].astype(full), axis=0).reshape(-1)
    vec = tail[: 13 * share].reshape(13, share)
    bup_own = tail[13 * share : used]
    return (
        result.astype(low)[None],
        grad_input[None],
        grad_source[None],
        vec[0:3],
        vec[3:6],
        vec[6:12].reshape(2, 3, share),
        qkv_own,
        out_own,
        cq_own,
        ckv_own,
        cout_own,
        upper_own,
        bup_own,
        lower_own,
        vec[12],
    )


def solution(mesh):
    ctx, fsdp = mesh.shape["ctx"], mesh.shape["fsdp"]
    inner = Mesh(mesh.devices.reshape(ctx // H, H // 2, 2, fsdp), ALL)
    tokens = P("fsdp", CTX, None)
    group = P("fsdp", None)
    owned = P(ALL, None)
    return jax.shard_map(
        per_device,
        mesh=inner,
        in_specs=(tokens,) * 3
        + (group,) * 4
        + (P(None, "fsdp"), P(None, "fsdp"), P(None, None, "fsdp"))
        + (group,) * 6
        + (P("fsdp"), group, P("fsdp")),
        out_specs=(tokens,) * 3
        + (P(None, ALL), P(None, ALL), P(None, None, ALL))
        + (owned,) * 6
        + (P(ALL), owned, P(ALL)),
        check_vma=False,
    )
```

time: 843 us -> 686 us (0.81)
  waiting for transfers between devices: 358 us -> 197 us
  Pallas kernels: 140 us -> 85.5 us
  starting transfers between devices: 60.2 us -> 103 us
  matrix products: 102 us -> 118 us
  other arithmetic: 43.3 us -> 55.9 us
    ppermute x9 -> x12, waiting for transfers between devices: 161 us -> 50.4 us  [swap_chip(): return lax.ppermute(value, CHIP, [(i, i ^ bit) for i in range(self.chips)])]
    all_gather x6 -> x0, waiting for transfers between devices: 102 us -> none  [the longest x5 70.9 us: gather_weight(): return lax.all_gather(mine, ('fsdp', 'core'), axis=0, tiled=True)]
    pallas_call x1, Pallas kernels: 44.2 us -> 13.5 us  [cross_forward(): pl.pallas_call(functools.partial(cross_forward_kernel, cross_tile(count))...]
    pallas_call x1 -> x4, Pallas kernels: 47 us -> 22.4 us  [the longest x1 13.7 us: cross_backward(): pl.pallas_call(functools.partial(cross_backward_kernel, cross_tiles(queri...]
    all_to_all x1, waiting for transfers between devices: 0.01 us -> 24.5 us  [per_device(): grad_qkv = lax.all_to_all(head_grad, HEADS, 0, 0, tiled=True)]
    all_to_all x1, waiting for transfers between devices: 0.01 us -> 23 us  [per_device(): grad_heads = lax.all_to_all(grad_self_att, HEADS, 0, 0, tiled=True)]
    dynamic_update_slice x2 -> x15, local copies, waits for them, and re-layouts: 2.59 us -> 24.8 us  [the longest x5 10.9 us: place(): lax.dynamic_update_slice_in_dim(base, held, start + self.core * piece, 0)]
    all_to_all x2 -> x6, waiting for transfers between devices: 4 us -> 24.4 us  [the longest x1 16.1 us: per_device(): head_exact = lax.all_to_all(kept, HEADS, 0, 0, tiled=True)]
  transfers between devices with their start and end apart: 44 -> 53, of which waited for: 18 -> 15; matrix products, arithmetic and copies ran while one was open for 27% -> 37% of each run, Pallas kernels for 17% -> 12%
where the time goes in v2:
time: 686 us; the launch traced here: 679 us
  waiting for transfers between devices  197 us (29%)
  matrix products  118 us (17%)
  local copies, waits for them, and re-layouts  104 us (15%)
  starting transfers between devices  103 us (15%)
  Pallas kernels  85.5 us (12%)
  other arithmetic  55.9 us (8%)
  between operations  15.9 us (2%)
    dot_general x18, matrix products, contract(): lax.dot_general(left, right, (((left_dim,), (right_dim,)), ((), ())), pre...  71.4 us
    ppermute x28, waiting for transfers between devices, swap(): return lax.ppermute(value, axis, [(0, 1), (1, 0)])  65 us
    ppermute x12, waiting for transfers between devices, swap_chip(): return lax.ppermute(value, CHIP, [(i, i ^ bit) for i in range(self.chips)])  50.4 us
    pallas_call x1, Pallas kernels, self_backward(): pl.pallas_call(functools.partial(self_backward_kernel, tile), out_shape=(...  27.6 us
    ppermute x28, starting transfers between devices, swap(): return lax.ppermute(value, axis, [(0, 1), (1, 0)])  26.2 us
    unnamed x191, local copies, waits for them, and re-layouts  24.5 us
    all_to_all x1, waiting for transfers between devices, per_device(): grad_qkv = lax.all_to_all(head_grad, HEADS, 0, 0, tiled=True)  24.5 us
    all_to_all x1, waiting for transfers between devices, per_device(): grad_heads = lax.all_to_all(grad_self_att, HEADS, 0, 0, tiled=True)  23 us
  transfers between devices with their start and end apart: 53, of which 15 were waited for; matrix products, arithmetic and copies ran while one was open for 37% of the time, Pallas kernels for 12%

profile of v2, /device:TPU:0, one launch (start us, length us, event | category | flops | bytes accessed | tf_op | source)
XLA Modules:
  0.0 679.2 jit_solution(3165014900011619883)
XLA Ops:
  20.9 30.2 %collective-permute-done = bf16[256,3072]{1,0:T(8,128)(2,1)} collective-permute-done((bf16[256,3072]{1,0:T(8,128)(2,1)S(1)}, bf16[256,3072]{1,0:T(8,128)(2,1)}, u32[]{:S(2)}, u32[]{:S(2)}) %collective-permute-start) | collective-permute-done | bytes 1572896 | tf_op jit(solution)/shard_map/ppermute | solution.py:639
  101.5 9.6 %all-to-all-done.own_ref.all_ref = bf16[16,192,256]{2,1,0:T(8,128)(2,1)S(1)} async-done(((bf16[16,192,256]{2,1,0:T(8,128)(2,1)}), bf16[16,192,256]{2,1,0:T(8,128)(2,1)S(1)}, u32[]{:S(2)}, u32[]{:S(2)}) %all-to-all-start) | async-done | bytes 1572896 | tf_op jit(solution)/shard_map/all_to_all | solution.py:873
  121.3 22.0 %self_forward.1 = (bf16[16,64,256]{2,1,0:T(8,128)(2,1)}, f32[64,4096]{1,0:T(8,128)}, f32[8,4096]{1,0:T(8,128)}) custom-call(s32[4,8]{1,0:T(4,128)} %get-tuple-element.76.plan, s32[32]{0:T(128)} %get-tuple-element.77.query_slot, s32[32]{0:T(128)} %get-tuple-element.78.key_slot, s32[2,4096]{1,0:T(2,128)} %get-tuple-element.79.range_ref, ...), custom_call_target="tpu_custom_call" | custom-call | flops 1 | bytes 1 | tf_op jit(solution)/shard_map/self_forward/pallas_call | solution.py:452
  145.8 6.3 all-to-all-start.1
  164.6 8.3 %all-to-all-done.1 = bf16[16,64,256]{2,1,0:T(8,128)(2,1)S(1)} async-done(((bf16[16,64,256]{2,1,0:T(8,128)(2,1)}), bf16[16,64,256]{2,1,0:T(8,128)(2,1)S(1)}, u32[]{:S(2)}, u32[]{:S(2)}) %all-to-all-start.1) | async-done | bytes 524320 | tf_op jit(solution)/shard_map/all_to_all | solution.py:885
  180.2 10.8 %collective-permute-done.9 = bf16[256,2048]{1,0:T(8,128)(2,1)} collective-permute-done((bf16[256,2048]{1,0:T(8,128)(2,1)}, bf16[256,2048]{1,0:T(8,128)(2,1)}, u32[]{:S(2)}, u32[]{:S(2)}) %collective-permute-start.9) | collective-permute-done | bytes 1048608 | tf_op jit(solution)/shard_map/ppermute | solution.py:639
  193.0 14.0 %fusion.6.key_ref.value_ref = bf16[2048,2048]{1,0:T(8,128)(2,1)} fusion(f32[2048]{0:T(1024)S(1)} %concatenate.93, bf16[1024,2048]{1,0:T(8,128)(2,1)} %constant_dynamic-update-slice_fusion.49, bf16[1,2048,1024]{2,1,0:T(8,128)(2,1)} %all-gather.6.cloned.1.call-done), kind=kOutput, calls=%fused_computation.11 | convolution fusion | flops 8598323200 | bytes 16785408 | tf_op jit(solution)/shard_map/dot_general | solution.py:895
  207.0 13.5 %cross_forward.1 = (bf16[1024,256]{1,0:T(8,128)(2,1)}, f32[1024,256]{1,0:T(8,128)}, f32[8,8,256]{2,1,0:T(8,128)}) custom-call(s32[4,1]{1,0:T(4,128)} %get-tuple-element.80.plan, s32[2,256]{1,0:T(2,128)} %get-tuple-element.82.range_ref, bf16[1024,256]{1,0:T(8,128)(2,1)} %fusion.32.query_ref, bf16[2048,2048]{1,0:T(8,128)(2,1)} %fusion.6.key_ref.value_ref, ...), custom_call_target="tpu_custom_call" | custom-call | flops 1 | bytes 1 | tf_op jit(solution)/shard_map/cross_forward/pallas_call | solution.py:519
  220.5 11.1 %collective-permute-start.20 = (bf16[512,1024]{1,0:T(8,128)(2,1)S(1)}, bf16[512,1024]{1,0:T(8,128)(2,1)S(1)}, u32[]{:S(2)}, u32[]{:S(2)}) collective-permute-start(bf16[512,1024]{1,0:T(8,128)(2,1)S(1)} %copy-done.33), channel_id=1, source_target_pairs={{0,1},{1,0},{2,3},{3,2},{4,5},{5,4},{6,7},{7,6},{8,9},{9,8},{10,11... | collective-permute-start | bytes 3145736 | tf_op jit(solution)/shard_map/ppermute | solution.py:639
  254.2 6.8 collective-permute-done.20
  261.2 20.5 %fusion.75 = f32[1024,2048]{1,0:T(8,128)} fusion(bf16[1024,2048]{1,0:T(8,128)(2,1)S(1)} %constant_dynamic-update-slice_fusion.45, bf16[256,1024]{1,0:T(8,128)(2,1)S(1)} %collective-permute-done.17, bf16[256,1024]{1,0:T(8,128)(2,1)S(1)} %collective-permute-done.16, bf16[256,1024]{1,0:T(8,128)(2,1)S(1)} %collective-permute-done.15, ...), kind=kOutput, calls=%fused_computation.261 | convolution fusion | flops 4303355904 | bytes 14680064 | tf_op jit(solution)/shard_map/dot_general | solution.py:935
  281.7 14.7 %convert_reduce_fusion = (f32[2048]{0:T(1024)S(1)}, bf16[1024,2048]{1,0:T(8,128)(2,1)S(1)}, bf16[1024,2048]{1,0:T(8,128)(2,1)}) fusion(f32[1024,2048]{1,0:T(8,128)} %fusion.75, f32[2048]{0:T(1024)S(1)} %pad_maximum_fusion.9, bf16[1024,1024]{1,0:T(8,128)(2,1)S(1)} %constant_dynamic-update-slice_fusion.10, ...), kind=kOutput, calls=%fused_computation.12 | convolution fusion | flops 4355782656 | bytes 23085056 | tf_op jit(solution)/shard_map/dot_general | solution.py:41
  349.6 16.1 %all-to-all-done.4.exact_ref = f32[16,72,256]{2,1,0:T(8,128)} async-done(((f32[16,72,256]{2,1,0:T(8,128)}), f32[16,72,256]{2,1,0:T(8,128)}, u32[]{:S(2)}, u32[]{:S(2)}) %all-to-all-start.4) | async-done | bytes 1179680 | tf_op jit(solution)/shard_map/all_to_all | solution.py:913
  365.7 8.0 %all-to-all-start.3 = ((bf16[16,64,256]{2,1,0:T(8,128)(2,1)}), bf16[16,64,256]{2,1,0:T(8,128)(2,1)}, u32[]{:S(2)}, u32[]{:S(2)}) async-start(bf16[16,64,256]{2,1,0:T(8,128)(2,1)} %bitcast.319), calls=%async_computation.3 | async-start | bytes 1048576 | tf_op jit(solution)/shard_map/all_to_all | solution.py:961
  373.6 7.4 %convolution_convert_fusion = bf16[1024,2048]{1,0:T(8,128)(2,1)S(1)} fusion(bf16[1024,1024]{1,0:T(8,128)(2,1)} %pad_maximum_fusion.3, bf16[1024,2048]{1,0:T(8,128)(2,1)} %copy-done.75), kind=kOutput, calls=%fused_computation.25 | convolution fusion | flops 4297064448 | bytes 10485760 | tf_op jit(solution)/shard_map/dot_general | solution.py:41
  388.3 13.7 %cross_backward.1 = (bf16[16,64,256]{2,1,0:T(8,128)(2,1)}, bf16[2048,128]{1,0:T(8,128)(2,1)}) custom-call(s32[4,8]{1,0:T(4,128)} %get-tuple-element.81.plan, s32[32]{0:T(128)} %get-tuple-element.77.query_slot, s32[2,4096]{1,0:T(2,128)} %get-tuple-element.83.range_ref, bf16[16,64,256]{2,1,0:T(8,128)(2,1)} %copy-done.46, ...), custom_call_target="tpu_custom_call" | custom-call | flops 1 | bytes 1 | tf_op jit(solution)/shard_map/cross_backward/pallas_call | solution.py:549
  416.9 7.9 %convolution_convert_fusion.5 = bf16[1024,1024]{1,0:T(8,128)(2,1)S(1)} fusion(bf16[1024,2048]{1,0:T(8,128)(2,1)} %get-tuple-element.117, bf16[2048,1024]{1,0:T(8,128)(2,1)} %copy-done.30), kind=kOutput, calls=%fused_computation.50 | convolution fusion | flops 4296015872 | bytes 10485760 | tf_op jit(solution)/shard_map/dot_general | solution.py:973
  469.0 23.0 %all-to-all-done.6.grad_ref = bf16[16,64,256]{2,1,0:T(8,128)(2,1)} async-done(((bf16[16,64,256]{2,1,0:T(8,128)(2,1)}), bf16[16,64,256]{2,1,0:T(8,128)(2,1)}, u32[]{:S(2)}, u32[]{:S(2)}) %all-to-all-start.6) | async-done | bytes 524320 | tf_op jit(solution)/shard_map/all_to_all | solution.py:987
  492.0 27.6 %self_backward.1 = (bf16[16,64,256]{2,1,0:T(8,128)(2,1)}, bf16[16,128,256]{2,1,0:T(8,128)(2,1)}, bf16[192,4096]{1,0:T(8,128)(2,1)}) custom-call(s32[4,8]{1,0:T(4,128)} %get-tuple-element.76.plan, s32[32]{0:T(128)} %get-tuple-element.77.query_slot, s32[32]{0:T(128)} %get-tuple-element.78.key_slot, s32[2,4096]{1,0:T(2,128)} %get-tuple-element.79.range_ref, ...), custom_call_target="tpu_custom_call" | custom-call | flops 1 | bytes 1 | tf_op jit(solution)/shard_map/self_backward/pallas_call | solution.py:477
  522.2 6.3 all-to-all-start.7
  558.5 24.5 %all-to-all-done.7 = bf16[16,192,256]{2,1,0:T(8,128)(2,1)S(1)} async-done(((bf16[16,192,256]{2,1,0:T(8,128)(2,1)}), bf16[16,192,256]{2,1,0:T(8,128)(2,1)S(1)}, u32[]{:S(2)}, u32[]{:S(2)}) %all-to-all-start.7) | async-done | bytes 1572896 | tf_op jit(solution)/shard_map/all_to_all | solution.py:1012
  583.1 28.3 %collective-permute-done.36 = bf16[4,32,2048]{2,1,0:T(8,128)(2,1)} collective-permute-done((bf16[4,32,2048]{2,1,0:T(8,128)(2,1)}, bf16[4,32,2048]{2,1,0:T(8,128)(2,1)}, u32[]{:S(2)}, u32[]{:S(2)}) %collective-permute-start.36) | collective-permute-done | bytes 524320 | tf_op jit(solution)/shard_map/ppermute | solution.py:642
  636.6 17.1 %collective-permute-done.34 = bf16[3,2,32,1024]{3,2,0,1:T(8,128)(2,1)} collective-permute-done((bf16[3,2,32,1024]{3,2,0,1:T(8,128)(2,1)}, bf16[3,2,32,1024]{3,2,0,1:T(8,128)(2,1)}, u32[]{:S(2)}, u32[]{:S(2)}) %collective-permute-start.34) | collective-permute-done | bytes 393248 | tf_op jit(solution)/shard_map/ppermute | solution.py:642
  655.3 7.8 %collective-permute-done.35 = bf16[3,32,1024]{2,1,0:T(8,128)(2,1)S(1)} collective-permute-done((bf16[3,32,1024]{2,1,0:T(8,128)(2,1)S(1)}, bf16[3,32,1024]{2,1,0:T(8,128)(2,1)S(1)}, u32[]{:S(2)}, u32[]{:S(2)}) %collective-permute-start.35) | collective-permute-done | bytes 196640 | tf_op jit(solution)/shard_map/ppermute | solution.py:639
  (465 shorter events, 307.9 us)
Async XLA Ops:
  7.2 185.8 %all-gather.6.cloned.1.call-start = ((), (), s32[]{:S(2)}) async-start(), calls=%async_computation.11 | async-start | bytes 4456448 | tf_op jit(solution)/shard_map/all_gather | solution.py:861
  10.3 49.7 %collective-permute-start.2 = (bf16[15,512]{1,0:T(8,128)(2,1)S(1)}, bf16[15,512]{1,0:T(8,128)(2,1)S(1)}, u32[]{:S(2)}, u32[]{:S(2)}) collective-permute-start(bf16[15,512]{1,0:T(8,128)(2,1)S(1)} %concatenate.83), channel_id=1, source_target_pairs={{0,1},{1,0},{2,3},{3,2},{4,5},{5,4},{6,7},{7,6},{8,9},{9,8},{10,11... | collective-permute-start | bytes 46088 | tf_op jit(solution)/shard_map/ppermute | solution.py:639
  73.1 37.9 %all-to-all-start = ((bf16[16,192,256]{2,1,0:T(8,128)(2,1)}), bf16[16,192,256]{2,1,0:T(8,128)(2,1)S(1)}, u32[]{:S(2)}, u32[]{:S(2)}) async-start(bf16[16,192,256]{2,1,0:T(8,128)(2,1)} %bitcast.297), calls=%async_computation | async-start | bytes 3145728 | tf_op jit(solution)/shard_map/all_to_all | solution.py:873
  79.1 309.3 %all-gather.4.cloned.1.call-start = ((), (), s32[]{:S(2)}) async-start(), calls=%async_computation.10 | async-start | bytes 8912896 | tf_op jit(solution)/shard_map/all_gather | solution.py:904
  98.3 45.0 %collective-permute-start.4 = (bf16[256,1024]{1,0:T(8,128)(2,1)}, bf16[256,1024]{1,0:T(8,128)(2,1)}, u32[]{:S(2)}, u32[]{:S(2)}) collective-permute-start(bf16[256,1024]{1,0:T(8,128)(2,1)} %constant_dynamic-slice_fusion.9), channel_id=1, source_target_pairs={{0,1},{1,0},{2,3},{3,2},{4,5},{5,4},{6,7},{7,6},{8,9},{9,8},{10,11... | collective-permute-start | bytes 1572872 | tf_op jit(solution)/shard_map/ppermute | solution.py:639
  100.9 44.8 %collective-permute-start.5 = (bf16[256,1024]{1,0:T(8,128)(2,1)S(1)}, bf16[256,1024]{1,0:T(8,128)(2,1)}, u32[]{:S(2)}, u32[]{:S(2)}) collective-permute-start(bf16[256,1024]{1,0:T(8,128)(2,1)S(1)} %copy-done.53), channel_id=1, source_target_pairs={{0,1},{1,0},{2,3},{3,2},{4,5},{5,4},{6,7},{7,6},{8,9},{9,8},{10,11... | collective-permute-start | bytes 1572872 | tf_op jit(solution)/shard_map/ppermute | solution.py:639
  121.2 41.0 %collective-permute-start.11 = (bf16[256,2048]{1,0:T(8,128)(2,1)}, bf16[256,2048]{1,0:T(8,128)(2,1)}, u32[]{:S(2)}, u32[]{:S(2)}) collective-permute-start(bf16[256,2048]{1,0:T(8,128)(2,1)} %collective-permute-done.3), channel_id=1, source_target_pairs={{0,2},{2,0},{1,3},{3,1},{4,6},{6,4},{5,7},{7,5},{8,10},{10,8},{9,1... | collective-permute-start | bytes 3145736 | tf_op jit(solution)/shard_map/ppermute | solution.py:639
  157.8 83.8 %collective-permute-start.18 = (bf16[256,1024]{1,0:T(8,128)(2,1)S(1)}, bf16[256,1024]{1,0:T(8,128)(2,1)S(1)}, u32[]{:S(2)}, u32[]{:S(2)}) collective-permute-start(bf16[256,1024]{1,0:T(8,128)(2,1)S(1)} %bitcast.296), channel_id=1, source_target_pairs={{0,2},{2,0},{1,3},{3,1},{4,6},{6,4},{5,7},{7,5},{8,10},{10,8},{9,1... | collective-permute-start | bytes 1572872 | tf_op jit(solution)/shard_map/ppermute | solution.py:639
  161.4 81.4 %collective-permute-start.19 = (bf16[256,1024]{1,0:T(8,128)(2,1)}, bf16[256,1024]{1,0:T(8,128)(2,1)}, u32[]{:S(2)}, u32[]{:S(2)}) collective-permute-start(bf16[256,1024]{1,0:T(8,128)(2,1)} %collective-permute-done.6), channel_id=1, source_target_pairs={{0,2},{2,0},{1,3},{3,1},{4,6},{6,4},{5,7},{7,5},{8,10},{10,8},{9,1... | collective-permute-start | bytes 1572872 | tf_op jit(solution)/shard_map/ppermute | solution.py:639
  172.9 47.6 %collective-permute-start.12 = (bf16[256,1024]{1,0:T(8,128)(2,1)}, bf16[256,1024]{1,0:T(8,128)(2,1)}, u32[]{:S(2)}, u32[]{:S(2)}) collective-permute-start(bf16[256,1024]{1,0:T(8,128)(2,1)} %collective-permute-done.10), channel_id=1, source_target_pairs={{0,2},{2,0},{1,3},{3,1},{4,6},{6,4},{5,7},{7,5},{8,10},{10,8},{9,1... | collective-permute-start | bytes 1572872 | tf_op jit(solution)/shard_map/ppermute | solution.py:639
  191.0 44.7 %collective-permute-start.13 = (bf16[256,2048]{1,0:T(8,128)(2,1)}, bf16[256,2048]{1,0:T(8,128)(2,1)}, u32[]{:S(2)}, u32[]{:S(2)}) collective-permute-start(bf16[256,2048]{1,0:T(8,128)(2,1)} %get-tuple-element.100), channel_id=1, source_target_pairs={{0,1},{1,0},{2,3},{3,2},{4,5},{5,4},{6,7},{7,6},{8,9},{9,8},{10,11... | collective-permute-start | bytes 3145736 | tf_op jit(solution)/shard_map/ppermute | solution.py:639
  191.5 48.3 %collective-permute-start.14 = (bf16[512,1024]{1,0:T(8,128)(2,1)}, bf16[512,1024]{1,0:T(8,128)(2,1)}, u32[]{:S(2)}, u32[]{:S(2)}) collective-permute-start(bf16[512,1024]{1,0:T(8,128)(2,1)} %get-tuple-element.101), channel_id=1, source_target_pairs={{0,1},{1,0},{2,3},{3,2},{4,5},{5,4},{6,7},{7,6},{8,9},{9,8},{10,11... | collective-permute-start | bytes 3145736 | tf_op jit(solution)/shard_map/ppermute | solution.py:639
  220.5 40.4 %collective-permute-start.20 = (bf16[512,1024]{1,0:T(8,128)(2,1)S(1)}, bf16[512,1024]{1,0:T(8,128)(2,1)S(1)}, u32[]{:S(2)}, u32[]{:S(2)}) collective-permute-start(bf16[512,1024]{1,0:T(8,128)(2,1)S(1)} %copy-done.33), channel_id=1, source_target_pairs={{0,1},{1,0},{2,3},{3,2},{4,5},{5,4},{6,7},{7,6},{8,9},{9,8},{10,11... | collective-permute-start | bytes 3145736 | tf_op jit(solution)/shard_map/ppermute | solution.py:639
  335.3 66.8 %collective-permute-start.25 = (bf16[2,2,256,1024]{3,2,1,0:T(8,128)(2,1)}, bf16[2,2,256,1024]{3,2,1,0:T(8,128)(2,1)}, u32[]{:S(2)}, u32[]{:S(2)}) collective-permute-start(bf16[2,2,256,1024]{3,2,1,0:T(8,128)(2,1)} %get-tuple-element.178), channel_id=1, source_target_pairs={{0,1},{1,0},{2,3},{3,2},{4,5},{5,4},{6,7},{7,6},{8,9},{9,8},{10,11... | collective-permute-start | bytes 6291464 | tf_op jit(solution)/shard_map/ppermute | solution.py:639
  383.6 59.2 %collective-permute-start.29 = (bf16[2,2,4,32,2048]{4,3,2,1,0:T(8,128)(2,1)}, bf16[2,2,4,32,2048]{4,3,2,1,0:T(8,128)(2,1)}, u32[]{:S(2)}, u32[]{:S(2)}) collective-permute-start(bf16[2,2,4,32,2048]{4,3,2,1,0:T(8,128)(2,1)} %get-tuple-element.176), channel_id=1, source_target_pairs={{0,1},{1,0},{2,3},{3,2},{4,5},{5,4},{6,7},{7,6},{8,9},{9,8},{10,11... | collective-permute-start | bytes 6291464 | tf_op jit(solution)/shard_map/ppermute | solution.py:639
  413.0 109.2 %collective-permute-start.30 = (bf16[2,256,1024]{2,1,0:T(8,128)(2,1)}, bf16[2,256,1024]{2,1,0:T(8,128)(2,1)}, u32[]{:S(2)}, u32[]{:S(2)}) collective-permute-start(bf16[2,256,1024]{2,1,0:T(8,128)(2,1)} %get-tuple-element.184), channel_id=1, source_target_pairs={{0,8},{4,12},{8,0},{12,4},{16,24},{20,28},{24,16},{28,20},{1,9},{5... | collective-permute-start | bytes 3145736 | tf_op jit(solution)/shard_map/ppermute | solution.py:642
  449.1 73.2 %collective-permute-start.32 = (bf16[2,2,3,2,32,1024]{5,4,2,3,0,1:T(8,128)(2,1)}, bf16[2,2,3,2,32,1024]{5,4,2,3,0,1:T(8,128)(2,1)}, u32[]{:S(2)}, u32[]{:S(2)}) collective-permute-start(bf16[2,2,3,2,32,1024]{5,4,2,3,0,1:T(8,128)(2,1)} %bitcast.284), channel_id=1, source_target_pairs={{0,4},{4,0},{8,12},{12,8},{16,20},{20,16},{24,28},{28,24},{1,5},{5... | collective-permute-start | bytes 4718600 | tf_op jit(solution)/shard_map/ppermute | solution.py:642
  452.2 70.0 %collective-permute-start.31 = (bf16[2,4,32,2048]{3,2,1,0:T(8,128)(2,1)}, bf16[2,4,32,2048]{3,2,1,0:T(8,128)(2,1)}, u32[]{:S(2)}, u32[]{:S(2)}) collective-permute-start(bf16[2,4,32,2048]{3,2,1,0:T(8,128)(2,1)} %get-tuple-element.186), channel_id=1, source_target_pairs={{0,8},{4,12},{8,0},{12,4},{16,24},{20,28},{24,16},{28,20},{1,9},{5... | collective-permute-start | bytes 3145736 | tf_op jit(solution)/shard_map/ppermute | solution.py:642
  453.7 38.3 %all-to-all-start.6 = ((bf16[16,64,256]{2,1,0:T(8,128)(2,1)}), bf16[16,64,256]{2,1,0:T(8,128)(2,1)}, u32[]{:S(2)}, u32[]{:S(2)}) async-start(bf16[16,64,256]{2,1,0:T(8,128)(2,1)} %bitcast.318), calls=%async_computation.6 | async-start | bytes 1048576 | tf_op jit(solution)/shard_map/all_to_all | solution.py:987
  465.9 69.9 %collective-permute-start.24 = (bf16[256,1024]{1,0:T(8,128)(2,1)}, bf16[256,1024]{1,0:T(8,128)(2,1)}, u32[]{:S(2)}, u32[]{:S(2)}) collective-permute-start(bf16[256,1024]{1,0:T(8,128)(2,1)} %fusion.54), channel_id=1, source_target_pairs={{0,4},{4,0},{8,12},{12,8},{16,20},{20,16},{24,28},{28,24},{1,5},{5... | collective-permute-start | bytes 1572872 | tf_op jit(solution)/shard_map/ppermute | solution.py:642
  522.2 60.7 %all-to-all-start.7 = ((bf16[16,192,256]{2,1,0:T(8,128)(2,1)}), bf16[16,192,256]{2,1,0:T(8,128)(2,1)S(1)}, u32[]{:S(2)}, u32[]{:S(2)}) async-start(bf16[16,192,256]{2,1,0:T(8,128)(2,1)} %pad_maximum_fusion.4), calls=%async_computation.7 | async-start | bytes 3145728 | tf_op jit(solution)/shard_map/all_to_all | solution.py:1012
  541.2 91.8 %collective-permute-start.40 = (bf16[256,1024]{1,0:T(8,128)(2,1)}, bf16[256,1024]{1,0:T(8,128)(2,1)}, u32[]{:S(2)}, u32[]{:S(2)}) collective-permute-start(bf16[256,1024]{1,0:T(8,128)(2,1)} %get-tuple-element.192), channel_id=1, source_target_pairs={{0,16},{4,20},{8,24},{12,28},{16,0},{20,4},{24,8},{28,12},{1,17},{... | collective-permute-start | bytes 1572872 | tf_op jit(solution)/shard_map/ppermute | solution.py:642
  547.0 64.4 %collective-permute-start.36 = (bf16[4,32,2048]{2,1,0:T(8,128)(2,1)}, bf16[4,32,2048]{2,1,0:T(8,128)(2,1)}, u32[]{:S(2)}, u32[]{:S(2)}) collective-permute-start(bf16[4,32,2048]{2,1,0:T(8,128)(2,1)} %get-tuple-element.194), channel_id=1, source_target_pairs={{0,16},{4,20},{8,24},{12,28},{16,0},{20,4},{24,8},{28,12},{1,17},{... | collective-permute-start | bytes 1572872 | tf_op jit(solution)/shard_map/ppermute | solution.py:642
  556.5 64.4 %collective-permute-start.33 = (bf16[2,3,2,32,1024]{4,3,1,2,0:T(8,128)(2,1)}, bf16[2,3,2,32,1024]{4,3,1,2,0:T(8,128)(2,1)}, u32[]{:S(2)}, u32[]{:S(2)}) collective-permute-start(bf16[2,3,2,32,1024]{4,3,1,2,0:T(8,128)(2,1)} %get-tuple-element.190), channel_id=1, source_target_pairs={{0,8},{4,12},{8,0},{12,4},{16,24},{20,28},{24,16},{28,20},{1,9},{5... | collective-permute-start | bytes 2359304 | tf_op jit(solution)/shard_map/ppermute | solution.py:642
  (106 other events, 1406.3 us)
Sparse Core Ops, SparseCore 0:
  13.5 50.7 all-gather.5
  121.4 81.6 all-gather.3

commit v3 on v2

--- a/solution.py
+++ b/solution.py
@@ -35,6 +35,15 @@
 
 def gelu_tanh(v):
     return 0.5 * v * (1.0 + jnp.tanh(0.7978845608028654 * (v + 0.044715 * v * v * v)))
+
+
+def in_thirds(value):
+    terms = []
+    for _ in range(3):
+        term = lax.reduce_precision(value, 8, 7)
+        terms.append(term.astype(low))
+        value = value - term
+    return terms
 
 
 def contract(left, right, left_dim, right_dim):
@@ -270,9 +279,16 @@
 
 
 def self_backward_kernel(
-    tiles, plan, query_slot, key_slot, range_ref, own_ref, all_ref, grad_ref, exact_ref, lse_ref,
-    dq_ref, dkv_ref, rows_ref, query_s, grad_s, key_s, keyt_s, value_s, dq_s, dk_s, dv_s,
+    tiles, joined, plan, query_slot, key_slot, range_ref, own_ref, all_ref, grad_ref, exact_ref, lse_ref,
+    *rest,
 ):
+    if joined:
+        carried_ref, dq_ref, *rest = rest
+        dkv_ref = dq_ref
+        dq_ref[:, dq_ref.shape[1] - carried_ref.shape[1] :, :] = carried_ref[...]
+    else:
+        dq_ref, dkv_ref, *rest = rest
+    rows_ref, query_s, grad_s, key_s, keyt_s, value_s, dq_s, dk_s, dv_s = rest
     query_tile, tile = tiles
     depth, queries = query_s.shape
     count = keyt_s.shape[1]
@@ -320,7 +336,7 @@
     def _(b):
         slot = query_slot[b]
         dq = (dq_s[:, tile_at(b, BLOCK)] * score_scale).astype(low)
-        dq_ref[slot >> 1, :, half_at(slot)] = dq
+        dq_ref[slot >> 1, 0:depth, half_at(slot)] = dq
         rows_ref[0:depth, tile_at(slot, BLOCK)] = dq
 
     @pl.loop(0, count // BLOCK)
@@ -328,8 +344,9 @@
         slot = key_slot[b]
         dk = dk_s[:, tile_at(b, BLOCK)].astype(dkv_ref.dtype)
         dv = dv_s[:, tile_at(b, BLOCK)].astype(dkv_ref.dtype)
-        dkv_ref[slot >> 1, 0:depth, half_at(slot)] = dk
-        dkv_ref[slot >> 1, depth : 2 * depth, half_at(slot)] = dv
+        at = depth if joined else 0
+        dkv_ref[slot >> 1, at : at + depth, half_at(slot)] = dk
+        dkv_ref[slot >> 1, at + depth : at + 2 * depth, half_at(slot)] = dv
         if count == queries:
             rows_ref[depth : 2 * depth, tile_at(slot, BLOCK)] = dk.astype(low)
             rows_ref[2 * depth : 3 * depth, tile_at(slot, BLOCK)] = dv.astype(low)
@@ -369,8 +386,8 @@
 
 
 def cross_backward_kernel(
-    tiles, plan, query_slot, range_ref, query_ref, keys_values_ref, grad_ref, exact_ref,
-    dq_ref, dkv_ref, query_s, grad_s, exact_s, keyt_s, dkv_s,
+    tiles, plan, query_slot, range_ref, query_ref, keys_values_ref, grad_ref,
+    dq_ref, dkv_ref, packed_ref, query_s, grad_s, keyt_s, dkv_s,
 ):
     query_tile, tile = tiles
     depth = query_ref.shape[1]
@@ -383,7 +400,6 @@
         at, there = tile_at(b, BLOCK), half_at(slot)
         query_s[:, at] = query_ref[slot >> 1, :, there] * low(score_scale)
         grad_s[:, at] = grad_ref[slot >> 1, :, there]
-        exact_s[:, at] = exact_ref[slot >> 1, :, there]
 
     @pl.loop(0, keyt_s.shape[1] // tile)
     def _(j):
@@ -396,10 +412,11 @@
     @pl.loop(0, queries // query_tile)
     def _(t):
         here = tile_at(t, query_tile)
-        grad = grad_s[:, here]
+        grad = grad_s[0:depth, here]
         start, stop = range_ref[0:1, here], range_ref[1:2, here]
-        lse = exact_s[depth : depth + 1, here]
-        delta = jnp.sum(grad.astype(full) * exact_s[0:depth, here], axis=0, keepdims=True)
+        extra = grad_s[depth : depth + 16, here].astype(full)
+        lse = extra[0:1] + extra[1:2] + extra[2:3]
+        delta = extra[3:4] + extra[4:5] + extra[5:6]
         wide_query = jnp.concatenate([query_s[:, here], blank], axis=0)
         wide_grad = jnp.concatenate([blank, grad], axis=0)
         sides = jnp.concatenate([wide_query, wide_grad], axis=1)
@@ -425,7 +442,12 @@
         slot = query_slot[b]
         dq_ref[slot >> 1, :, half_at(slot)] = query_s[:, tile_at(b, BLOCK)]
 
-    dkv_ref[...] = dkv_s[...].astype(dkv_ref.dtype)
+    total = dkv_s[...].astype(dkv_ref.dtype)
+    dkv_ref[...] = total
+    devices, half, _ = packed_ref.shape
+    total = total.reshape(devices, 2, half, 2 * depth)
+    packed_ref[:, :, 0 : 2 * depth] = total[:, 0].astype(low)
+    packed_ref[:, :, 2 * depth : 4 * depth] = total[:, 1].astype(low)
 
 
 def smem():
@@ -469,20 +491,26 @@
     )(plan, query_slot, key_slot, ranges, own, everyone)
 
 
-def self_backward(plan, query_slot, key_slot, ranges, own, everyone, grad, exact, lse, kv_type):
+def self_backward(plan, query_slot, key_slot, ranges, own, everyone, grad, exact, lse, kv_type, carried):
     heads, three, rows = own.shape
     depth = three // 3
     queries, count = heads * rows, everyone.shape[0] * rows
     tile = self_tiles(queries)
-    return pl.pallas_call(
-        functools.partial(self_backward_kernel, tile),
-        out_shape=(
+    joined = heads == everyone.shape[0]
+    if joined:
+        shapes = (jax.ShapeDtypeStruct((heads, 3 * depth + carried.shape[1], rows), low),)
+        extra = (carried,)
+    else:
+        shapes = (
             jax.ShapeDtypeStruct((heads, depth, rows), low),
             jax.ShapeDtypeStruct((everyone.shape[0], 2 * depth, rows), kv_type),
-            jax.ShapeDtypeStruct((3 * depth, queries), low),
-        ),
-        in_specs=[smem()] * 3 + [vmem()] * 6,
-        out_specs=(vmem(),) * 3,
+        )
+        extra = ()
+    return pl.pallas_call(
+        functools.partial(self_backward_kernel, tile, joined),
+        out_shape=shapes + (jax.ShapeDtypeStruct((3 * depth, queries), low),),
+        in_specs=[smem()] * 3 + [vmem()] * (6 + len(extra)),
+        out_specs=(vmem(),) * (len(shapes) + 1),
         scratch_shapes=[
             pltpu.VMEM((depth, queries), low),
             pltpu.VMEM((depth, queries), low),
@@ -496,7 +524,7 @@
         compiler_params=params(),
         cost_estimate=pl.CostEstimate(flops=1, bytes_accessed=1, transcendentals=0),
         name="self_backward",
-    )(plan, query_slot, key_slot, ranges, own, everyone, grad, exact, lse)
+    )(plan, query_slot, key_slot, ranges, own, everyone, grad, exact, lse, *extra)
 
 
 def cross_tiles(queries, count):
@@ -543,7 +571,7 @@
     )(plan, ranges, query, keys_values, keys_values)
 
 
-def cross_backward(plan, query_slot, ranges, query, keys_values, grad, exact, kv_type):
+def cross_backward(plan, query_slot, ranges, query, keys_values, grad, kv_type, parts):
     heads, depth, rows = query.shape
     queries, count = heads * rows, keys_values.shape[0]
     return pl.pallas_call(
@@ -551,24 +579,25 @@
         out_shape=(
             jax.ShapeDtypeStruct((heads, depth, rows), low),
             jax.ShapeDtypeStruct((count, 2 * depth), kv_type),
+            jax.ShapeDtypeStruct((parts, count // parts // 2, 4 * depth), low),
         ),
-        in_specs=[smem()] * 2 + [vmem()] * 5,
-        out_specs=(vmem(),) * 2,
+        in_specs=[smem()] * 2 + [vmem()] * 4,
+        out_specs=(vmem(),) * 3,
         scratch_shapes=[
             pltpu.VMEM((depth, queries), low),
-            pltpu.VMEM((depth, queries), low),
-            pltpu.VMEM((exact.shape[1], queries), full),
+            pltpu.VMEM((grad.shape[1], queries), low),
             pltpu.VMEM((depth, count), low),
             pltpu.VMEM((count, 2 * depth), full),
         ],
         compiler_params=params(),
         cost_estimate=pl.CostEstimate(flops=1, bytes_accessed=1, transcendentals=0),
         name="cross_backward",
-    )(plan, query_slot, ranges, query, keys_values, grad, exact)
-
-
-def copy_kernel(_, value_ref, out_ref):
-    out_ref[...] = value_ref[...]
+    )(plan, query_slot, ranges, query, keys_values, grad)
+
+
+def copy_kernel(_, value_ref, square_ref, row_ref):
+    square_ref[...] = value_ref[...]
+    row_ref[...] = value_ref[...]
 
 
 def strided_columns(value, first, step, wide):
@@ -576,12 +605,18 @@
     count = cols // (step * wide)
     return pl.pallas_call(
         copy_kernel,
-        out_shape=jax.ShapeDtypeStruct((rows, count * wide), value.dtype),
+        out_shape=(
+            jax.ShapeDtypeStruct((2 * rows, count // 2 * wide), value.dtype),
+            jax.ShapeDtypeStruct((rows, count * wide), value.dtype),
+        ),
         grid_spec=pltpu.PrefetchScalarGridSpec(
             num_scalar_prefetch=1,
             grid=(count,),
             in_specs=[pl.BlockSpec((rows, wide), lambda i, at: (0, i * step + at[0]))],
-            out_specs=pl.BlockSpec((rows, wide), lambda i, at: (0, i)),
+            out_specs=(
+                pl.BlockSpec((rows, wide), lambda i, at: (i // 2, i % 2)),
+                pl.BlockSpec((rows, wide), lambda i, at: (0, i)),
+            ),
         ),
         compiler_params=params(),
         name="strided_columns",
@@ -650,15 +685,22 @@
             return lax.all_gather(mine, ("fsdp", "core"), axis=0, tiled=True)
         return self.swap(after(mine, *begin) if begin else mine, "fsdp")
 
-    def place(self, base, across, hold=()):
+    def place(self, base, across, corner):
         if not self.paired:
             return across
         piece = across.shape[0]
-        held = after(across, *hold) if hold else across
-        corner = self.swap(held, "core")
         start = (1 - self.row) * 2 * piece
-        whole = lax.dynamic_update_slice_in_dim(base, held, start + self.core * piece, 0)
+        whole = lax.dynamic_update_slice_in_dim(base, across, start + self.core * piece, 0)
         return lax.dynamic_update_slice_in_dim(whole, corner, start + (1 - self.core) * piece, 0)
+
+    def place_all(self, bases, across):
+        corner = self.swap(across, "core") if self.paired else across
+        placed, at = [], 0
+        for base in bases:
+            cols = slice(at, at + base.shape[1])
+            placed.append(self.place(base, across[:, cols], corner[:, cols]))
+            at += base.shape[1]
+        return placed
 
     def gather_last(self, shard):
         if not self.paired:
@@ -687,20 +729,8 @@
         if self.cube:
             return strided_columns(shard, self.corner, 4, hidden // 16)
         split = shard.reshape(rows, self.fsdp, 2, hidden // (2 * self.fsdp))
-        return lax.dynamic_index_in_dim(split, self.core, 2, keepdims=False)
-
-    def trade(self, mine, begin):
-        half = mine.shape[0] // 2
-        return [
-            self.swap(after(mine[i * half : (i + 1) * half], *begin[i]), "fsdp") for i in range(2)
-        ]
-
-    def joined(self, base, theirs, hold):
-        half = theirs[0].shape[0]
-        start = (1 - self.row) * 2 * half
-        for i in range(2):
-            base = lax.dynamic_update_slice_in_dim(base, after(theirs[i], *hold[i]), start + i * half, 0)
-        return base
+        mine = lax.dynamic_index_in_dim(split, self.core, 2, keepdims=False)
+        return mine, mine
 
     def swap_beside(self, value):
         return self.swap_chip(value, 1) if self.cube else self.swap(value, "fsdp")
@@ -725,6 +755,24 @@
         got = self.swap_beside(both[1].astype(low))
         return (both[0], got), theirs
 
+    def quad_direct(self, value):
+        if not self.paired:
+            return lax.psum_scatter(value, QUAD, scatter_dimension=0, tiled=True).astype(full)
+        rows = value.shape[0] // 4
+        mine, beside, across, corner = [value[i * rows : (i + 1) * rows] for i in range(4)]
+        if self.cube:
+            moves = [(i, i ^ 3) for i in range(2 * self.chips)]
+            far = lax.ppermute(corner, CTX, moves)
+        else:
+            far = lax.ppermute(corner, QUAD, [(i, 3 - i) for i in range(4)])
+        return mine, self.swap(beside, "core"), self.swap_beside(across), far
+
+    def quad_total(self, pending, hold):
+        if not self.paired:
+            return pending
+        mine = after(pending[0], *hold)
+        return sum(piece.astype(full) for piece in (mine,) + pending[1:])
+
     def quad_end(self, pending, hold=()):
         if not self.paired:
             return pending
@@ -784,9 +832,7 @@
         value = value.reshape(share, 2, self.fsdp, wide).transpose(0, 2, 1, 3)
         return value.reshape(share, quad * wide)
 
-    def corner_columns(self, value):
-        _, share, wide = value.shape
-
+    def corner_columns(self, value, hold):
         def block(bits):
             return lax.dynamic_index_in_dim(value, self.corner ^ bits, 0, keepdims=False)
 
@@ -796,10 +842,11 @@
             self.swap_chip(block(2), 1),
             lax.ppermute(block(3), CTX, [(i, i ^ 3) for i in range(2 * self.chips)]),
         ]
+        got = [after(piece, *hold) for piece in got]
         got = [jnp.where(self.core == 0, got[i], got[i ^ 1]) for i in range(4)]
         got = [jnp.where(self.chip & 1 == 0, got[i], got[i ^ 2]) for i in range(4)]
         got = [piece.astype(full) for piece in got]
-        step = wide // 4
+        step = value.shape[2] // 4
         return jnp.concatenate(
             [got[i][:, z * step : (z + 1) * step] for z in range(4) for i in range(4)], axis=1
         )
@@ -849,44 +896,42 @@
         bias_up = jnp.concatenate([small[13, :half], small[14, :half], small[13, half:], small[14, half:]])
     bias_up = bias_up.astype(full)
     gains, shifts, biases, bias_down = small[0:3], small[3:6], small[6:12].reshape(2, 3, width), small[12]
-    shards = (cross_kv, self_qkv, self_out, cross_q, cross_out)
-    ckv_piece, qkv_piece, out_piece, cq_piece, cout_piece = [move.own_piece(w) for w in shards]
+    shards = (cross_kv, self_out, cross_q, cross_out)
+    middle = jnp.concatenate([move.own_piece(w) for w in shards], axis=1)
+    qkv_piece = move.own_piece(self_qkv)
     bases = [jnp.concatenate([w, w], axis=0) if move.paired else w for w in shards]
-    up_mine = move.up_part(w_up)
+    qkv_base = jnp.concatenate([self_qkv, self_qkv], axis=0) if move.paired else self_qkv
+    up_mine, up_local = move.up_part(w_up)
     down_mine = move.hidden_parts(w_down, 0)
-    up_base = jnp.concatenate([up_mine, up_mine], axis=0)
-    down_base = jnp.concatenate([down_mine, down_mine], axis=0)
+    if move.cube:
+        shard_rows = w_up.shape[0]
+        branch_piece = jnp.concatenate([up_mine, down_mine], axis=0)
+        up_base = jnp.concatenate([up_local, up_local], axis=0)
+        down_base = jnp.concatenate([down_mine, down_mine], axis=0)
+        later = (up_base, down_base, branch_piece)
+    else:
+        later = ()
 
     got_qkv = move.fetch(qkv_piece)
     group_source = lax.all_gather(source, HEADS, axis=0, tiled=True)
 
     norm_one, back_one = jax.vjp(layer_norm, resid, gains[0], shifts[0])
     normed_one = norm_one.astype(low)
-    w_qkv = move.place(bases[1], got_qkv)
-    ready = after(
-        normed_one, *plan, bases[1], ckv_piece, out_piece, cq_piece, cout_piece, up_mine
-    )
-    projected = contract(w_qkv, ready, 0, 1)
+    w_qkv, = move.place_all([qkv_base], after(got_qkv, *plan, *bases, middle, up_mine))
+    projected = contract(w_qkv, normed_one, 0, 1)
     shift_qkv = jnp.concatenate([biases[0, 0], jnp.zeros((width,), full), biases[0, 1]])
     projected = (projected + shift_qkv[:, None]).astype(low)
     projected = projected.reshape(3, H, depth, rows).transpose(1, 0, 2, 3).reshape(H, 3 * depth, rows)
     own_heads = lax.all_to_all(projected, HEADS, 0, 0, tiled=True)
 
-    got_out = move.fetch(out_piece, (got_qkv,))
-    got_cq = move.fetch(cq_piece, (got_qkv,))
-    got_cout = move.fetch(cout_piece, (own_heads,))
-    got_ckv = move.fetch(ckv_piece, (got_qkv,))
-    self_in = after(own_heads, got_ckv, bases[0], *bases[2:], up_base, down_base)
+    got_middle = move.fetch(middle, (got_qkv,))
+    self_in = after(own_heads, *later)
     all_heads = self_in if parts == 1 else lax.all_gather(self_in, "part", axis=0, tiled=True)
     self_args = (self_plan, query_slot, key_slot, self_ranges, self_in, all_heads)
     self_low, self_exact, self_lse = self_forward(*self_args)
-    grad_quad, got_quad = move.quad_gather(after(grad_low, own_heads), (self_low,))
-    out_low = after(self_low, got_out, got_cq, *got_quad)
-    self_att = lax.all_to_all(out_low, HEADS, 0, 0, tiled=True).reshape(width, rows)
-    w_ckv = move.place(bases[0], got_ckv, (own_heads,))
-    w_out = move.place(bases[2], got_out, (self_low,))
-    w_cq = move.place(bases[3], got_cq, (self_low,))
-    w_cout = move.place(bases[4], got_cout, (self_att,))
+    self_att = lax.all_to_all(self_low, HEADS, 0, 0, tiled=True).reshape(width, rows)
+    w_ckv, w_out, w_cq, w_cout = move.place_all(bases, after(got_middle, self_low))
+    grad_quad, got_quad = move.quad_gather(after(grad_low, self_low), (self_att,))
 
     every_source = group_source
     if parts > 1:
@@ -898,48 +943,48 @@
     norm_two, back_two = jax.vjp(layer_norm, mixed_one, gains[1], shifts[1])
     normed_two = norm_two.astype(low)
     cross_query = (contract(w_cq, normed_two, 0, 1) + biases[1, 0][:, None]).astype(low)
-    if move.cube:
-        got_up = move.trade(up_mine, ((self_low,), (self_att,)))
-        cross_query = after(cross_query, got_up[0], got_cout)
-    group_one = lax.all_gather(normed_one, HEADS, axis=0, tiled=True)
+    cross_query = after(cross_query, *got_quad) if move.cube else cross_query
+    group_one = lax.all_gather(after(norm_one, self_att).astype(low), HEADS, axis=0, tiled=True)
     cross_att, cross_exact, cross_lse = cross_forward(cross_plan, cross_ranges, cross_query, src_kv)
     mixed_two = mixed_one + contract(cross_att, w_cout, 0, 0) + biases[1, 2]
 
     head = lax.axis_index(HEADS)
-    lse_rows = cross_lse[:, 0:2].reshape(H, 1, rows)
-    kept = jnp.concatenate(
-        [cross_exact.reshape(H, depth, rows), jnp.broadcast_to(lse_rows, (H, 8, rows))], axis=1
-    )
-    head_exact = lax.all_to_all(kept, HEADS, 0, 0, tiled=True)
-    head_query = lax.all_to_all(cross_query.reshape(H, depth, rows), HEADS, 0, 0, tiled=True)
     head_cols = [
         lax.dynamic_slice_in_dim(w_ckv, i * width + head * depth, depth, 1) for i in range(2)
     ]
     head_shift = jnp.concatenate(
         [jnp.zeros((depth,), full), lax.dynamic_slice_in_dim(biases[1, 1], head * depth, depth, 0)]
     )
-    head_kv = jnp.dot(every_source, jnp.concatenate(head_cols, axis=1), preferred_element_type=full)
+    head_kv = jnp.dot(after(every_source, cross_att), jnp.concatenate(head_cols, axis=1), preferred_element_type=full)
     head_kv = (head_kv + head_shift).astype(low)
 
     norm_three, back_three = jax.vjp(layer_norm, mixed_two, gains[2], shifts[2])
     three_low = norm_three.astype(low)
     if move.cube:
-        got_down = move.trade(down_mine, ((self_att,), (cross_att,)))
-        three_low = after(three_low, got_up[1], got_down[0])
-        w_upper = move.joined(up_base, got_up, ((self_att,), (cross_att,)))
+        got_branch = move.swap(after(branch_piece, got_middle), "fsdp")
+        theirs = after(got_branch, cross_att)
+        start = (1 - move.row) * shard_rows
+        half = up_mine.shape[1]
+        w_upper = lax.dynamic_update_slice(up_base, theirs[:shard_rows], (start, 0))
+        w_upper = lax.dynamic_update_slice(w_upper, theirs[shard_rows : 2 * shard_rows], (start, half))
+        w_lower = lax.dynamic_update_slice_in_dim(
+            down_base, theirs[2 * shard_rows :], (1 - move.row) * down_mine.shape[0], 0
+        )
     else:
         w_upper = lax.all_to_all(up_mine, "fsdp", 1, 0, tiled=True).reshape(width, -1)
         w_lower = down_mine
     wide = w_upper.shape[1]
     quad_three, _ = move.quad_gather(three_low)
+    if move.cube:
+        quad_three = after(quad_three, got_branch, head_kv)
     hidden_pre = jnp.dot(quad_three, w_upper, preferred_element_type=full) + bias_up
-    if move.cube:
-        w_lower = move.joined(down_base, got_down, ((cross_att,), (cross_att,)))
+    head_query = after(cross_query.reshape(H, depth, rows), quad_three)
+    head_query = lax.all_to_all(head_query, HEADS, 0, 0, tiled=True)
     activated, back_gelu = jax.vjp(gelu_tanh, hidden_pre)
     act_low = activated.astype(low)
     grad_act = contract(grad_quad, w_lower, 1, 1)
     grad_hidden = back_gelu(grad_act)[0].astype(low)
-    grad_three, met = move.quad_sum(contract(grad_hidden, w_upper, 1, 1).astype(low))
+    grad_three, met = move.quad_sum(contract(after(grad_hidden, head_query), w_upper, 1, 1).astype(low))
 
     grad_out = grad_low.astype(full)
     grad_b_lower = column_sums(grad_low)
@@ -957,26 +1002,32 @@
     grad_two_low = grad_two.astype(low)
     grad_b_cout = column_sums(grad_two_low)
     grad_cross_att = contract(w_cout, grad_two_low, 1, 1).astype(low)
-    sent_cross = after(grad_cross_att.reshape(H, depth, rows), *sent) if sent else grad_cross_att.reshape(H, depth, rows)
-    grad_head = lax.all_to_all(sent_cross, HEADS, 0, 0, tiled=True)
+    cross_rows = grad_cross_att.reshape(H, depth, rows)
+    deltas = jnp.sum(cross_rows.astype(full) * cross_exact.reshape(H, depth, rows), axis=1)
+    lse_rows = cross_lse[:, 0:2].reshape(H, rows)
+    extra = jnp.stack(in_thirds(lse_rows) + in_thirds(deltas), axis=1)
+    extra = jnp.pad(extra, ((0, 0), (0, 10), (0, 0)))
+    cross_rows = jnp.concatenate([cross_rows, extra], axis=1)
+    grad_head = lax.all_to_all(cross_rows, HEADS, 0, 0, tiled=True)
     grad_w_upper = contract(after(quad_three, grad_cross_att), grad_hidden, 0, 0).astype(low)
-    got_lower = lower[1] if move.cube else grad_head
-    head_in = after(grad_head, head_exact, head_query, head_kv, grad_w_upper, group_one)
-    head_cq, head_dkv_rows = cross_backward(
-        group_plan, query_slot, group_ranges, head_query, head_kv, head_in, head_exact,
-        low if parts == 1 else full,
+    branch = jnp.dot(after(act_low, grad_cross_att), w_lower, preferred_element_type=full).astype(low)
+    branch_sum = move.quad_direct(branch)
+    sent_b = grad_w_upper
+    if move.cube:
+        upper = grad_w_upper.reshape(2, 2, 4, 2, -1, wide)
+        sent_b, upper = move.send_half(upper, 3, move.row, lambda v: move.swap(v, "fsdp"))
+    head_in = after(grad_head, head_query, head_kv, sent_b, group_one)
+    head_cq, head_dkv_rows, packed_dkv = cross_backward(
+        group_plan, query_slot, group_ranges, head_query, head_kv, head_in,
+        low if parts == 1 else full, ctx_count,
     )
     if parts > 1:
         head_dkv_rows = lax.psum_scatter(head_dkv_rows, "part", scatter_dimension=0, tiled=True).astype(low)
-    head_cq_sent = after(head_cq, got_lower) if move.cube else head_cq
+    head_cq_sent = after(head_cq, lower[1]) if move.cube else head_cq
     grad_cq = lax.all_to_all(head_cq_sent, HEADS, 0, 0, tiled=True).reshape(width, rows)
-    branch = jnp.dot(after(act_low, head_cq), w_lower, preferred_element_type=full).astype(low)
-    result = mixed_two + move.quad_end(move.quad_sum(branch)[0]) + bias_down
     if move.cube:
         lower = move.add(lower, head_cq).astype(low)
         _, lower = move.send_half(lower, 1, move.near, lambda v: move.swap_chip(v, 2))
-        upper = grad_w_upper.reshape(2, 2, 4, 2, -1, wide)
-        sent_b, upper = move.send_half(upper, 3, move.row, lambda v: move.swap(v, "fsdp"))
     grad_b_cq = jnp.sum(grad_cq.astype(full), axis=1)
     grad_ln_two, gain_two, shift_two = back_two(contract(grad_cq, w_cq, 0, 1))
     grad_one = grad_two + grad_ln_two
@@ -985,92 +1036,117 @@
     grad_b_out = column_sums(grad_one_low)
     grad_self_att = contract(w_out, grad_one_low, 1, 1).astype(low).reshape(H, depth, rows)
     grad_heads = lax.all_to_all(grad_self_att, HEADS, 0, 0, tiled=True)
-    grad_w_cout = contract(cross_att, grad_two_low, 1, 0).astype(low)
-    grad_w_cq = contract(normed_two, grad_cq, 0, 1).astype(low)
-    grad_w_out = contract(self_att, grad_one_low, 1, 0).astype(low)
+    grad_w_cout = contract(after(cross_att, head_cq), grad_two_low, 1, 0).astype(low)
+    grad_w_cq = contract(after(normed_two, grad_self_att), grad_cq, 0, 1).astype(low)
+    grad_w_out = contract(after(self_att, grad_self_att), grad_one_low, 1, 0).astype(low)
     if move.cube:
         square = []
         for one in (grad_w_cout, grad_w_cq, grad_w_out):
             _, both = move.send_half(move.device_shape(one), 1, move.core, lambda v: move.swap(v, "core"))
             square.append(move.add(both).astype(low))
-        square = jnp.stack(square, axis=1)
-        square = square.reshape((2, 2, 2) + square.shape[1:])
-        _, square = move.send_half(square, 2, move.chip & 1, lambda v: move.swap_chip(v, 1))
-        grad_heads = after(grad_heads, square[0], upper[1])
+        sent_c, square = move.send_half(jnp.stack(square, axis=1), 2, move.row, lambda v: move.swap(v, "fsdp"))
         upper = move.add(upper, grad_self_att).astype(low)
-        _, upper = move.send_half(upper, 1, move.near, lambda v: move.swap_chip(v, 2))
-    head_dq, head_dkv, head_rows = self_backward(
-        *self_args, grad_heads, self_exact, self_lse, low if parts == 1 else full
+        sent_b, upper = move.send_half(upper, 1, move.near, lambda v: move.swap_chip(v, 2))
+        grad_heads = after(grad_heads, sent_b, sent_c)
+    *head_grads, head_rows = self_backward(
+        *self_args, grad_heads, self_exact, self_lse, low if parts == 1 else full, packed_dkv
     )
     if parts > 1:
-        head_dkv = lax.psum_scatter(head_dkv, "part", scatter_dimension=0, tiled=True).astype(low)
-    head_grad = jnp.concatenate([head_dq, head_dkv], axis=1)
-    if parts > 1:
+        head_dkv = lax.psum_scatter(head_grads[1], "part", scatter_dimension=0, tiled=True).astype(low)
+        head_grad = jnp.concatenate([head_grads[0], head_dkv], axis=1)
         head_rows = head_grad.transpose(1, 0, 2).reshape(3 * depth, H * rows)
-    if move.cube:
-        head_grad = after(head_grad, lower[1], upper[1], square[1])
+        own_dkv = lax.all_to_all(head_dkv_rows.reshape(H, src_rows, 2 * depth), HEADS, 0, 0, tiled=True)
+    else:
+        head_grad = head_grads[0]
+    if move.cube:
+        head_grad = after(head_grad, upper[1], square[1])
     grad_qkv = lax.all_to_all(head_grad, HEADS, 0, 0, tiled=True)
-    if move.cube:
+    if parts == 1:
+        packed = grad_qkv[:, 3 * depth :]
+        own_dkv = jnp.concatenate([packed[:, :, : 2 * depth], packed[:, :, 2 * depth :]], axis=1)
+        grad_qkv = grad_qkv[:, : 3 * depth]
+    if move.cube:
+        upper = move.add(upper, head_rows).astype(low)
+        sent_b, upper = move.send_half(upper, 0, move.far, lambda v: move.swap_chip(v, 4))
+        square = move.add(square, head_rows).astype(low)
+        square = square.reshape((2, 2, 2) + square.shape[1:])
+        sent_c, square = move.send_half(square, 2, move.chip & 1, lambda v: move.swap_chip(v, 1))
         lower = move.add(lower, head_rows).astype(low)
-        _, lower = move.send_half(lower, 0, move.far, lambda v: move.swap_chip(v, 4))
-        upper = move.add(upper, head_rows).astype(low)
-        _, upper = move.send_half(upper, 0, move.far, lambda v: move.swap_chip(v, 4))
-        square = move.add(square, head_rows).astype(low)
-        _, square = move.send_half(square, 1, move.near, lambda v: move.swap_chip(v, 2))
+        sent_a, lower = move.send_half(lower, 0, move.far, lambda v: move.swap_chip(v, 4))
+        soon = (sent_a, sent_b, sent_c)
+    else:
+        soon = (head_rows,)
+    head_w = contract(after(head_rows, *soon), group_one, 1, 0).astype(low)
+    head_c = contract(group_source, after(head_dkv_rows, *soon), 0, 0).astype(low)
+    flown = ()
+    if move.cube:
+        square = move.add(square, head_w).astype(low)
+        sent_a, square = move.send_half(square, 1, move.near, lambda v: move.swap_chip(v, 2))
+        flown = (sent_a,)
     grad_qkv = grad_qkv.reshape(H, 3, depth, rows).transpose(1, 0, 2, 3).reshape(3 * width, rows)
-    sums = jnp.sum(grad_qkv.astype(full), axis=1).reshape(3, width)
-    grad_ln_one, gain_one, shift_one = back_one(contract(grad_qkv, w_qkv, 0, 1))
+    grad_ln_one, gain_one, shift_one = back_one(contract(after(grad_qkv, *flown), w_qkv, 0, 1))
     grad_input = grad_one + grad_ln_one
 
-    head_w = contract(head_rows, group_one, 1, 0).astype(low)
-    head_c = contract(group_source, head_dkv_rows, 0, 0).astype(low)
-    own_dkv = lax.all_to_all(head_dkv_rows.reshape(H, src_rows, 2 * depth), HEADS, 0, 0, tiled=True)
     own_dk = own_dkv[:, :, :depth].transpose(1, 0, 2).reshape(src_rows, width)
     own_dv = own_dkv[:, :, depth:].transpose(1, 0, 2).reshape(src_rows, width)
     head_all = jnp.concatenate([head_w.T, head_c], axis=1)
     grad_source = contract(jnp.concatenate([own_dk, own_dv], axis=1), w_ckv, 1, 1)
-    grad_b_cv = column_sums(own_dv)
     cols = head_all.shape[1]
     share = width // devices
 
-    if move.cube:
-        lower_own = move.add(lower, grad_qkv)
-        square = move.add(square, grad_qkv).astype(low)
-        _, square = move.send_half(square, 0, move.far, lambda v: move.swap_chip(v, 4))
-        square = move.add(square).astype(low)
-        _, square = move.send_half(square, 1, move.row, lambda v: move.swap(v, "fsdp"))
-        cout_own, cq_own, out_own = tuple(move.add(square))
-        upper_own = move.corner_columns(move.add(upper, grad_qkv).astype(low))
-    else:
+    if not move.cube:
         lower_own = move.to_owner(move.chip_scatter(grad_w_lower).astype(low)).astype(full)
         upper_own = move.quad_columns(move.chip_scatter(grad_w_upper).astype(low)).astype(full)
         cout_own, cq_own, out_own = move.device_scatter([grad_w_cout, grad_w_cq, grad_w_out])
 
-    vectors = jnp.stack(
-        [gain_one, gain_two, gain_three, shift_one, shift_two, shift_three,
-         sums[0], sums[2], grad_b_out, grad_b_cq, grad_b_cv, grad_b_cout, grad_b_lower]
+    head_sums = jnp.sum(head_rows.astype(full), axis=1)
+    spread = [
+        lax.dynamic_update_slice_in_dim(jnp.zeros((width,), full), part, head * depth, 0)
+        for part in (head_sums[:depth], head_sums[2 * depth :], column_sums(head_dkv_rows[:, depth:]))
+    ]
+    early = [gain_two, gain_three, shift_two, shift_three, spread[0], spread[1],
+             grad_b_out, grad_b_cq, spread[2], grad_b_cout, grad_b_lower]
+
+    def by_owner(vectors):
+        stacked = jnp.stack(vectors).reshape(len(vectors), devices, share)
+        return stacked.transpose(1, 0, 2).reshape(devices, len(vectors) * share)
+
+    def in_rows(values):
+        count = -(-values.shape[1] // cols)
+        values = jnp.pad(values, ((0, 0), (0, count * cols - values.shape[1])))
+        return values.astype(low).reshape(devices, count, cols)
+
+    hidden = wide * 2 * move.fsdp
+    early_rows = in_rows(
+        jnp.concatenate([by_owner(early), move.hidden_vector(grad_b_upper, hidden)], axis=1)
     )
-    vectors = vectors.reshape(13, devices, share).transpose(1, 0, 2).reshape(devices, 13 * share)
-    hidden = wide * 2 * move.fsdp
-    upper_sums = move.hidden_vector(grad_b_upper, hidden)
-    vectors = jnp.concatenate([vectors, upper_sums], axis=1)
-    used = vectors.shape[1]
-    extra = -(-used // cols)
-    vectors = jnp.pad(vectors, ((0, 0), (0, extra * cols - used))).reshape(devices, extra, cols)
-    outgoing = jnp.concatenate([head_all.reshape(devices, share, cols), vectors.astype(low)], axis=1)
+    late_rows = in_rows(by_owner([gain_one, shift_one]))
+    outgoing = jnp.concatenate(
+        [head_all.reshape(devices, share, cols), early_rows, late_rows], axis=1
+    )
     incoming = lax.all_to_all(outgoing, ALL, 0, 0, tiled=True)
+    result = mixed_two + move.quad_total(branch_sum, soon) + bias_down
+    if move.cube:
+        lower_own = move.add(lower, outgoing)
+        upper_own = move.corner_columns(move.add(upper, outgoing).astype(low), (incoming,))
+        square = move.add(square, outgoing).astype(low)
+        _, square = move.send_half(square, 0, move.far, lambda v: move.swap_chip(v, 4))
+        cout_own, cq_own, out_own = tuple(move.add(square, incoming))
     heads_in = incoming[:, :share].reshape(parts, H, move.fsdp, share, cols)
     qkv_own, ckv_own = owned_columns(heads_in, depth)
-    tail = jnp.sum(incoming[:, share:].astype(full), axis=0).reshape(-1)
-    vec = tail[: 13 * share].reshape(13, share)
-    bup_own = tail[13 * share : used]
+    tail = jnp.sum(incoming[:, share:].astype(full), axis=0)
+    at = early_rows.shape[1]
+    first = tail[:at].reshape(-1)
+    vec = first[: 11 * share].reshape(11, share)
+    bup_own = first[11 * share : 11 * share + hidden // devices]
+    last = tail[at:].reshape(-1)[: 2 * share].reshape(2, share)
     return (
         result.astype(low)[None],
         grad_input[None],
         grad_source[None],
-        vec[0:3],
-        vec[3:6],
-        vec[6:12].reshape(2, 3, share),
+        jnp.stack([last[0], vec[0], vec[1]]),
+        jnp.stack([last[1], vec[2], vec[3]]),
+        vec[4:10].reshape(2, 3, share),
         qkv_own,
         out_own,
         cq_own,
@@ -1079,7 +1155,7 @@
         upper_own,
         bup_own,
         lower_own,
-        vec[12],
+        vec[10],
     )
 
 

time: 686 us -> 598 us (0.87)
  waiting for transfers between devices: 197 us -> 132 us
  starting transfers between devices: 103 us -> 80.7 us
  matrix products: 118 us -> 100 us
  Pallas kernels: 85.5 us -> 103 us
    ppermute x28 -> x19, waiting for transfers between devices: 65 us -> 26 us  [swap(): return lax.ppermute(value, axis, [(0, 1), (1, 0)])]
    all_to_all x5 -> x3, waiting for transfers between devices: 24.4 us -> 0.01 us  [the longest x1 0.01 us: per_device(): head_query = lax.all_to_all(head_query, HEADS, 0, 0, tiled=True)]
    all_to_all x1, waiting for transfers between devices: 23 us -> 0.01 us  [per_device(): grad_heads = lax.all_to_all(grad_self_att, HEADS, 0, 0, tiled=True)]
    ppermute x28 -> x19, starting transfers between devices: 26.2 us -> 11.6 us  [swap(): return lax.ppermute(value, axis, [(0, 1), (1, 0)])]
    ppermute x12, waiting for transfers between devices: 50.4 us -> 63.9 us  [swap_chip(): return lax.ppermute(value, CHIP, [(i, i ^ bit) for i in range(self.chips)])]
    dot_general x1, matrix products: 20.5 us -> 7.08 us  [per_device(): jnp.dot(quad_three, w_upper, preferred_element_type=full) + bias_up]
    all_to_all x1, waiting for transfers between devices: 9.58 us -> 22.2 us  [per_device(): own_heads = lax.all_to_all(projected, HEADS, 0, 0, tiled=True)]
    all_to_all x5 -> x3, starting transfers between devices: 29.4 us -> 18.1 us  [the longest x1 6.24 us: per_device(): head_query = lax.all_to_all(head_query, HEADS, 0, 0, tiled=True)]
  transfers between devices with their start and end apart: 53 -> 43, of which waited for: 15 -> 13; matrix products, arithmetic and copies ran while one was open for 37% -> 40% of each run, Pallas kernels for 12% -> 17%
where the time goes in v3:
time: 598 us; the launch traced here: 589 us
  waiting for transfers between devices  132 us (22%)
  Pallas kernels  103 us (17%)
  local copies, waits for them, and re-layouts  100 us (17%)
  matrix products  100 us (17%)
  starting transfers between devices  80.7 us (13%)
  other arithmetic  56.8 us (9%)
  between operations  15.7 us (3%)
    dot_general x18, matrix products, contract(): lax.dot_general(left, right, (((left_dim,), (right_dim,)), ((), ())), pre...  68.7 us
    ppermute x12, waiting for transfers between devices, swap_chip(): return lax.ppermute(value, CHIP, [(i, i ^ bit) for i in range(self.chips)])  63.9 us
    pallas_call x1, Pallas kernels, self_backward(): pl.pallas_call(functools.partial(self_backward_kernel, tile, joined), out...  28 us
    ppermute x19, waiting for transfers between devices, swap(): return lax.ppermute(value, axis, [(0, 1), (1, 0)])  26 us
    unnamed x181, local copies, waits for them, and re-layouts  24.1 us
    pallas_call x1, Pallas kernels, cross_forward(): pl.pallas_call(functools.partial(cross_forward_kernel, cross_tile(count))...  24 us
    all_to_all x1, waiting for transfers between devices, per_device(): own_heads = lax.all_to_all(projected, HEADS, 0, 0, tiled=True)  22.2 us
    pallas_call x1, Pallas kernels, self_forward(): pl.pallas_call(functools.partial(self_forward_kernel, tile), out_shape=(j...  22 us
  transfers between devices with their start and end apart: 43, of which 13 were waited for; matrix products, arithmetic and copies ran while one was open for 40% of the time, Pallas kernels for 17%

profile of v3, /device:TPU:0, one launch (start us, length us, event | category | flops | bytes accessed | tf_op | source)
XLA Modules:
  0.0 589.0 jit_solution(9968534682448247569)
XLA Ops:
  59.9 6.4 %all-to-all-start = ((bf16[16,192,256]{2,1,0:T(8,128)(2,1)}), bf16[16,192,256]{2,1,0:T(8,128)(2,1)S(1)}, u32[]{:S(2)}, u32[]{:S(2)}) async-start(bf16[16,192,256]{2,1,0:T(8,128)(2,1)} %bitcast.272), calls=%async_computation | async-start | bytes 3145728 | tf_op jit(solution)/shard_map/all_to_all | solution.py:925
  76.0 22.2 %all-to-all-done.own_ref.all_ref = bf16[16,192,256]{2,1,0:T(8,128)(2,1)S(1)} async-done(((bf16[16,192,256]{2,1,0:T(8,128)(2,1)}), bf16[16,192,256]{2,1,0:T(8,128)(2,1)S(1)}, u32[]{:S(2)}, u32[]{:S(2)}) %all-to-all-start) | async-done | bytes 1572896 | tf_op jit(solution)/shard_map/all_to_all | solution.py:925
  99.4 22.0 %self_forward.1 = (bf16[16,64,256]{2,1,0:T(8,128)(2,1)}, f32[64,4096]{1,0:T(8,128)}, f32[8,4096]{1,0:T(8,128)}) custom-call(s32[4,8]{1,0:T(4,128)} %get-tuple-element.80.plan, s32[32]{0:T(128)} %get-tuple-element.81.query_slot, s32[32]{0:T(128)} %get-tuple-element.82.key_slot, s32[2,4096]{1,0:T(2,128)} %get-tuple-element.83.range_ref, ...), custom_call_target="tpu_custom_call" | custom-call | flops 1 | bytes 1 | tf_op jit(solution)/shard_map/self_forward/pallas_call | solution.py:474
  126.0 5.8 all-to-all-start.1
  139.6 12.2 %collective-permute-done.5 = bf16[256,1024]{1,0:T(8,128)(2,1)S(1)} collective-permute-done((bf16[256,1024]{1,0:T(8,128)(2,1)S(1)}, bf16[256,1024]{1,0:T(8,128)(2,1)S(1)}, u32[]{:S(2)}, u32[]{:S(2)}) %collective-permute-start.5) | collective-permute-done | bytes 524320 | tf_op jit(solution)/shard_map/ppermute | solution.py:677
  164.7 14.4 %fusion.6.key_ref.value_ref = bf16[2048,2048]{1,0:T(8,128)(2,1)} fusion(f32[2048]{0:T(1024)S(1)} %concatenate.103, bf16[1024,2048]{1,0:T(8,128)(2,1)} %slice_dynamic-update-slice_fusion.1, bf16[1,2048,1024]{2,1,0:T(8,128)(2,1)} %all-gather.6.cloned.1.call-done), kind=kOutput, calls=%fused_computation.11 | convolution fusion | flops 8598323200 | bytes 16785408 | tf_op jit(solution)/shard_map/dot_general | solution.py:940
  181.8 24.0 %cross_forward.1 = (bf16[1024,256]{1,0:T(8,128)(2,1)}, f32[1024,256]{1,0:T(8,128)}, f32[8,8,256]{2,1,0:T(8,128)}) custom-call(s32[4,1]{1,0:T(4,128)} %get-tuple-element.84.plan, s32[2,256]{1,0:T(2,128)} %get-tuple-element.86.range_ref, bf16[1024,256]{1,0:T(8,128)(2,1)} %fusion.20.query_ref, bf16[2048,2048]{1,0:T(8,128)(2,1)} %fusion.6.key_ref.value_ref, ...), custom_call_target="tpu_custom_call" | custom-call | flops 1 | bytes 1 | tf_op jit(solution)/shard_map/cross_forward/pallas_call | solution.py:547
  210.1 16.2 %collective-permute-done.9 = bf16[2048,1024]{1,0:T(8,128)(2,1)} collective-permute-done((bf16[2048,1024]{1,0:T(8,128)(2,1)}, bf16[2048,1024]{1,0:T(8,128)(2,1)}, u32[]{:S(2)}, u32[]{:S(2)}) %collective-permute-start.9) | collective-permute-done | bytes 4194336 | tf_op jit(solution)/shard_map/ppermute | solution.py:674
  238.8 6.2 %all-to-all-start.2 = ((bf16[16,64,256]{2,1,0:T(8,128)(2,1)}), bf16[16,64,256]{2,1,0:T(8,128)(2,1)S(1)}, u32[]{:S(2)}, u32[]{:S(2)}) async-start(bf16[16,64,256]{2,1,0:T(8,128)(2,1)} %bitcast.283), calls=%async_computation.2 | async-start | bytes 1048576 | tf_op jit(solution)/shard_map/all_to_all | solution.py:982
  245.0 7.1 %fusion.79 = f32[1024,2048]{1,0:T(8,128)S(1)} fusion(bf16[1024,1024]{1,0:T(8,128)(2,1)} %pad_maximum_fusion.7, bf16[1024,2048]{1,0:T(8,128)(2,1)} %slice_dynamic-update-slice_fusion.2), kind=kOutput, calls=%fused_computation.297 | convolution fusion | flops 4294967296 | bytes 14680064 | tf_op jit(solution)/shard_map/dot_general | solution.py:980
  252.1 15.2 %convert_reduce_fusion = (f32[2048]{0:T(1024)S(1)}, bf16[1024,2048]{1,0:T(8,128)(2,1)}, bf16[1024,2048]{1,0:T(8,128)(2,1)}) fusion(f32[1024,2048]{1,0:T(8,128)S(1)} %fusion.79, f32[2048]{0:T(1024)S(1)} %pad_maximum_fusion.12, bf16[1024,1024]{1,0:T(8,128)(2,1)} %constant_dynamic-update-slice_fusion.10, bf16[2048,1024]{1,0:T(8,128)(2,1)S(1)} %copy-done.26), kind=kOutput, calls=%fused_computation.12 | convolution fusion | flops 4355782656 | bytes 23085056 | tf_op jit(solution)/shard_map/dot_general | solution.py:50
  267.3 8.2 %convolution_convert_fusion.6 = bf16[1024,1024]{1,0:T(8,128)(2,1)S(1)} fusion(bf16[1024,2048]{1,0:T(8,128)(2,1)} %get-tuple-element.104, bf16[1024,2048]{1,0:T(8,128)(2,1)} %slice_dynamic-update-slice_fusion.2), kind=kOutput, calls=%fused_computation.50 | convolution fusion | flops 4296015872 | bytes 10485760 | tf_op jit(solution)/shard_map/dot_general | solution.py:50
  285.2 6.6 %convolution_convert_fusion.1 = bf16[2048,1024]{1,0:T(8,128)(2,1)S(1)} fusion(bf16[1024,2048]{1,0:T(8,128)(2,1)S(1)} %copy-done.70, bf16[1024,1024]{1,0:T(8,128)(2,1)} %constant_dynamic-update-slice_fusion.10), kind=kOutput, calls=%fused_computation.24 | convolution fusion | flops 4297064448 | bytes 10485760 | tf_op jit(solution)/shard_map/dot_general | solution.py:50
  301.8 6.3 %convolution_convert_fusion = bf16[1024,2048]{1,0:T(8,128)(2,1)} fusion(bf16[1024,1024]{1,0:T(8,128)(2,1)S(1)} %copy-done.38, bf16[1024,2048]{1,0:T(8,128)(2,1)S(1)} %copy-done.69), kind=kOutput, calls=%fused_computation.23 | convolution fusion | flops 4297064448 | bytes 10485760 | tf_op jit(solution)/shard_map/dot_general | solution.py:50
  310.3 6.0 %all-to-all-start.3 = ((bf16[16,80,256]{2,1,0:T(8,128)(2,1)}), bf16[16,80,256]{2,1,0:T(8,128)(2,1)}, u32[]{:S(2)}, u32[]{:S(2)}) async-start(bf16[16,80,256]{2,1,0:T(8,128)(2,1)} %fusion.32), calls=%async_computation.3 | async-start | bytes 1310720 | tf_op jit(solution)/shard_map/all_to_all | solution.py:1011
  322.8 8.0 %convolution_convert_fusion.5 = bf16[1024,1024]{1,0:T(8,128)(2,1)S(1)} fusion(bf16[1024,2048]{1,0:T(8,128)(2,1)} %get-tuple-element.107, bf16[2048,1024]{1,0:T(8,128)(2,1)} %copy-done.25), kind=kOutput, calls=%fused_computation.49 | convolution fusion | flops 4296015872 | bytes 10485760 | tf_op jit(solution)/shard_map/dot_general | solution.py:1013
  334.2 19.3 %cross_backward.1 = (bf16[16,64,256]{2,1,0:T(8,128)(2,1)}, bf16[2048,128]{1,0:T(8,128)(2,1)}, bf16[16,64,256]{2,1,0:T(8,128)(2,1)}) custom-call(s32[4,8]{1,0:T(4,128)} %get-tuple-element.85.plan, s32[32]{0:T(128)} %get-tuple-element.81.query_slot, s32[2,4096]{1,0:T(2,128)} %get-tuple-element.87.range_ref, bf16[16,64,256]{2,1,0:T(8,128)(2,1)} %copy-done.35, ...), custom_call_target="tpu_custom_call" | custom-call | flops 1 | bytes 1 | tf_op jit(solution)/shard_map/cross_backward/pallas_call | solution.py:577
  401.7 28.0 %self_backward.1 = (bf16[16,256,256]{2,1,0:T(8,128)(2,1)}, bf16[192,4096]{1,0:T(8,128)(2,1)}) custom-call(s32[4,8]{1,0:T(4,128)} %get-tuple-element.80.plan, s32[32]{0:T(128)} %get-tuple-element.81.query_slot, s32[32]{0:T(128)} %get-tuple-element.82.key_slot, s32[2,4096]{1,0:T(2,128)} %get-tuple-element.83.range_ref, bf16[16,192,256]{2,1,0:T(8,128)(2,1)} %copy-done, ...), custom_call_target="tpu_custom_call" | custom-call | flops 1 | bytes 1 | tf_op jit(solution)/shard_map/self_backward/pallas_call | solution.py:509
  432.0 8.4 %collective-permute-done.20 = bf16[2,4,32,2048]{3,2,1,0:T(8,128)(2,1)} collective-permute-done((bf16[2,4,32,2048]{3,2,1,0:T(8,128)(2,1)}, bf16[2,4,32,2048]{3,2,1,0:T(8,128)(2,1)}, u32[]{:S(2)}, u32[]{:S(2)}) %collective-permute-start.20) | collective-permute-done | bytes 1048608 | tf_op jit(solution)/shard_map/ppermute | solution.py:677
  441.5 5.6 all-to-all-start.6
  469.7 23.0 %collective-permute-done.25 = bf16[2,2,3,32,1024]{4,3,2,0,1:T(8,128)(2,1)} collective-permute-done((bf16[2,2,3,32,1024]{4,3,2,0,1:T(8,128)(2,1)}, bf16[2,2,3,32,1024]{4,3,2,0,1:T(8,128)(2,1)}, u32[]{:S(2)}, u32[]{:S(2)}) %collective-permute-start.25) | collective-permute-done | bytes 786464 | tf_op jit(solution)/shard_map/ppermute | solution.py:677
  495.1 15.8 %all-to-all-done.6 = bf16[16,256,256]{2,1,0:T(8,128)(2,1)} async-done(((bf16[16,256,256]{2,1,0:T(8,128)(2,1)}), bf16[16,256,256]{2,1,0:T(8,128)(2,1)}, u32[]{:S(2)}, u32[]{:S(2)}) %all-to-all-start.6) | async-done | bytes 2097184 | tf_op jit(solution)/shard_map/all_to_all | solution.py:1063
  521.3 10.9 %all-to-all-start.7 = ((bf16[32,35,320]{2,1,0:T(8,128)(2,1)}), bf16[32,35,320]{2,1,0:T(8,128)(2,1)}, u32[]{:S(2)}, u32[]{:S(2)}) async-start(bf16[32,35,320]{2,1,0:T(8,128)(2,1)} %pad_maximum_fusion.8), calls=%async_computation.7 | async-start | bytes 1966080 | tf_op jit(solution)/shard_map/all_to_all | solution.py:1127
  532.1 18.7 %collective-permute-done.28 = bf16[4,32,2048]{2,1,0:T(8,128)(2,1)} collective-permute-done((bf16[4,32,2048]{2,1,0:T(8,128)(2,1)}, bf16[4,32,2048]{2,1,0:T(8,128)(2,1)}, u32[]{:S(2)}, u32[]{:S(2)}) %collective-permute-start.28) | collective-permute-done | bytes 524320 | tf_op jit(solution)/shard_map/ppermute | solution.py:677
  (451 shorter events, 256.7 us)
Async XLA Ops:
  7.2 157.5 %all-gather.6.cloned.1.call-start = ((), (), s32[]{:S(2)}) async-start(), calls=%async_computation.9 | async-start | bytes 4456448 | tf_op jit(solution)/shard_map/all_gather | solution.py:916
  10.1 37.8 %collective-permute-start = (bf16[256,3072]{1,0:T(8,128)(2,1)}, bf16[256,3072]{1,0:T(8,128)(2,1)}, u32[]{:S(2)}, u32[]{:S(2)}) collective-permute-start(bf16[256,3072]{1,0:T(8,128)(2,1)} %constant_dynamic-slice_fusion.11), channel_id=1, source_target_pairs={{0,1},{1,0},{2,3},{3,2},{4,5},{5,4},{6,7},{7,6},{8,9},{9,8},{10,11... | collective-permute-start | bytes 4718600 | tf_op jit(solution)/shard_map/ppermute | solution.py:674
  14.1 34.2 %collective-permute-start.2 = (bf16[15,512]{1,0:T(8,128)(2,1)S(1)}, bf16[15,512]{1,0:T(8,128)(2,1)S(1)}, u32[]{:S(2)}, u32[]{:S(2)}) collective-permute-start(bf16[15,512]{1,0:T(8,128)(2,1)S(1)} %concatenate.96), channel_id=1, source_target_pairs={{0,1},{1,0},{2,3},{3,2},{4,5},{5,4},{6,7},{7,6},{8,9},{9,8},{10,11... | collective-permute-start | bytes 46088 | tf_op jit(solution)/shard_map/ppermute | solution.py:674
  59.9 38.4 %all-to-all-start = ((bf16[16,192,256]{2,1,0:T(8,128)(2,1)}), bf16[16,192,256]{2,1,0:T(8,128)(2,1)S(1)}, u32[]{:S(2)}, u32[]{:S(2)}) async-start(bf16[16,192,256]{2,1,0:T(8,128)(2,1)} %bitcast.272), calls=%async_computation | async-start | bytes 3145728 | tf_op jit(solution)/shard_map/all_to_all | solution.py:925
  66.3 59.6 %collective-permute-start.3 = (bf16[256,5120]{1,0:T(8,128)(2,1)}, bf16[256,5120]{1,0:T(8,128)(2,1)}, u32[]{:S(2)}, u32[]{:S(2)}) collective-permute-start(bf16[256,5120]{1,0:T(8,128)(2,1)} %pad_maximum_fusion.6), channel_id=1, source_target_pairs={{0,1},{1,0},{2,3},{3,2},{4,5},{5,4},{6,7},{7,6},{8,9},{9,8},{10,11... | collective-permute-start | bytes 7864328 | tf_op jit(solution)/shard_map/ppermute | solution.py:674
  125.9 31.3 %collective-permute-start.4 = (bf16[256,5120]{1,0:T(8,128)(2,1)}, bf16[256,5120]{1,0:T(8,128)(2,1)}, u32[]{:S(2)}, u32[]{:S(2)}) collective-permute-start(bf16[256,5120]{1,0:T(8,128)(2,1)} %collective-permute-done.3), channel_id=1, source_target_pairs={{0,2},{2,0},{1,3},{3,1},{4,6},{6,4},{5,7},{7,5},{8,10},{10,8},{9,1... | collective-permute-start | bytes 7864328 | tf_op jit(solution)/shard_map/ppermute | solution.py:674
  131.9 202.3 %all-gather.4.cloned.1.call-start = ((), (), s32[]{:S(2)}) async-start(), calls=%async_computation.8 | async-start | bytes 8912896 | tf_op jit(solution)/shard_map/all_gather | solution.py:947
  133.1 93.2 %collective-permute-start.9 = (bf16[2048,1024]{1,0:T(8,128)(2,1)}, bf16[2048,1024]{1,0:T(8,128)(2,1)}, u32[]{:S(2)}, u32[]{:S(2)}) collective-permute-start(bf16[2048,1024]{1,0:T(8,128)(2,1)} %get-tuple-element.98), channel_id=1, source_target_pairs={{0,1},{1,0},{2,3},{3,2},{4,5},{5,4},{6,7},{7,6},{8,9},{9,8},{10,11... | collective-permute-start | bytes 12582920 | tf_op jit(solution)/shard_map/ppermute | solution.py:674
  210.0 27.3 %collective-permute-start.6 = (bf16[256,1024]{1,0:T(8,128)(2,1)S(1)}, bf16[256,1024]{1,0:T(8,128)(2,1)S(1)}, u32[]{:S(2)}, u32[]{:S(2)}) collective-permute-start(bf16[256,1024]{1,0:T(8,128)(2,1)S(1)} %add_convert_fusion.9), channel_id=1, source_target_pairs={{0,2},{2,0},{1,3},{3,1},{4,6},{6,4},{5,7},{7,5},{8,10},{10,8},{9,1... | collective-permute-start | bytes 1572872 | tf_op jit(solution)/shard_map/ppermute | solution.py:674
  238.8 28.5 %all-to-all-start.2 = ((bf16[16,64,256]{2,1,0:T(8,128)(2,1)}), bf16[16,64,256]{2,1,0:T(8,128)(2,1)S(1)}, u32[]{:S(2)}, u32[]{:S(2)}) async-start(bf16[16,64,256]{2,1,0:T(8,128)(2,1)} %bitcast.283), calls=%async_computation.2 | async-start | bytes 1048576 | tf_op jit(solution)/shard_map/all_to_all | solution.py:982
  294.3 59.2 %collective-permute-start.14 = (bf16[2,2,256,1024]{3,2,1,0:T(8,128)(2,1)}, bf16[2,2,256,1024]{3,2,1,0:T(8,128)(2,1)}, u32[]{:S(2)}, u32[]{:S(2)}) collective-permute-start(bf16[2,2,256,1024]{3,2,1,0:T(8,128)(2,1)} %get-tuple-element.215), channel_id=1, source_target_pairs={{0,1},{1,0},{2,3},{3,2},{4,5},{5,4},{6,7},{7,6},{8,9},{9,8},{10,11... | collective-permute-start | bytes 6291464 | tf_op jit(solution)/shard_map/ppermute | solution.py:674
  321.1 65.9 %collective-permute-start.15 = (bf16[2,2,4,32,2048]{4,3,2,1,0:T(8,128)(2,1)}, bf16[2,2,4,32,2048]{4,3,2,1,0:T(8,128)(2,1)}, u32[]{:S(2)}, u32[]{:S(2)}) collective-permute-start(bf16[2,2,4,32,2048]{4,3,2,1,0:T(8,128)(2,1)} %get-tuple-element.213), channel_id=1, source_target_pairs={{0,1},{1,0},{2,3},{3,2},{4,5},{5,4},{6,7},{7,6},{8,9},{9,8},{10,11... | collective-permute-start | bytes 6291464 | tf_op jit(solution)/shard_map/ppermute | solution.py:674
  332.2 134.1 %collective-permute-start.22 = (bf16[256,1024]{1,0:T(8,128)(2,1)}, bf16[256,1024]{1,0:T(8,128)(2,1)}, u32[]{:S(2)}, u32[]{:S(2)}) collective-permute-start(bf16[256,1024]{1,0:T(8,128)(2,1)} %get-tuple-element.235), channel_id=1, source_target_pairs={{0,2},{2,0},{1,3},{3,1},{4,6},{6,4},{5,7},{7,5},{8,10},{10,8},{9,1... | collective-permute-start | bytes 1572872 | tf_op jit(solution)/shard_map/ppermute | solution.py:674
  332.4 134.5 %collective-permute-start.23 = (bf16[256,1024]{1,0:T(8,128)(2,1)}, bf16[256,1024]{1,0:T(8,128)(2,1)}, u32[]{:S(2)}, u32[]{:S(2)}) collective-permute-start(bf16[256,1024]{1,0:T(8,128)(2,1)} %get-tuple-element.234), channel_id=1, source_target_pairs={{0,4},{4,0},{8,12},{12,8},{16,20},{20,16},{24,28},{28,24},{1,5},{5... | collective-permute-start | bytes 1572872 | tf_op jit(solution)/shard_map/ppermute | solution.py:677
  362.6 27.0 %collective-permute-start.16 = (bf16[8,2,32,1024]{3,2,1,0:T(8,128)(2,1)}, bf16[8,2,32,1024]{3,2,1,0:T(8,128)(2,1)}, u32[]{:S(2)}, u32[]{:S(2)}) collective-permute-start(bf16[8,2,32,1024]{3,2,1,0:T(8,128)(2,1)} %dynamic-slice_bitcast_fusion.10), channel_id=1, source_target_pairs={{0,2},{2,0},{1,3},{3,1},{4,6},{6,4},{5,7},{7,5},{8,10},{10,8},{9,1... | collective-permute-start | bytes 3145736 | tf_op jit(solution)/shard_map/ppermute | solution.py:674
  389.6 58.6 %collective-permute-start.19 = (bf16[2,256,1024]{2,1,0:T(8,128)(2,1)}, bf16[2,256,1024]{2,1,0:T(8,128)(2,1)}, u32[]{:S(2)}, u32[]{:S(2)}) collective-permute-start(bf16[2,256,1024]{2,1,0:T(8,128)(2,1)} %get-tuple-element.231), channel_id=1, source_target_pairs={{0,8},{4,12},{8,0},{12,4},{16,24},{20,28},{24,16},{28,20},{1,9},{5... | collective-permute-start | bytes 3145736 | tf_op jit(solution)/shard_map/ppermute | solution.py:677
  396.5 45.0 %collective-permute-start.21 = (bf16[8,3,32,1024]{3,2,0,1:T(8,128)(2,1)}, bf16[8,3,32,1024]{3,2,0,1:T(8,128)(2,1)}, u32[]{:S(2)}, u32[]{:S(2)}) collective-permute-start(bf16[8,3,32,1024]{3,2,0,1:T(8,128)(2,1)} %get-tuple-element.219), channel_id=1, source_target_pairs={{0,1},{1,0},{2,3},{3,2},{4,5},{5,4},{6,7},{7,6},{8,9},{9,8},{10,11... | collective-permute-start | bytes 4718600 | tf_op jit(solution)/shard_map/ppermute | solution.py:674
  398.7 41.8 %collective-permute-start.20 = (bf16[2,4,32,2048]{3,2,1,0:T(8,128)(2,1)}, bf16[2,4,32,2048]{3,2,1,0:T(8,128)(2,1)}, u32[]{:S(2)}, u32[]{:S(2)}) collective-permute-start(bf16[2,4,32,2048]{3,2,1,0:T(8,128)(2,1)} %get-tuple-element.229), channel_id=1, source_target_pairs={{0,8},{4,12},{8,0},{12,4},{16,24},{20,28},{24,16},{28,20},{1,9},{5... | collective-permute-start | bytes 3145736 | tf_op jit(solution)/shard_map/ppermute | solution.py:677
  441.5 69.3 %all-to-all-start.6 = ((bf16[16,256,256]{2,1,0:T(8,128)(2,1)}), bf16[16,256,256]{2,1,0:T(8,128)(2,1)}, u32[]{:S(2)}, u32[]{:S(2)}) async-start(bf16[16,256,256]{2,1,0:T(8,128)(2,1)} %get-tuple-element.130), calls=%async_computation.6 | async-start | bytes 4194304 | tf_op jit(solution)/shard_map/all_to_all | solution.py:1063
  451.1 116.7 %collective-permute-start.32 = (bf16[256,1024]{1,0:T(8,128)(2,1)}, bf16[256,1024]{1,0:T(8,128)(2,1)}, u32[]{:S(2)}, u32[]{:S(2)}) collective-permute-start(bf16[256,1024]{1,0:T(8,128)(2,1)} %get-tuple-element.241), channel_id=1, source_target_pairs={{0,16},{4,20},{8,24},{12,28},{16,0},{20,4},{24,8},{28,12},{1,17},{... | collective-permute-start | bytes 1572872 | tf_op jit(solution)/shard_map/ppermute | solution.py:677
  460.5 32.1 %collective-permute-start.25 = (bf16[2,2,3,32,1024]{4,3,2,0,1:T(8,128)(2,1)}, bf16[2,2,3,32,1024]{4,3,2,0,1:T(8,128)(2,1)}, u32[]{:S(2)}, u32[]{:S(2)}) collective-permute-start(bf16[2,2,3,32,1024]{4,3,2,0,1:T(8,128)(2,1)} %bitcast.262), channel_id=1, source_target_pairs={{0,4},{4,0},{8,12},{12,8},{16,20},{20,16},{24,28},{28,24},{1,5},{5... | collective-permute-start | bytes 2359304 | tf_op jit(solution)/shard_map/ppermute | solution.py:677
  466.3 84.5 %collective-permute-start.28 = (bf16[4,32,2048]{2,1,0:T(8,128)(2,1)}, bf16[4,32,2048]{2,1,0:T(8,128)(2,1)}, u32[]{:S(2)}, u32[]{:S(2)}) collective-permute-start(bf16[4,32,2048]{2,1,0:T(8,128)(2,1)} %get-tuple-element.243), channel_id=1, source_target_pairs={{0,16},{4,20},{8,24},{12,28},{16,0},{20,4},{24,8},{28,12},{1,17},{... | collective-permute-start | bytes 1572872 | tf_op jit(solution)/shard_map/ppermute | solution.py:677
  494.9 60.8 %collective-permute-start.26 = (bf16[2,3,32,1024]{3,2,1,0:T(8,128)(2,1)}, bf16[2,3,32,1024]{3,2,1,0:T(8,128)(2,1)}, u32[]{:S(2)}, u32[]{:S(2)}) collective-permute-start(bf16[2,3,32,1024]{3,2,1,0:T(8,128)(2,1)} %get-tuple-element.245), channel_id=1, source_target_pairs={{0,8},{4,12},{8,0},{12,4},{16,24},{20,28},{24,16},{28,20},{1,9},{5... | collective-permute-start | bytes 1179656 | tf_op jit(solution)/shard_map/ppermute | solution.py:677
  521.3 48.8 %all-to-all-start.7 = ((bf16[32,35,320]{2,1,0:T(8,128)(2,1)}), bf16[32,35,320]{2,1,0:T(8,128)(2,1)}, u32[]{:S(2)}, u32[]{:S(2)}) async-start(bf16[32,35,320]{2,1,0:T(8,128)(2,1)} %pad_maximum_fusion.8), calls=%async_computation.7 | async-start | bytes 1966080 | tf_op jit(solution)/shard_map/all_to_all | solution.py:1127
  (92 other events, 984.2 us)
Sparse Core Ops, SparseCore 0:
  14.3 52.2 all-gather.5
  155.6 77.4 all-gather.3

commit v4 on v3

--- a/solution.py
+++ b/solution.py
@@ -1071,9 +1071,7 @@
         square = move.add(square, head_rows).astype(low)
         square = square.reshape((2, 2, 2) + square.shape[1:])
         sent_c, square = move.send_half(square, 2, move.chip & 1, lambda v: move.swap_chip(v, 1))
-        lower = move.add(lower, head_rows).astype(low)
-        sent_a, lower = move.send_half(lower, 0, move.far, lambda v: move.swap_chip(v, 4))
-        soon = (sent_a, sent_b, sent_c)
+        soon = (sent_b, sent_c)
     else:
         soon = (head_rows,)
     head_w = contract(after(head_rows, *soon), group_one, 1, 0).astype(low)
@@ -1127,8 +1125,10 @@
     incoming = lax.all_to_all(outgoing, ALL, 0, 0, tiled=True)
     result = mixed_two + move.quad_total(branch_sum, soon) + bias_down
     if move.cube:
-        lower_own = move.add(lower, outgoing)
-        upper_own = move.corner_columns(move.add(upper, outgoing).astype(low), (incoming,))
+        lower = move.add(lower, outgoing).astype(low)
+        _, lower = move.send_half(lower, 0, move.far, lambda v: move.swap_chip(v, 4))
+        lower_own = move.add(lower, incoming)
+        upper_own = move.corner_columns(move.add(upper, grad_ln_one).astype(low), (incoming,))
         square = move.add(square, outgoing).astype(low)
         _, square = move.send_half(square, 0, move.far, lambda v: move.swap_chip(v, 4))
         cout_own, cq_own, out_own = tuple(move.add(square, incoming))

time: 598 us -> 596 us (level)
  waiting for transfers between devices: 132 us -> 117 us
  starting transfers between devices: 80.7 us -> 87.7 us
    ppermute x12, waiting for transfers between devices: 63.9 us -> 26.4 us  [swap_chip(): return lax.ppermute(value, CHIP, [(i, i ^ bit) for i in range(self.chips)])]
    all_to_all x1, waiting for transfers between devices: 0.01 us -> 22.9 us  [per_device(): incoming = lax.all_to_all(outgoing, ALL, 0, 0, tiled=True)]
    ppermute x12, starting transfers between devices: 17.9 us -> 28.7 us  [swap_chip(): return lax.ppermute(value, CHIP, [(i, i ^ bit) for i in range(self.chips)])]
    unnamed x181 -> x177, local copies, waits for them, and re-layouts: 24.1 us -> 24.2 us
  transfers between devices with their start and end apart: 43 -> 43, of which waited for: 13 -> 12; matrix products, arithmetic and copies ran while one was open for 40% -> 41% of each run, Pallas kernels for 17% -> 18%
where the time goes in v4:
time: 596 us; the launch traced here: 586 us
  waiting for transfers between devices  117 us (20%)
  matrix products  105 us (18%)
  Pallas kernels  103 us (17%)
  local copies, waits for them, and re-layouts  101 us (17%)
  starting transfers between devices  87.7 us (15%)
  other arithmetic  57.3 us (10%)
  between operations  16.1 us (3%)
    dot_general x18, matrix products, contract(): lax.dot_general(left, right, (((left_dim,), (right_dim,)), ((), ())), pre...  72 us
    ppermute x12, starting transfers between devices, swap_chip(): return lax.ppermute(value, CHIP, [(i, i ^ bit) for i in range(self.chips)])  28.7 us
    pallas_call x1, Pallas kernels, self_backward(): pl.pallas_call(functools.partial(self_backward_kernel, tile, joined), out...  28.2 us
    ppermute x12, waiting for transfers between devices, swap_chip(): return lax.ppermute(value, CHIP, [(i, i ^ bit) for i in range(self.chips)])  26.4 us
    ppermute x19, waiting for transfers between devices, swap(): return lax.ppermute(value, axis, [(0, 1), (1, 0)])  26 us
    unnamed x177, local copies, waits for them, and re-layouts  24.2 us
    pallas_call x1, Pallas kernels, cross_forward(): pl.pallas_call(functools.partial(cross_forward_kernel, cross_tile(count))...  23.5 us
    all_to_all x1, waiting for transfers between devices, per_device(): incoming = lax.all_to_all(outgoing, ALL, 0, 0, tiled=True)  22.9 us
  transfers between devices with their start and end apart: 43, of which 12 were waited for; matrix products, arithmetic and copies ran while one was open for 41% of the time, Pallas kernels for 18%

profile of v4, /device:TPU:0, one launch (start us, length us, event | category | flops | bytes accessed | tf_op | source)
XLA Modules:
  0.0 586.4 jit_solution(12616446174724636640)
XLA Ops:
  59.9 6.4 %all-to-all-start = ((bf16[16,192,256]{2,1,0:T(8,128)(2,1)}), bf16[16,192,256]{2,1,0:T(8,128)(2,1)S(1)}, u32[]{:S(2)}, u32[]{:S(2)}) async-start(bf16[16,192,256]{2,1,0:T(8,128)(2,1)} %bitcast.273), calls=%async_computation | async-start | bytes 3145728 | tf_op jit(solution)/shard_map/all_to_all | solution.py:925
  76.0 22.3 %all-to-all-done.own_ref.all_ref = bf16[16,192,256]{2,1,0:T(8,128)(2,1)S(1)} async-done(((bf16[16,192,256]{2,1,0:T(8,128)(2,1)}), bf16[16,192,256]{2,1,0:T(8,128)(2,1)S(1)}, u32[]{:S(2)}, u32[]{:S(2)}) %all-to-all-start) | async-done | bytes 1572896 | tf_op jit(solution)/shard_map/all_to_all | solution.py:925
  99.5 22.0 %self_forward.1 = (bf16[16,64,256]{2,1,0:T(8,128)(2,1)}, f32[64,4096]{1,0:T(8,128)}, f32[8,4096]{1,0:T(8,128)}) custom-call(s32[4,8]{1,0:T(4,128)} %get-tuple-element.80.plan, s32[32]{0:T(128)} %get-tuple-element.81.query_slot, s32[32]{0:T(128)} %get-tuple-element.82.key_slot, s32[2,4096]{1,0:T(2,128)} %get-tuple-element.83.range_ref, ...), custom_call_target="tpu_custom_call" | custom-call | flops 1 | bytes 1 | tf_op jit(solution)/shard_map/self_forward/pallas_call | solution.py:474
  139.6 12.3 %collective-permute-done.5 = bf16[256,1024]{1,0:T(8,128)(2,1)S(1)} collective-permute-done((bf16[256,1024]{1,0:T(8,128)(2,1)S(1)}, bf16[256,1024]{1,0:T(8,128)(2,1)S(1)}, u32[]{:S(2)}, u32[]{:S(2)}) %collective-permute-start.5) | collective-permute-done | bytes 524320 | tf_op jit(solution)/shard_map/ppermute | solution.py:677
  164.8 14.2 %fusion.6.key_ref.value_ref = bf16[2048,2048]{1,0:T(8,128)(2,1)} fusion(f32[2048]{0:T(1024)S(1)} %concatenate.103, bf16[1024,2048]{1,0:T(8,128)(2,1)} %slice_dynamic-update-slice_fusion.1, bf16[1,2048,1024]{2,1,0:T(8,128)(2,1)} %all-gather.6.cloned.1.call-done), kind=kOutput, calls=%fused_computation.11 | convolution fusion | flops 8598323200 | bytes 16785408 | tf_op jit(solution)/shard_map/dot_general | solution.py:940
  181.7 23.5 %cross_forward.1 = (bf16[1024,256]{1,0:T(8,128)(2,1)}, f32[1024,256]{1,0:T(8,128)}, f32[8,8,256]{2,1,0:T(8,128)}) custom-call(s32[4,1]{1,0:T(4,128)} %get-tuple-element.84.plan, s32[2,256]{1,0:T(2,128)} %get-tuple-element.86.range_ref, bf16[1024,256]{1,0:T(8,128)(2,1)} %fusion.20.query_ref, bf16[2048,2048]{1,0:T(8,128)(2,1)} %fusion.6.key_ref.value_ref, ...), custom_call_target="tpu_custom_call" | custom-call | flops 1 | bytes 1 | tf_op jit(solution)/shard_map/cross_forward/pallas_call | solution.py:547
  209.9 16.4 %collective-permute-done.9 = bf16[2048,1024]{1,0:T(8,128)(2,1)} collective-permute-done((bf16[2048,1024]{1,0:T(8,128)(2,1)}, bf16[2048,1024]{1,0:T(8,128)(2,1)}, u32[]{:S(2)}, u32[]{:S(2)}) %collective-permute-start.9) | collective-permute-done | bytes 4194336 | tf_op jit(solution)/shard_map/ppermute | solution.py:674
  238.8 6.0 %all-to-all-start.2 = ((bf16[16,64,256]{2,1,0:T(8,128)(2,1)}), bf16[16,64,256]{2,1,0:T(8,128)(2,1)S(1)}, u32[]{:S(2)}, u32[]{:S(2)}) async-start(bf16[16,64,256]{2,1,0:T(8,128)(2,1)} %bitcast.284), calls=%async_computation.2 | async-start | bytes 1048576 | tf_op jit(solution)/shard_map/all_to_all | solution.py:982
  244.9 7.1 %fusion.79 = f32[1024,2048]{1,0:T(8,128)S(1)} fusion(bf16[1024,1024]{1,0:T(8,128)(2,1)} %pad_maximum_fusion.7, bf16[1024,2048]{1,0:T(8,128)(2,1)} %slice_dynamic-update-slice_fusion.2), kind=kOutput, calls=%fused_computation.298 | convolution fusion | flops 4294967296 | bytes 14680064 | tf_op jit(solution)/shard_map/dot_general | solution.py:980
  252.0 15.2 %convert_reduce_fusion = (f32[2048]{0:T(1024)S(1)}, bf16[1024,2048]{1,0:T(8,128)(2,1)}, bf16[1024,2048]{1,0:T(8,128)(2,1)}) fusion(f32[1024,2048]{1,0:T(8,128)S(1)} %fusion.79, f32[2048]{0:T(1024)S(1)} %pad_maximum_fusion.12, bf16[1024,1024]{1,0:T(8,128)(2,1)} %constant_dynamic-update-slice_fusion.10, bf16[2048,1024]{1,0:T(8,128)(2,1)S(1)} %copy-done.30), kind=kOutput, calls=%fused_computation.12 | convolution fusion | flops 4355782656 | bytes 23085056 | tf_op jit(solution)/shard_map/dot_general | solution.py:50
  267.1 8.2 %convolution_convert_fusion.6 = bf16[1024,1024]{1,0:T(8,128)(2,1)S(1)} fusion(bf16[1024,2048]{1,0:T(8,128)(2,1)} %get-tuple-element.104, bf16[1024,2048]{1,0:T(8,128)(2,1)} %slice_dynamic-update-slice_fusion.2), kind=kOutput, calls=%fused_computation.50 | convolution fusion | flops 4296015872 | bytes 10485760 | tf_op jit(solution)/shard_map/dot_general | solution.py:50
  285.1 6.4 %convolution_convert_fusion.1 = bf16[2048,1024]{1,0:T(8,128)(2,1)S(1)} fusion(bf16[1024,2048]{1,0:T(8,128)(2,1)S(1)} %copy-done.70, bf16[1024,1024]{1,0:T(8,128)(2,1)} %constant_dynamic-update-slice_fusion.10), kind=kOutput, calls=%fused_computation.24 | convolution fusion | flops 4297064448 | bytes 10485760 | tf_op jit(solution)/shard_map/dot_general | solution.py:50
  303.3 6.2 %all-to-all-start.3 = ((bf16[16,80,256]{2,1,0:T(8,128)(2,1)}), bf16[16,80,256]{2,1,0:T(8,128)(2,1)}, u32[]{:S(2)}, u32[]{:S(2)}) async-start(bf16[16,80,256]{2,1,0:T(8,128)(2,1)} %fusion.32), calls=%async_computation.3 | async-start | bytes 1310720 | tf_op jit(solution)/shard_map/all_to_all | solution.py:1011
  309.5 7.4 %convolution_convert_fusion = bf16[1024,2048]{1,0:T(8,128)(2,1)S(1)} fusion(bf16[1024,1024]{1,0:T(8,128)(2,1)} %pad_maximum_fusion.7, bf16[1024,2048]{1,0:T(8,128)(2,1)} %get-tuple-element.104), kind=kOutput, calls=%fused_computation.23 | convolution fusion | flops 4297064448 | bytes 10485760 | tf_op jit(solution)/shard_map/dot_general | solution.py:50
  321.1 9.2 %convolution_convert_fusion.5 = bf16[1024,1024]{1,0:T(8,128)(2,1)} fusion(bf16[1024,2048]{1,0:T(8,128)(2,1)} %get-tuple-element.107, bf16[2048,1024]{1,0:T(8,128)(2,1)} %copy-done.29), kind=kOutput, calls=%fused_computation.49 | convolution fusion | flops 4296015872 | bytes 10485760 | tf_op jit(solution)/shard_map/dot_general | solution.py:1013
  330.3 19.3 %cross_backward.1 = (bf16[16,64,256]{2,1,0:T(8,128)(2,1)}, bf16[2048,128]{1,0:T(8,128)(2,1)}, bf16[16,64,256]{2,1,0:T(8,128)(2,1)}) custom-call(s32[4,8]{1,0:T(4,128)} %get-tuple-element.85.plan, s32[32]{0:T(128)} %get-tuple-element.81.query_slot, s32[2,4096]{1,0:T(2,128)} %get-tuple-element.87.range_ref, bf16[16,64,256]{2,1,0:T(8,128)(2,1)} %copy-done.39, ...), custom_call_target="tpu_custom_call" | custom-call | flops 1 | bytes 1 | tf_op jit(solution)/shard_map/cross_backward/pallas_call | solution.py:577
  349.7 6.3 %all-to-all-start.4 = ((bf16[16,64,256]{2,1,0:T(8,128)(2,1)}), bf16[16,64,256]{2,1,0:T(8,128)(2,1)}, u32[]{:S(2)}, u32[]{:S(2)}) async-start(bf16[16,64,256]{2,1,0:T(8,128)(2,1)} %get-tuple-element.114), calls=%async_computation.4 | async-start | bytes 1048576 | tf_op jit(solution)/shard_map/all_to_all | solution.py:1027
  363.2 7.3 %all-to-all-done.4 = bf16[16,64,256]{2,1,0:T(8,128)(2,1)} async-done(((bf16[16,64,256]{2,1,0:T(8,128)(2,1)}), bf16[16,64,256]{2,1,0:T(8,128)(2,1)}, u32[]{:S(2)}, u32[]{:S(2)}) %all-to-all-start.4) | async-done | bytes 524320 | tf_op jit(solution)/shard_map/all_to_all | solution.py:1027
  408.7 28.2 %self_backward.1 = (bf16[16,256,256]{2,1,0:T(8,128)(2,1)}, bf16[192,4096]{1,0:T(8,128)(2,1)}) custom-call(s32[4,8]{1,0:T(4,128)} %get-tuple-element.80.plan, s32[32]{0:T(128)} %get-tuple-element.81.query_slot, s32[32]{0:T(128)} %get-tuple-element.82.key_slot, s32[2,4096]{1,0:T(2,128)} %get-tuple-element.83.range_ref, bf16[16,192,256]{2,1,0:T(8,128)(2,1)} %copy-done, ...), custom_call_target="tpu_custom_call" | custom-call | flops 1 | bytes 1 | tf_op jit(solution)/shard_map/self_backward/pallas_call | solution.py:509
  471.5 7.4 %collective-permute-done.24 = bf16[2,2,3,32,1024]{4,3,2,0,1:T(8,128)(2,1)} collective-permute-done((bf16[2,2,3,32,1024]{4,3,2,0,1:T(8,128)(2,1)}, bf16[2,2,3,32,1024]{4,3,2,0,1:T(8,128)(2,1)}, u32[]{:S(2)}, u32[]{:S(2)}) %collective-permute-start.24) | collective-permute-done | bytes 786464 | tf_op jit(solution)/shard_map/ppermute | solution.py:677
  481.1 9.5 %collective-permute-start.25 = (bf16[2,3,32,1024]{3,2,1,0:T(8,128)(2,1)}, bf16[2,3,32,1024]{3,2,1,0:T(8,128)(2,1)}, u32[]{:S(2)}, u32[]{:S(2)}) collective-permute-start(bf16[2,3,32,1024]{3,2,1,0:T(8,128)(2,1)} %get-tuple-element.247), channel_id=1, source_target_pairs={{0,8},{4,12},{8,0},{12,4},{16,24},{20,28},{24,16},{28,20},{1,9},{5... | collective-permute-start | bytes 1179656 | tf_op jit(solution)/shard_map/ppermute | solution.py:677
  490.6 11.8 %all-to-all-done.6 = bf16[16,256,256]{2,1,0:T(8,128)(2,1)} async-done(((bf16[16,256,256]{2,1,0:T(8,128)(2,1)}), bf16[16,256,256]{2,1,0:T(8,128)(2,1)}, u32[]{:S(2)}, u32[]{:S(2)}) %all-to-all-start.6) | async-done | bytes 2097184 | tf_op jit(solution)/shard_map/all_to_all | solution.py:1063
  513.8 6.7 %all-to-all-start.7 = ((bf16[32,35,320]{2,1,0:T(8,128)(2,1)}), bf16[32,35,320]{2,1,0:T(8,128)(2,1)}, u32[]{:S(2)}, u32[]{:S(2)}) async-start(bf16[32,35,320]{2,1,0:T(8,128)(2,1)} %pad_maximum_fusion.8), calls=%async_computation.7 | async-start | bytes 1966080 | tf_op jit(solution)/shard_map/all_to_all | solution.py:1125
  538.3 22.9 %all-to-all-done.7 = bf16[32,35,320]{2,1,0:T(8,128)(2,1)} async-done(((bf16[32,35,320]{2,1,0:T(8,128)(2,1)}), bf16[32,35,320]{2,1,0:T(8,128)(2,1)}, u32[]{:S(2)}, u32[]{:S(2)}) %all-to-all-start.7) | async-done | bytes 716832 | tf_op jit(solution)/shard_map/all_to_all | solution.py:1125
  (446 shorter events, 268.2 us)
Async XLA Ops:
  7.2 157.6 %all-gather.6.cloned.1.call-start = ((), (), s32[]{:S(2)}) async-start(), calls=%async_computation.9 | async-start | bytes 4456448 | tf_op jit(solution)/shard_map/all_gather | solution.py:916
  10.1 37.8 %collective-permute-start = (bf16[256,3072]{1,0:T(8,128)(2,1)}, bf16[256,3072]{1,0:T(8,128)(2,1)}, u32[]{:S(2)}, u32[]{:S(2)}) collective-permute-start(bf16[256,3072]{1,0:T(8,128)(2,1)} %constant_dynamic-slice_fusion.11), channel_id=1, source_target_pairs={{0,1},{1,0},{2,3},{3,2},{4,5},{5,4},{6,7},{7,6},{8,9},{9,8},{10,11... | collective-permute-start | bytes 4718600 | tf_op jit(solution)/shard_map/ppermute | solution.py:674
  14.1 34.2 %collective-permute-start.2 = (bf16[15,512]{1,0:T(8,128)(2,1)S(1)}, bf16[15,512]{1,0:T(8,128)(2,1)S(1)}, u32[]{:S(2)}, u32[]{:S(2)}) collective-permute-start(bf16[15,512]{1,0:T(8,128)(2,1)S(1)} %concatenate.96), channel_id=1, source_target_pairs={{0,1},{1,0},{2,3},{3,2},{4,5},{5,4},{6,7},{7,6},{8,9},{9,8},{10,11... | collective-permute-start | bytes 46088 | tf_op jit(solution)/shard_map/ppermute | solution.py:674
  59.9 38.4 %all-to-all-start = ((bf16[16,192,256]{2,1,0:T(8,128)(2,1)}), bf16[16,192,256]{2,1,0:T(8,128)(2,1)S(1)}, u32[]{:S(2)}, u32[]{:S(2)}) async-start(bf16[16,192,256]{2,1,0:T(8,128)(2,1)} %bitcast.273), calls=%async_computation | async-start | bytes 3145728 | tf_op jit(solution)/shard_map/all_to_all | solution.py:925
  66.3 59.6 %collective-permute-start.3 = (bf16[256,5120]{1,0:T(8,128)(2,1)}, bf16[256,5120]{1,0:T(8,128)(2,1)}, u32[]{:S(2)}, u32[]{:S(2)}) collective-permute-start(bf16[256,5120]{1,0:T(8,128)(2,1)} %pad_maximum_fusion.6), channel_id=1, source_target_pairs={{0,1},{1,0},{2,3},{3,2},{4,5},{5,4},{6,7},{7,6},{8,9},{9,8},{10,11... | collective-permute-start | bytes 7864328 | tf_op jit(solution)/shard_map/ppermute | solution.py:674
  125.9 31.3 %collective-permute-start.4 = (bf16[256,5120]{1,0:T(8,128)(2,1)}, bf16[256,5120]{1,0:T(8,128)(2,1)}, u32[]{:S(2)}, u32[]{:S(2)}) collective-permute-start(bf16[256,5120]{1,0:T(8,128)(2,1)} %collective-permute-done.3), channel_id=1, source_target_pairs={{0,2},{2,0},{1,3},{3,1},{4,6},{6,4},{5,7},{7,5},{8,10},{10,8},{9,1... | collective-permute-start | bytes 7864328 | tf_op jit(solution)/shard_map/ppermute | solution.py:674
  131.9 198.4 %all-gather.4.cloned.1.call-start = ((), (), s32[]{:S(2)}) async-start(), calls=%async_computation.8 | async-start | bytes 8912896 | tf_op jit(solution)/shard_map/all_gather | solution.py:947
  133.1 93.2 %collective-permute-start.9 = (bf16[2048,1024]{1,0:T(8,128)(2,1)}, bf16[2048,1024]{1,0:T(8,128)(2,1)}, u32[]{:S(2)}, u32[]{:S(2)}) collective-permute-start(bf16[2048,1024]{1,0:T(8,128)(2,1)} %get-tuple-element.98), channel_id=1, source_target_pairs={{0,1},{1,0},{2,3},{3,2},{4,5},{5,4},{6,7},{7,6},{8,9},{9,8},{10,11... | collective-permute-start | bytes 12582920 | tf_op jit(solution)/shard_map/ppermute | solution.py:674
  294.0 55.7 %collective-permute-start.14 = (bf16[2,2,256,1024]{3,2,1,0:T(8,128)(2,1)}, bf16[2,2,256,1024]{3,2,1,0:T(8,128)(2,1)}, u32[]{:S(2)}, u32[]{:S(2)}) collective-permute-start(bf16[2,2,256,1024]{3,2,1,0:T(8,128)(2,1)} %get-tuple-element.215), channel_id=1, source_target_pairs={{0,1},{1,0},{2,3},{3,2},{4,5},{5,4},{6,7},{7,6},{8,9},{9,8},{10,11... | collective-permute-start | bytes 6291464 | tf_op jit(solution)/shard_map/ppermute | solution.py:674
  319.5 81.9 %collective-permute-start.15 = (bf16[2,2,4,32,2048]{4,3,2,1,0:T(8,128)(2,1)}, bf16[2,2,4,32,2048]{4,3,2,1,0:T(8,128)(2,1)}, u32[]{:S(2)}, u32[]{:S(2)}) collective-permute-start(bf16[2,2,4,32,2048]{4,3,2,1,0:T(8,128)(2,1)} %get-tuple-element.217), channel_id=1, source_target_pairs={{0,1},{1,0},{2,3},{3,2},{4,5},{5,4},{6,7},{7,6},{8,9},{9,8},{10,11... | collective-permute-start | bytes 6291464 | tf_op jit(solution)/shard_map/ppermute | solution.py:674
  359.0 107.3 %collective-permute-start.21 = (bf16[256,1024]{1,0:T(8,128)(2,1)}, bf16[256,1024]{1,0:T(8,128)(2,1)}, u32[]{:S(2)}, u32[]{:S(2)}) collective-permute-start(bf16[256,1024]{1,0:T(8,128)(2,1)} %get-tuple-element.237), channel_id=1, source_target_pairs={{0,2},{2,0},{1,3},{3,1},{4,6},{6,4},{5,7},{7,5},{8,10},{10,8},{9,1... | collective-permute-start | bytes 1572872 | tf_op jit(solution)/shard_map/ppermute | solution.py:674
  391.6 77.1 %collective-permute-start.22 = (bf16[256,1024]{1,0:T(8,128)(2,1)}, bf16[256,1024]{1,0:T(8,128)(2,1)}, u32[]{:S(2)}, u32[]{:S(2)}) collective-permute-start(bf16[256,1024]{1,0:T(8,128)(2,1)} %get-tuple-element.236), channel_id=1, source_target_pairs={{0,4},{4,0},{8,12},{12,8},{16,20},{20,16},{24,28},{28,24},{1,5},{5... | collective-permute-start | bytes 1572872 | tf_op jit(solution)/shard_map/ppermute | solution.py:677
  395.6 73.1 %collective-permute-start.23 = (bf16[256,1024]{1,0:T(8,128)(2,1)}, bf16[256,1024]{1,0:T(8,128)(2,1)}, u32[]{:S(2)}, u32[]{:S(2)}) collective-permute-start(bf16[256,1024]{1,0:T(8,128)(2,1)} %get-tuple-element.235), channel_id=1, source_target_pairs={{0,6},{2,4},{4,2},{6,0},{8,14},{10,12},{12,10},{14,8},{16,22},{18,... | collective-permute-start | bytes 1572872 | tf_op jit(solution)/shard_map/ppermute | solution.py:765
  401.4 38.1 %collective-permute-start.20 = (bf16[8,3,32,1024]{3,2,0,1:T(8,128)(2,1)}, bf16[8,3,32,1024]{3,2,0,1:T(8,128)(2,1)}, u32[]{:S(2)}, u32[]{:S(2)}) collective-permute-start(bf16[8,3,32,1024]{3,2,0,1:T(8,128)(2,1)} %get-tuple-element.221), channel_id=1, source_target_pairs={{0,1},{1,0},{2,3},{3,2},{4,5},{5,4},{6,7},{7,6},{8,9},{9,8},{10,11... | collective-permute-start | bytes 4718600 | tf_op jit(solution)/shard_map/ppermute | solution.py:674
  405.4 33.7 %collective-permute-start.19 = (bf16[2,4,32,2048]{3,2,1,0:T(8,128)(2,1)}, bf16[2,4,32,2048]{3,2,1,0:T(8,128)(2,1)}, u32[]{:S(2)}, u32[]{:S(2)}) collective-permute-start(bf16[2,4,32,2048]{3,2,1,0:T(8,128)(2,1)} %get-tuple-element.233), channel_id=1, source_target_pairs={{0,8},{4,12},{8,0},{12,4},{16,24},{20,28},{24,16},{28,20},{1,9},{5... | collective-permute-start | bytes 3145736 | tf_op jit(solution)/shard_map/ppermute | solution.py:677
  439.0 81.4 %collective-permute-start.31 = (bf16[2,256,1024]{2,1,0:T(8,128)(2,1)}, bf16[2,256,1024]{2,1,0:T(8,128)(2,1)}, u32[]{:S(2)}, u32[]{:S(2)}) collective-permute-start(bf16[2,256,1024]{2,1,0:T(8,128)(2,1)} %get-tuple-element.229), channel_id=1, source_target_pairs={{0,8},{4,12},{8,0},{12,4},{16,24},{20,28},{24,16},{28,20},{1,9},{5... | collective-permute-start | bytes 3145736 | tf_op jit(solution)/shard_map/ppermute | solution.py:677
  439.5 63.0 %all-to-all-start.6 = ((bf16[16,256,256]{2,1,0:T(8,128)(2,1)}), bf16[16,256,256]{2,1,0:T(8,128)(2,1)}, u32[]{:S(2)}, u32[]{:S(2)}) async-start(bf16[16,256,256]{2,1,0:T(8,128)(2,1)} %get-tuple-element.128), calls=%async_computation.6 | async-start | bytes 4194304 | tf_op jit(solution)/shard_map/all_to_all | solution.py:1063
  466.3 60.2 %collective-permute-start.27 = (bf16[4,32,2048]{2,1,0:T(8,128)(2,1)}, bf16[4,32,2048]{2,1,0:T(8,128)(2,1)}, u32[]{:S(2)}, u32[]{:S(2)}) collective-permute-start(bf16[4,32,2048]{2,1,0:T(8,128)(2,1)} %get-tuple-element.245), channel_id=1, source_target_pairs={{0,16},{4,20},{8,24},{12,28},{16,0},{20,4},{24,8},{28,12},{1,17},{... | collective-permute-start | bytes 1572872 | tf_op jit(solution)/shard_map/ppermute | solution.py:677
  481.1 49.5 %collective-permute-start.25 = (bf16[2,3,32,1024]{3,2,1,0:T(8,128)(2,1)}, bf16[2,3,32,1024]{3,2,1,0:T(8,128)(2,1)}, u32[]{:S(2)}, u32[]{:S(2)}) collective-permute-start(bf16[2,3,32,1024]{3,2,1,0:T(8,128)(2,1)} %get-tuple-element.247), channel_id=1, source_target_pairs={{0,8},{4,12},{8,0},{12,4},{16,24},{20,28},{24,16},{28,20},{1,9},{5... | collective-permute-start | bytes 1179656 | tf_op jit(solution)/shard_map/ppermute | solution.py:677
  513.8 47.4 %all-to-all-start.7 = ((bf16[32,35,320]{2,1,0:T(8,128)(2,1)}), bf16[32,35,320]{2,1,0:T(8,128)(2,1)}, u32[]{:S(2)}, u32[]{:S(2)}) async-start(bf16[32,35,320]{2,1,0:T(8,128)(2,1)} %pad_maximum_fusion.8), calls=%async_computation.7 | async-start | bytes 1966080 | tf_op jit(solution)/shard_map/all_to_all | solution.py:1125
  522.3 54.6 %collective-permute-start.32 = (bf16[256,1024]{1,0:T(8,128)(2,1)S(1)}, bf16[256,1024]{1,0:T(8,128)(2,1)}, u32[]{:S(2)}, u32[]{:S(2)}) collective-permute-start(bf16[256,1024]{1,0:T(8,128)(2,1)S(1)} %get-tuple-element.243), channel_id=1, source_target_pairs={{0,16},{4,20},{8,24},{12,28},{16,0},{20,4},{24,8},{28,12},{1,17},{... | collective-permute-start | bytes 1572872 | tf_op jit(solution)/shard_map/ppermute | solution.py:677
  529.9 31.3 %collective-permute-start.30 = (bf16[32,2048]{1,0:T(8,128)(2,1)}, bf16[32,2048]{1,0:T(8,128)(2,1)}, u32[]{:S(2)}, u32[]{:S(2)}) collective-permute-start(bf16[32,2048]{1,0:T(8,128)(2,1)} %get-tuple-element.252), channel_id=1, source_target_pairs={{0,6},{2,4},{4,2},{6,0},{8,14},{10,12},{12,10},{14,8},{16,22},{18,... | collective-permute-start | bytes 393224 | tf_op jit(solution)/shard_map/ppermute | solution.py:843
  529.9 32.3 %collective-permute-start.28 = (bf16[32,2048]{1,0:T(8,128)(2,1)}, bf16[32,2048]{1,0:T(8,128)(2,1)}, u32[]{:S(2)}, u32[]{:S(2)}) collective-permute-start(bf16[32,2048]{1,0:T(8,128)(2,1)} %get-tuple-element.254), channel_id=1, source_target_pairs={{0,2},{2,0},{1,3},{3,1},{4,6},{6,4},{5,7},{7,5},{8,10},{10,8},{9,1... | collective-permute-start | bytes 393224 | tf_op jit(solution)/shard_map/ppermute | solution.py:674
  531.8 44.3 %collective-permute-start.26 = (bf16[3,32,1024]{2,1,0:T(8,128)(2,1)S(1)}, bf16[3,32,1024]{2,1,0:T(8,128)(2,1)S(1)}, u32[]{:S(2)}, u32[]{:S(2)}) collective-permute-start(bf16[3,32,1024]{2,1,0:T(8,128)(2,1)S(1)} %get-tuple-element.262), channel_id=1, source_target_pairs={{0,16},{4,20},{8,24},{12,28},{16,0},{20,4},{24,8},{28,12},{1,17},{... | collective-permute-start | bytes 589832 | tf_op jit(solution)/shard_map/ppermute | solution.py:677
  (90 other events, 1010.4 us)
Sparse Core Ops, SparseCore 0:
  14.4 52.2 all-gather.5
  155.6 77.7 all-gather.3

commit v5 on v4

--- a/solution.py
+++ b/solution.py
@@ -1080,7 +1080,9 @@
     if move.cube:
         square = move.add(square, head_w).astype(low)
         sent_a, square = move.send_half(square, 1, move.near, lambda v: move.swap_chip(v, 2))
-        flown = (sent_a,)
+        lower = move.add(lower, head_c).astype(low)
+        sent_b, lower = move.send_half(lower, 0, move.far, lambda v: move.swap_chip(v, 4))
+        flown = (sent_a, sent_b)
     grad_qkv = grad_qkv.reshape(H, 3, depth, rows).transpose(1, 0, 2, 3).reshape(3 * width, rows)
     grad_ln_one, gain_one, shift_one = back_one(contract(after(grad_qkv, *flown), w_qkv, 0, 1))
     grad_input = grad_one + grad_ln_one
@@ -1125,8 +1127,6 @@
     incoming = lax.all_to_all(outgoing, ALL, 0, 0, tiled=True)
     result = mixed_two + move.quad_total(branch_sum, soon) + bias_down
     if move.cube:
-        lower = move.add(lower, outgoing).astype(low)
-        _, lower = move.send_half(lower, 0, move.far, lambda v: move.swap_chip(v, 4))
         lower_own = move.add(lower, incoming)
         upper_own = move.corner_columns(move.add(upper, grad_ln_one).astype(low), (incoming,))
         square = move.add(square, outgoing).astype(low)

time: 596 us -> 587 us (0.985)
  waiting for transfers between devices: 117 us -> 134 us
  Pallas kernels: 103 us -> 86.7 us
    ppermute x12, waiting for transfers between devices: 26.4 us -> 40.7 us  [swap_chip(): return lax.ppermute(value, CHIP, [(i, i ^ bit) for i in range(self.chips)])]
    pallas_call x1, Pallas kernels: 23.5 us -> 13.7 us  [cross_forward(): pl.pallas_call(functools.partial(cross_forward_kernel, cross_tile(count))...]
    ppermute x19, waiting for transfers between devices: 26 us -> 33.6 us  [swap(): return lax.ppermute(value, axis, [(0, 1), (1, 0)])]
    unnamed x177 -> x165, local copies, waits for them, and re-layouts: 24.2 us -> 22.1 us
  transfers between devices with their start and end apart: 43 -> 43, of which waited for: 12 -> 13; matrix products, arithmetic and copies ran while one was open for 41% -> 41% of each run, Pallas kernels for 18% -> 15%
where the time goes in v5:
time: 587 us; the launch traced here: 576 us
  waiting for transfers between devices  134 us (23%)
  matrix products  104 us (18%)
  local copies, waits for them, and re-layouts  95.6 us (16%)
  Pallas kernels  86.7 us (15%)
  starting transfers between devices  85.5 us (15%)
  other arithmetic  54.3 us (9%)
  between operations  15.7 us (3%)
    dot_general x18, matrix products, contract(): lax.dot_general(left, right, (((left_dim,), (right_dim,)), ((), ())), pre...  73 us
    ppermute x12, waiting for transfers between devices, swap_chip(): return lax.ppermute(value, CHIP, [(i, i ^ bit) for i in range(self.chips)])  40.7 us
    ppermute x19, waiting for transfers between devices, swap(): return lax.ppermute(value, axis, [(0, 1), (1, 0)])  33.6 us
    pallas_call x1, Pallas kernels, self_backward(): pl.pallas_call(functools.partial(self_backward_kernel, tile, joined), out...  28 us
    ppermute x12, starting transfers between devices, swap_chip(): return lax.ppermute(value, CHIP, [(i, i ^ bit) for i in range(self.chips)])  26.7 us
    all_to_all x1, waiting for transfers between devices, per_device(): incoming = lax.all_to_all(outgoing, ALL, 0, 0, tiled=True)  25.2 us
    all_to_all x1, waiting for transfers between devices, per_device(): own_heads = lax.all_to_all(projected, HEADS, 0, 0, tiled=True)  22.2 us
    unnamed x165, local copies, waits for them, and re-layouts  22.1 us
  transfers between devices with their start and end apart: 43, of which 13 were waited for; matrix products, arithmetic and copies ran while one was open for 41% of the time, Pallas kernels for 15%

profile of v5, /device:TPU:0, one launch (start us, length us, event | category | flops | bytes accessed | tf_op | source)
XLA Modules:
  0.0 576.5 jit_solution(2997910988338422857)
XLA Ops:
  59.8 6.4 %all-to-all-start = ((bf16[16,192,256]{2,1,0:T(8,128)(2,1)}), bf16[16,192,256]{2,1,0:T(8,128)(2,1)S(1)}, u32[]{:S(2)}, u32[]{:S(2)}) async-start(bf16[16,192,256]{2,1,0:T(8,128)(2,1)} %bitcast.273), calls=%async_computation | async-start | bytes 3145728 | tf_op jit(solution)/shard_map/all_to_all | solution.py:925
  76.0 22.2 %all-to-all-done.own_ref.all_ref = bf16[16,192,256]{2,1,0:T(8,128)(2,1)S(1)} async-done(((bf16[16,192,256]{2,1,0:T(8,128)(2,1)}), bf16[16,192,256]{2,1,0:T(8,128)(2,1)S(1)}, u32[]{:S(2)}, u32[]{:S(2)}) %all-to-all-start) | async-done | bytes 1572896 | tf_op jit(solution)/shard_map/all_to_all | solution.py:925
  99.4 22.0 %self_forward.1 = (bf16[16,64,256]{2,1,0:T(8,128)(2,1)}, f32[64,4096]{1,0:T(8,128)}, f32[8,4096]{1,0:T(8,128)}) custom-call(s32[4,8]{1,0:T(4,128)} %get-tuple-element.80.plan, s32[32]{0:T(128)} %get-tuple-element.81.query_slot, s32[32]{0:T(128)} %get-tuple-element.82.key_slot, s32[2,4096]{1,0:T(2,128)} %get-tuple-element.83.range_ref, ...), custom_call_target="tpu_custom_call" | custom-call | flops 1 | bytes 1 | tf_op jit(solution)/shard_map/self_forward/pallas_call | solution.py:474
  125.9 5.8 %all-to-all-start.1 = ((bf16[16,64,256]{2,1,0:T(8,128)(2,1)}), bf16[16,64,256]{2,1,0:T(8,128)(2,1)S(1)}, u32[]{:S(2)}, u32[]{:S(2)}) async-start(bf16[16,64,256]{2,1,0:T(8,128)(2,1)} %get-tuple-element.92), calls=%async_computation.1 | async-start | bytes 1048576 | tf_op jit(solution)/shard_map/all_to_all | solution.py:932
  139.7 12.1 %collective-permute-done.5 = bf16[256,1024]{1,0:T(8,128)(2,1)S(1)} collective-permute-done((bf16[256,1024]{1,0:T(8,128)(2,1)S(1)}, bf16[256,1024]{1,0:T(8,128)(2,1)S(1)}, u32[]{:S(2)}, u32[]{:S(2)}) %collective-permute-start.5) | collective-permute-done | bytes 524320 | tf_op jit(solution)/shard_map/ppermute | solution.py:677
  164.8 14.3 %fusion.6.key_ref.value_ref = bf16[2048,2048]{1,0:T(8,128)(2,1)} fusion(f32[2048]{0:T(1024)S(1)} %concatenate.103, bf16[1024,2048]{1,0:T(8,128)(2,1)} %slice_dynamic-update-slice_fusion.1, bf16[1,2048,1024]{2,1,0:T(8,128)(2,1)} %all-gather.6.cloned.1.call-done), kind=kOutput, calls=%fused_computation.11 | convolution fusion | flops 8598323200 | bytes 16785408 | tf_op jit(solution)/shard_map/dot_general | solution.py:940
  181.7 13.7 %cross_forward.1 = (bf16[1024,256]{1,0:T(8,128)(2,1)}, f32[1024,256]{1,0:T(8,128)}, f32[8,8,256]{2,1,0:T(8,128)}) custom-call(s32[4,1]{1,0:T(4,128)} %get-tuple-element.84.plan, s32[2,256]{1,0:T(2,128)} %get-tuple-element.86.range_ref, bf16[1024,256]{1,0:T(8,128)(2,1)} %fusion.20.query_ref, bf16[2048,2048]{1,0:T(8,128)(2,1)} %fusion.6.key_ref.value_ref, ...), custom_call_target="tpu_custom_call" | custom-call | flops 1 | bytes 1 | tf_op jit(solution)/shard_map/cross_forward/pallas_call | solution.py:547
  197.8 12.1 %collective-permute-start.7 = (bf16[256,1024]{1,0:T(8,128)(2,1)S(1)}, bf16[256,1024]{1,0:T(8,128)(2,1)S(1)}, u32[]{:S(2)}, u32[]{:S(2)}) collective-permute-start(bf16[256,1024]{1,0:T(8,128)(2,1)S(1)} %add_convert_fusion.9), channel_id=1, source_target_pairs={{0,4},{4,0},{8,12},{12,8},{16,20},{20,16},{24,28},{28,24},{1,5},{5... | collective-permute-start | bytes 1572872 | tf_op jit(solution)/shard_map/ppermute | solution.py:677
  210.0 16.2 %collective-permute-done.9 = bf16[2048,1024]{1,0:T(8,128)(2,1)} collective-permute-done((bf16[2048,1024]{1,0:T(8,128)(2,1)}, bf16[2048,1024]{1,0:T(8,128)(2,1)}, u32[]{:S(2)}, u32[]{:S(2)}) %collective-permute-start.9) | collective-permute-done | bytes 4194336 | tf_op jit(solution)/shard_map/ppermute | solution.py:674
  238.7 6.2 %all-to-all-start.2 = ((bf16[16,64,256]{2,1,0:T(8,128)(2,1)}), bf16[16,64,256]{2,1,0:T(8,128)(2,1)S(1)}, u32[]{:S(2)}, u32[]{:S(2)}) async-start(bf16[16,64,256]{2,1,0:T(8,128)(2,1)} %bitcast.284), calls=%async_computation.2 | async-start | bytes 1048576 | tf_op jit(solution)/shard_map/all_to_all | solution.py:982
  245.0 7.1 %fusion.79 = f32[1024,2048]{1,0:T(8,128)S(1)} fusion(bf16[1024,1024]{1,0:T(8,128)(2,1)} %pad_maximum_fusion.7, bf16[1024,2048]{1,0:T(8,128)(2,1)} %slice_dynamic-update-slice_fusion.2), kind=kOutput, calls=%fused_computation.298 | convolution fusion | flops 4294967296 | bytes 14680064 | tf_op jit(solution)/shard_map/dot_general | solution.py:980
  252.1 15.2 %convert_reduce_fusion = (f32[2048]{0:T(1024)S(1)}, bf16[1024,2048]{1,0:T(8,128)(2,1)}, bf16[1024,2048]{1,0:T(8,128)(2,1)}) fusion(f32[1024,2048]{1,0:T(8,128)S(1)} %fusion.79, f32[2048]{0:T(1024)S(1)} %pad_maximum_fusion.12, bf16[1024,1024]{1,0:T(8,128)(2,1)} %constant_dynamic-update-slice_fusion.10, bf16[2048,1024]{1,0:T(8,128)(2,1)S(1)} %copy-done.26), kind=kOutput, calls=%fused_computation.12 | convolution fusion | flops 4355782656 | bytes 23085056 | tf_op jit(solution)/shard_map/dot_general | solution.py:50
  267.3 8.2 %convolution_convert_fusion.6 = bf16[1024,1024]{1,0:T(8,128)(2,1)S(1)} fusion(bf16[1024,2048]{1,0:T(8,128)(2,1)} %get-tuple-element.104, bf16[1024,2048]{1,0:T(8,128)(2,1)} %slice_dynamic-update-slice_fusion.2), kind=kOutput, calls=%fused_computation.50 | convolution fusion | flops 4296015872 | bytes 10485760 | tf_op jit(solution)/shard_map/dot_general | solution.py:50
  285.2 6.4 %convolution_convert_fusion.1 = bf16[2048,1024]{1,0:T(8,128)(2,1)S(1)} fusion(bf16[1024,2048]{1,0:T(8,128)(2,1)S(1)} %copy-done.64, bf16[1024,1024]{1,0:T(8,128)(2,1)} %constant_dynamic-update-slice_fusion.10), kind=kOutput, calls=%fused_computation.24 | convolution fusion | flops 4297064448 | bytes 10485760 | tf_op jit(solution)/shard_map/dot_general | solution.py:50
  303.4 6.0 %all-to-all-start.3 = ((bf16[16,80,256]{2,1,0:T(8,128)(2,1)}), bf16[16,80,256]{2,1,0:T(8,128)(2,1)}, u32[]{:S(2)}, u32[]{:S(2)}) async-start(bf16[16,80,256]{2,1,0:T(8,128)(2,1)} %fusion.32), calls=%async_computation.3 | async-start | bytes 1310720 | tf_op jit(solution)/shard_map/all_to_all | solution.py:1011
  309.4 7.4 %convolution_convert_fusion = bf16[1024,2048]{1,0:T(8,128)(2,1)S(1)} fusion(bf16[1024,1024]{1,0:T(8,128)(2,1)} %pad_maximum_fusion.7, bf16[1024,2048]{1,0:T(8,128)(2,1)} %get-tuple-element.104), kind=kOutput, calls=%fused_computation.23 | convolution fusion | flops 4297064448 | bytes 10485760 | tf_op jit(solution)/shard_map/dot_general | solution.py:50
  321.1 8.0 %convolution_convert_fusion.5 = bf16[1024,1024]{1,0:T(8,128)(2,1)S(1)} fusion(bf16[1024,2048]{1,0:T(8,128)(2,1)} %get-tuple-element.107, bf16[2048,1024]{1,0:T(8,128)(2,1)} %copy-done.25), kind=kOutput, calls=%fused_computation.49 | convolution fusion | flops 4296015872 | bytes 10485760 | tf_op jit(solution)/shard_map/dot_general | solution.py:1013
  332.4 13.4 %cross_backward.1 = (bf16[16,64,256]{2,1,0:T(8,128)(2,1)}, bf16[2048,128]{1,0:T(8,128)(2,1)}, bf16[16,64,256]{2,1,0:T(8,128)(2,1)}) custom-call(s32[4,8]{1,0:T(4,128)} %get-tuple-element.85.plan, s32[32]{0:T(128)} %get-tuple-element.81.query_slot, s32[2,4096]{1,0:T(2,128)} %get-tuple-element.87.range_ref, bf16[16,64,256]{2,1,0:T(8,128)(2,1)} %copy-done.34, ...), custom_call_target="tpu_custom_call" | custom-call | flops 1 | bytes 1 | tf_op jit(solution)/shard_map/cross_backward/pallas_call | solution.py:577
  379.1 7.7 %collective-permute-done.15 = bf16[2,2,4,32,2048]{4,3,2,1,0:T(8,128)(2,1)} collective-permute-done((bf16[2,2,4,32,2048]{4,3,2,1,0:T(8,128)(2,1)}, bf16[2,2,4,32,2048]{4,3,2,1,0:T(8,128)(2,1)}, u32[]{:S(2)}, u32[]{:S(2)}) %collective-permute-start.15) | collective-permute-done | bytes 2097184 | tf_op jit(solution)/shard_map/ppermute | solution.py:674
  400.8 28.0 %self_backward.1 = (bf16[16,256,256]{2,1,0:T(8,128)(2,1)}, bf16[192,4096]{1,0:T(8,128)(2,1)}) custom-call(s32[4,8]{1,0:T(4,128)} %get-tuple-element.80.plan, s32[32]{0:T(128)} %get-tuple-element.81.query_slot, s32[32]{0:T(128)} %get-tuple-element.82.key_slot, s32[2,4096]{1,0:T(2,128)} %get-tuple-element.83.range_ref, bf16[16,192,256]{2,1,0:T(8,128)(2,1)} %copy-done, ...), custom_call_target="tpu_custom_call" | custom-call | flops 1 | bytes 1 | tf_op jit(solution)/shard_map/self_backward/pallas_call | solution.py:509
  457.8 17.5 %collective-permute-done.25 = bf16[2,256,1024]{2,1,0:T(8,128)(2,1)} collective-permute-done((bf16[2,256,1024]{2,1,0:T(8,128)(2,1)}, bf16[2,256,1024]{2,1,0:T(8,128)(2,1)}, u32[]{:S(2)}, u32[]{:S(2)}) %collective-permute-start.25) | collective-permute-done | bytes 1048608 | tf_op jit(solution)/shard_map/ppermute | solution.py:677
  485.8 8.1 %all-to-all-done.6 = bf16[16,256,256]{2,1,0:T(8,128)(2,1)} async-done(((bf16[16,256,256]{2,1,0:T(8,128)(2,1)}), bf16[16,256,256]{2,1,0:T(8,128)(2,1)}, u32[]{:S(2)}, u32[]{:S(2)}) %all-to-all-start.6) | async-done | bytes 2097184 | tf_op jit(solution)/shard_map/all_to_all | solution.py:1063
  511.7 9.3 %collective-permute-done.28 = bf16[4,32,2048]{2,1,0:T(8,128)(2,1)} collective-permute-done((bf16[4,32,2048]{2,1,0:T(8,128)(2,1)}, bf16[4,32,2048]{2,1,0:T(8,128)(2,1)}, u32[]{:S(2)}, u32[]{:S(2)}) %collective-permute-start.28) | collective-permute-done | bytes 524320 | tf_op jit(solution)/shard_map/ppermute | solution.py:677
  532.2 25.2 %all-to-all-done.7 = bf16[32,35,320]{2,1,0:T(8,128)(2,1)} async-done(((bf16[32,35,320]{2,1,0:T(8,128)(2,1)}), bf16[32,35,320]{2,1,0:T(8,128)(2,1)}, u32[]{:S(2)}, u32[]{:S(2)}) %all-to-all-start.7) | async-done | bytes 716832 | tf_op jit(solution)/shard_map/all_to_all | solution.py:1127
  (434 shorter events, 262.3 us)
Async XLA Ops:
  7.2 157.6 %all-gather.6.cloned.1.call-start = ((), (), s32[]{:S(2)}) async-start(), calls=%async_computation.9 | async-start | bytes 4456448 | tf_op jit(solution)/shard_map/all_gather | solution.py:916
  10.1 37.8 %collective-permute-start = (bf16[256,3072]{1,0:T(8,128)(2,1)}, bf16[256,3072]{1,0:T(8,128)(2,1)}, u32[]{:S(2)}, u32[]{:S(2)}) collective-permute-start(bf16[256,3072]{1,0:T(8,128)(2,1)} %constant_dynamic-slice_fusion.11), channel_id=1, source_target_pairs={{0,1},{1,0},{2,3},{3,2},{4,5},{5,4},{6,7},{7,6},{8,9},{9,8},{10,11... | collective-permute-start | bytes 4718600 | tf_op jit(solution)/shard_map/ppermute | solution.py:674
  14.1 34.2 %collective-permute-start.2 = (bf16[15,512]{1,0:T(8,128)(2,1)S(1)}, bf16[15,512]{1,0:T(8,128)(2,1)S(1)}, u32[]{:S(2)}, u32[]{:S(2)}) collective-permute-start(bf16[15,512]{1,0:T(8,128)(2,1)S(1)} %concatenate.96), channel_id=1, source_target_pairs={{0,1},{1,0},{2,3},{3,2},{4,5},{5,4},{6,7},{7,6},{8,9},{9,8},{10,11... | collective-permute-start | bytes 46088 | tf_op jit(solution)/shard_map/ppermute | solution.py:674
  59.8 38.4 %all-to-all-start = ((bf16[16,192,256]{2,1,0:T(8,128)(2,1)}), bf16[16,192,256]{2,1,0:T(8,128)(2,1)S(1)}, u32[]{:S(2)}, u32[]{:S(2)}) async-start(bf16[16,192,256]{2,1,0:T(8,128)(2,1)} %bitcast.273), calls=%async_computation | async-start | bytes 3145728 | tf_op jit(solution)/shard_map/all_to_all | solution.py:925
  66.2 59.6 %collective-permute-start.3 = (bf16[256,5120]{1,0:T(8,128)(2,1)}, bf16[256,5120]{1,0:T(8,128)(2,1)}, u32[]{:S(2)}, u32[]{:S(2)}) collective-permute-start(bf16[256,5120]{1,0:T(8,128)(2,1)} %pad_maximum_fusion.6), channel_id=1, source_target_pairs={{0,1},{1,0},{2,3},{3,2},{4,5},{5,4},{6,7},{7,6},{8,9},{9,8},{10,11... | collective-permute-start | bytes 7864328 | tf_op jit(solution)/shard_map/ppermute | solution.py:674
  131.8 200.6 %all-gather.4.cloned.1.call-start = ((), (), s32[]{:S(2)}) async-start(), calls=%async_computation.8 | async-start | bytes 8912896 | tf_op jit(solution)/shard_map/all_gather | solution.py:947
  133.0 93.2 %collective-permute-start.9 = (bf16[2048,1024]{1,0:T(8,128)(2,1)}, bf16[2048,1024]{1,0:T(8,128)(2,1)}, u32[]{:S(2)}, u32[]{:S(2)}) collective-permute-start(bf16[2048,1024]{1,0:T(8,128)(2,1)} %get-tuple-element.98), channel_id=1, source_target_pairs={{0,1},{1,0},{2,3},{3,2},{4,5},{5,4},{6,7},{7,6},{8,9},{9,8},{10,11... | collective-permute-start | bytes 12582920 | tf_op jit(solution)/shard_map/ppermute | solution.py:674
  294.1 51.7 %collective-permute-start.14 = (bf16[2,2,256,1024]{3,2,1,0:T(8,128)(2,1)}, bf16[2,2,256,1024]{3,2,1,0:T(8,128)(2,1)}, u32[]{:S(2)}, u32[]{:S(2)}) collective-permute-start(bf16[2,2,256,1024]{3,2,1,0:T(8,128)(2,1)} %get-tuple-element.215), channel_id=1, source_target_pairs={{0,1},{1,0},{2,3},{3,2},{4,5},{5,4},{6,7},{7,6},{8,9},{9,8},{10,11... | collective-permute-start | bytes 6291464 | tf_op jit(solution)/shard_map/ppermute | solution.py:674
  319.4 67.4 %collective-permute-start.15 = (bf16[2,2,4,32,2048]{4,3,2,1,0:T(8,128)(2,1)}, bf16[2,2,4,32,2048]{4,3,2,1,0:T(8,128)(2,1)}, u32[]{:S(2)}, u32[]{:S(2)}) collective-permute-start(bf16[2,2,4,32,2048]{4,3,2,1,0:T(8,128)(2,1)} %get-tuple-element.217), channel_id=1, source_target_pairs={{0,1},{1,0},{2,3},{3,2},{4,5},{5,4},{6,7},{7,6},{8,9},{9,8},{10,11... | collective-permute-start | bytes 6291464 | tf_op jit(solution)/shard_map/ppermute | solution.py:674
  330.4 147.6 %collective-permute-start.21 = (bf16[256,1024]{1,0:T(8,128)(2,1)}, bf16[256,1024]{1,0:T(8,128)(2,1)}, u32[]{:S(2)}, u32[]{:S(2)}) collective-permute-start(bf16[256,1024]{1,0:T(8,128)(2,1)} %get-tuple-element.237), channel_id=1, source_target_pairs={{0,2},{2,0},{1,3},{3,1},{4,6},{6,4},{5,7},{7,5},{8,10},{10,8},{9,1... | collective-permute-start | bytes 1572872 | tf_op jit(solution)/shard_map/ppermute | solution.py:674
  330.6 150.3 %collective-permute-start.22 = (bf16[256,1024]{1,0:T(8,128)(2,1)}, bf16[256,1024]{1,0:T(8,128)(2,1)}, u32[]{:S(2)}, u32[]{:S(2)}) collective-permute-start(bf16[256,1024]{1,0:T(8,128)(2,1)} %get-tuple-element.236), channel_id=1, source_target_pairs={{0,4},{4,0},{8,12},{12,8},{16,20},{20,16},{24,28},{28,24},{1,5},{5... | collective-permute-start | bytes 1572872 | tf_op jit(solution)/shard_map/ppermute | solution.py:677
  355.1 34.0 %collective-permute-start.16 = (bf16[8,2,32,1024]{3,2,1,0:T(8,128)(2,1)}, bf16[8,2,32,1024]{3,2,1,0:T(8,128)(2,1)}, u32[]{:S(2)}, u32[]{:S(2)}) collective-permute-start(bf16[8,2,32,1024]{3,2,1,0:T(8,128)(2,1)} %dynamic-slice_bitcast_fusion.10), channel_id=1, source_target_pairs={{0,2},{2,0},{1,3},{3,1},{4,6},{6,4},{5,7},{7,5},{8,10},{10,8},{9,1... | collective-permute-start | bytes 3145736 | tf_op jit(solution)/shard_map/ppermute | solution.py:674
  389.2 91.8 %collective-permute-start.23 = (bf16[256,1024]{1,0:T(8,128)(2,1)}, bf16[256,1024]{1,0:T(8,128)(2,1)}, u32[]{:S(2)}, u32[]{:S(2)}) collective-permute-start(bf16[256,1024]{1,0:T(8,128)(2,1)} %get-tuple-element.235), channel_id=1, source_target_pairs={{0,6},{2,4},{4,2},{6,0},{8,14},{10,12},{12,10},{14,8},{16,22},{18,... | collective-permute-start | bytes 1572872 | tf_op jit(solution)/shard_map/ppermute | solution.py:765
  395.1 36.7 %collective-permute-start.20 = (bf16[8,3,32,1024]{3,2,0,1:T(8,128)(2,1)}, bf16[8,3,32,1024]{3,2,0,1:T(8,128)(2,1)}, u32[]{:S(2)}, u32[]{:S(2)}) collective-permute-start(bf16[8,3,32,1024]{3,2,0,1:T(8,128)(2,1)} %get-tuple-element.221), channel_id=1, source_target_pairs={{0,1},{1,0},{2,3},{3,2},{4,5},{5,4},{6,7},{7,6},{8,9},{9,8},{10,11... | collective-permute-start | bytes 4718600 | tf_op jit(solution)/shard_map/ppermute | solution.py:674
  431.2 44.2 %collective-permute-start.25 = (bf16[2,256,1024]{2,1,0:T(8,128)(2,1)}, bf16[2,256,1024]{2,1,0:T(8,128)(2,1)}, u32[]{:S(2)}, u32[]{:S(2)}) collective-permute-start(bf16[2,256,1024]{2,1,0:T(8,128)(2,1)} %get-tuple-element.231), channel_id=1, source_target_pairs={{0,8},{4,12},{8,0},{12,4},{16,24},{20,28},{24,16},{28,20},{1,9},{5... | collective-permute-start | bytes 3145736 | tf_op jit(solution)/shard_map/ppermute | solution.py:677
  431.8 62.1 %all-to-all-start.6 = ((bf16[16,256,256]{2,1,0:T(8,128)(2,1)}), bf16[16,256,256]{2,1,0:T(8,128)(2,1)}, u32[]{:S(2)}, u32[]{:S(2)}) async-start(bf16[16,256,256]{2,1,0:T(8,128)(2,1)} %get-tuple-element.128), calls=%async_computation.6 | async-start | bytes 4194304 | tf_op jit(solution)/shard_map/all_to_all | solution.py:1063
  445.4 38.1 %collective-permute-start.24 = (bf16[2,2,3,32,1024]{4,3,2,0,1:T(8,128)(2,1)}, bf16[2,2,3,32,1024]{4,3,2,0,1:T(8,128)(2,1)}, u32[]{:S(2)}, u32[]{:S(2)}) collective-permute-start(bf16[2,2,3,32,1024]{4,3,2,0,1:T(8,128)(2,1)} %bitcast.263), channel_id=1, source_target_pairs={{0,4},{4,0},{8,12},{12,8},{16,20},{20,16},{24,28},{28,24},{1,5},{5... | collective-permute-start | bytes 2359304 | tf_op jit(solution)/shard_map/ppermute | solution.py:677
  475.3 45.7 %collective-permute-start.28 = (bf16[4,32,2048]{2,1,0:T(8,128)(2,1)}, bf16[4,32,2048]{2,1,0:T(8,128)(2,1)}, u32[]{:S(2)}, u32[]{:S(2)}) collective-permute-start(bf16[4,32,2048]{2,1,0:T(8,128)(2,1)} %get-tuple-element.245), channel_id=1, source_target_pairs={{0,16},{4,20},{8,24},{12,28},{16,0},{20,4},{24,8},{28,12},{1,17},{... | collective-permute-start | bytes 1572872 | tf_op jit(solution)/shard_map/ppermute | solution.py:677
  478.0 89.2 %collective-permute-start.32 = (bf16[256,1024]{1,0:T(8,128)(2,1)}, bf16[256,1024]{1,0:T(8,128)(2,1)}, u32[]{:S(2)}, u32[]{:S(2)}) collective-permute-start(bf16[256,1024]{1,0:T(8,128)(2,1)} %get-tuple-element.243), channel_id=1, source_target_pairs={{0,16},{4,20},{8,24},{12,28},{16,0},{20,4},{24,8},{28,12},{1,17},{... | collective-permute-start | bytes 1572872 | tf_op jit(solution)/shard_map/ppermute | solution.py:677
  485.8 38.6 %collective-permute-start.26 = (bf16[2,3,32,1024]{3,2,1,0:T(8,128)(2,1)}, bf16[2,3,32,1024]{3,2,1,0:T(8,128)(2,1)}, u32[]{:S(2)}, u32[]{:S(2)}) collective-permute-start(bf16[2,3,32,1024]{3,2,1,0:T(8,128)(2,1)} %get-tuple-element.247), channel_id=1, source_target_pairs={{0,8},{4,12},{8,0},{12,4},{16,24},{20,28},{24,16},{28,20},{1,9},{5... | collective-permute-start | bytes 1179656 | tf_op jit(solution)/shard_map/ppermute | solution.py:677
  504.3 53.2 %all-to-all-start.7 = ((bf16[32,35,320]{2,1,0:T(8,128)(2,1)}), bf16[32,35,320]{2,1,0:T(8,128)(2,1)}, u32[]{:S(2)}, u32[]{:S(2)}) async-start(bf16[32,35,320]{2,1,0:T(8,128)(2,1)} %pad_maximum_fusion.8), calls=%async_computation.7 | async-start | bytes 1966080 | tf_op jit(solution)/shard_map/all_to_all | solution.py:1127
  523.7 33.7 %collective-permute-start.31 = (bf16[32,2048]{1,0:T(8,128)(2,1)S(1)}, bf16[32,2048]{1,0:T(8,128)(2,1)S(1)}, u32[]{:S(2)}, u32[]{:S(2)}) collective-permute-start(bf16[32,2048]{1,0:T(8,128)(2,1)S(1)} %get-tuple-element.252), channel_id=1, source_target_pairs={{0,6},{2,4},{4,2},{6,0},{8,14},{10,12},{12,10},{14,8},{16,22},{18,... | collective-permute-start | bytes 393224 | tf_op jit(solution)/shard_map/ppermute | solution.py:843
  523.7 34.8 %collective-permute-start.29 = (bf16[32,2048]{1,0:T(8,128)(2,1)S(1)}, bf16[32,2048]{1,0:T(8,128)(2,1)S(1)}, u32[]{:S(2)}, u32[]{:S(2)}) collective-permute-start(bf16[32,2048]{1,0:T(8,128)(2,1)S(1)} %get-tuple-element.254), channel_id=1, source_target_pairs={{0,2},{2,0},{1,3},{3,1},{4,6},{6,4},{5,7},{7,5},{8,10},{10,8},{9,1... | collective-permute-start | bytes 393224 | tf_op jit(solution)/shard_map/ppermute | solution.py:674
  525.6 40.8 %collective-permute-start.27 = (bf16[3,32,1024]{2,1,0:T(8,128)(2,1)S(1)}, bf16[3,32,1024]{2,1,0:T(8,128)(2,1)S(1)}, u32[]{:S(2)}, u32[]{:S(2)}) collective-permute-start(bf16[3,32,1024]{2,1,0:T(8,128)(2,1)S(1)} %get-tuple-element.262), channel_id=1, source_target_pairs={{0,16},{4,20},{8,24},{12,28},{16,0},{20,4},{24,8},{28,12},{1,17},{... | collective-permute-start | bytes 589832 | tf_op jit(solution)/shard_map/ppermute | solution.py:677
  (84 other events, 1049.0 us)
Sparse Core Ops, SparseCore 0:
  14.3 52.2 all-gather.5
  155.5 81.8 all-gather.3

commit v6 on v5

--- a/solution.py
+++ b/solution.py
@@ -623,32 +623,35 @@
     )(first.astype(jnp.int32).reshape(1), value)
 
 
-def owned_kernel(depth, pieces_ref, qkv_ref, ckv_ref):
-    _, heads, groups, share, _ = pieces_ref.shape
-    width = heads * depth
+def owned_kernel(depth, heads, groups, pieces_ref, qkv_ref, ckv_ref, rest_ref):
+    parts = pieces_ref.shape[0] // (heads * groups)
+    share, width = qkv_ref.shape[0], heads * depth
+    everything = 0.0
     for head in range(heads):
         total = 0.0
-        for p in range(pieces_ref.shape[0]):
+        for p in range(parts):
             for g in range(groups):
-                total = total + pieces_ref[p, head, g].astype(full)
+                total = total + pieces_ref[(p * heads + head) * groups + g].astype(full)
+        everything = everything + total
         at = head * depth
         for i in range(3):
-            qkv_ref[:, i * width + at : i * width + at + depth] = total[:, i * depth : (i + 1) * depth]
+            qkv_ref[:, i * width + at : i * width + at + depth] = total[:share, i * depth : (i + 1) * depth]
         for i in range(2):
-            ckv_ref[:, i * width + at : i * width + at + depth] = total[:, (3 + i) * depth : (4 + i) * depth]
-
-
-def owned_columns(pieces, depth):
-    _, heads, _, share, _ = pieces.shape
-    width = heads * depth
+            ckv_ref[:, i * width + at : i * width + at + depth] = total[:share, (3 + i) * depth : (4 + i) * depth]
+    rest_ref[...] = everything[share:]
+
+
+def owned_columns(pieces, share, groups, depth):
+    _, rows, cols = pieces.shape
     return pl.pallas_call(
-        functools.partial(owned_kernel, depth),
+        functools.partial(owned_kernel, depth, H, groups),
         out_shape=(
-            jax.ShapeDtypeStruct((share, 3 * width), full),
-            jax.ShapeDtypeStruct((share, 2 * width), full),
+            jax.ShapeDtypeStruct((share, 3 * H * depth), full),
+            jax.ShapeDtypeStruct((share, 2 * H * depth), full),
+            jax.ShapeDtypeStruct((rows - share, cols), full),
         ),
         in_specs=[vmem()],
-        out_specs=(vmem(),) * 2,
+        out_specs=(vmem(),) * 3,
         compiler_params=params(),
         name="owned_columns",
     )(pieces)
@@ -1132,9 +1135,7 @@
         square = move.add(square, outgoing).astype(low)
         _, square = move.send_half(square, 0, move.far, lambda v: move.swap_chip(v, 4))
         cout_own, cq_own, out_own = tuple(move.add(square, incoming))
-    heads_in = incoming[:, :share].reshape(parts, H, move.fsdp, share, cols)
-    qkv_own, ckv_own = owned_columns(heads_in, depth)
-    tail = jnp.sum(incoming[:, share:].astype(full), axis=0)
+    qkv_own, ckv_own, tail = owned_columns(incoming, share, move.fsdp, depth)
     at = early_rows.shape[1]
     first = tail[:at].reshape(-1)
     vec = first[: 11 * share].reshape(11, share)

time: 587 us -> 585 us (level)
  Pallas kernels: 86.7 us -> 103 us
  starting transfers between devices: 85.5 us -> 75.6 us
  waiting for transfers between devices: 134 us -> 128 us
    ppermute x12, starting transfers between devices: 26.7 us -> 16.4 us  [swap_chip(): return lax.ppermute(value, CHIP, [(i, i ^ bit) for i in range(self.chips)])]
    pallas_call x1, Pallas kernels: 13.7 us -> 23.5 us  [cross_forward(): pl.pallas_call(functools.partial(cross_forward_kernel, cross_tile(count))...]
    pallas_call x1, Pallas kernels: 13.4 us -> 19.4 us  [cross_backward(): pl.pallas_call(functools.partial(cross_backward_kernel, cross_tiles(queri...]
  transfers between devices with their start and end apart: 43 -> 43, of which waited for: 13 -> 13; matrix products, arithmetic and copies ran while one was open for 41% -> 41% of each run, Pallas kernels for 15% -> 18%
where the time goes in v6:
time: 585 us; the launch traced here: 575 us
  waiting for transfers between devices  128 us (22%)
  matrix products  105 us (18%)
  Pallas kernels  103 us (18%)
  local copies, waits for them, and re-layouts  94.9 us (16%)
  starting transfers between devices  75.6 us (13%)
  other arithmetic  53.3 us (9%)
  between operations  15.7 us (3%)
    dot_general x18, matrix products, contract(): lax.dot_general(left, right, (((left_dim,), (right_dim,)), ((), ())), pre...  73 us
    ppermute x12, waiting for transfers between devices, swap_chip(): return lax.ppermute(value, CHIP, [(i, i ^ bit) for i in range(self.chips)])  40.5 us
    pallas_call x1, Pallas kernels, self_backward(): pl.pallas_call(functools.partial(self_backward_kernel, tile, joined), out...  28 us
    ppermute x19, waiting for transfers between devices, swap(): return lax.ppermute(value, axis, [(0, 1), (1, 0)])  27.8 us
    all_to_all x1, waiting for transfers between devices, per_device(): incoming = lax.all_to_all(outgoing, ALL, 0, 0, tiled=True)  25.1 us
    pallas_call x1, Pallas kernels, cross_forward(): pl.pallas_call(functools.partial(cross_forward_kernel, cross_tile(count))...  23.5 us
    all_to_all x1, waiting for transfers between devices, per_device(): own_heads = lax.all_to_all(projected, HEADS, 0, 0, tiled=True)  22.3 us
    unnamed x165, local copies, waits for them, and re-layouts  22.1 us
  transfers between devices with their start and end apart: 43, of which 13 were waited for; matrix products, arithmetic and copies ran while one was open for 41% of the time, Pallas kernels for 18%

profile of v6, /device:TPU:0, one launch (start us, length us, event | category | flops | bytes accessed | tf_op | source)
XLA Modules:
  0.0 574.7 jit_solution(12071142466422147886)
XLA Ops:
  59.9 6.4 %all-to-all-start = ((bf16[16,192,256]{2,1,0:T(8,128)(2,1)}), bf16[16,192,256]{2,1,0:T(8,128)(2,1)S(1)}, u32[]{:S(2)}, u32[]{:S(2)}) async-start(bf16[16,192,256]{2,1,0:T(8,128)(2,1)} %bitcast.272), calls=%async_computation | async-start | bytes 3145728 | tf_op jit(solution)/shard_map/all_to_all | solution.py:928
  76.0 22.3 %all-to-all-done.own_ref.all_ref = bf16[16,192,256]{2,1,0:T(8,128)(2,1)S(1)} async-done(((bf16[16,192,256]{2,1,0:T(8,128)(2,1)}), bf16[16,192,256]{2,1,0:T(8,128)(2,1)S(1)}, u32[]{:S(2)}, u32[]{:S(2)}) %all-to-all-start) | async-done | bytes 1572896 | tf_op jit(solution)/shard_map/all_to_all | solution.py:928
  99.5 22.0 %self_forward.1 = (bf16[16,64,256]{2,1,0:T(8,128)(2,1)}, f32[64,4096]{1,0:T(8,128)}, f32[8,4096]{1,0:T(8,128)}) custom-call(s32[4,8]{1,0:T(4,128)} %get-tuple-element.81.plan, s32[32]{0:T(128)} %get-tuple-element.82.query_slot, s32[32]{0:T(128)} %get-tuple-element.83.key_slot, s32[2,4096]{1,0:T(2,128)} %get-tuple-element.84.range_ref, ...), custom_call_target="tpu_custom_call" | custom-call | flops 1 | bytes 1 | tf_op jit(solution)/shard_map/self_forward/pallas_call | solution.py:474
  126.0 5.8 %all-to-all-start.1 = ((bf16[16,64,256]{2,1,0:T(8,128)(2,1)}), bf16[16,64,256]{2,1,0:T(8,128)(2,1)S(1)}, u32[]{:S(2)}, u32[]{:S(2)}) async-start(bf16[16,64,256]{2,1,0:T(8,128)(2,1)} %get-tuple-element.93), calls=%async_computation.1 | async-start | bytes 1048576 | tf_op jit(solution)/shard_map/all_to_all | solution.py:935
  139.6 12.3 %collective-permute-done.5 = bf16[256,1024]{1,0:T(8,128)(2,1)S(1)} collective-permute-done((bf16[256,1024]{1,0:T(8,128)(2,1)S(1)}, bf16[256,1024]{1,0:T(8,128)(2,1)S(1)}, u32[]{:S(2)}, u32[]{:S(2)}) %collective-permute-start.5) | collective-permute-done | bytes 524320 | tf_op jit(solution)/shard_map/ppermute | solution.py:680
  164.8 14.3 %fusion.6.key_ref.value_ref = bf16[2048,2048]{1,0:T(8,128)(2,1)} fusion(f32[2048]{0:T(1024)S(1)} %concatenate.103, bf16[1024,2048]{1,0:T(8,128)(2,1)} %slice_dynamic-update-slice_fusion.1, bf16[1,2048,1024]{2,1,0:T(8,128)(2,1)} %all-gather.6.cloned.1.call-done), kind=kOutput, calls=%fused_computation.11 | convolution fusion | flops 8598323200 | bytes 16785408 | tf_op jit(solution)/shard_map/dot_general | solution.py:943
  181.8 23.5 %cross_forward.1 = (bf16[1024,256]{1,0:T(8,128)(2,1)}, f32[1024,256]{1,0:T(8,128)}, f32[8,8,256]{2,1,0:T(8,128)}) custom-call(s32[4,1]{1,0:T(4,128)} %get-tuple-element.85.plan, s32[2,256]{1,0:T(2,128)} %get-tuple-element.87.range_ref, bf16[1024,256]{1,0:T(8,128)(2,1)} %fusion.20.query_ref, bf16[2048,2048]{1,0:T(8,128)(2,1)} %fusion.6.key_ref.value_ref, ...), custom_call_target="tpu_custom_call" | custom-call | flops 1 | bytes 1 | tf_op jit(solution)/shard_map/cross_forward/pallas_call | solution.py:547
  210.0 16.3 %collective-permute-done.9 = bf16[2048,1024]{1,0:T(8,128)(2,1)} collective-permute-done((bf16[2048,1024]{1,0:T(8,128)(2,1)}, bf16[2048,1024]{1,0:T(8,128)(2,1)}, u32[]{:S(2)}, u32[]{:S(2)}) %collective-permute-start.9) | collective-permute-done | bytes 4194336 | tf_op jit(solution)/shard_map/ppermute | solution.py:677
  238.8 6.3 %all-to-all-start.2 = ((bf16[16,64,256]{2,1,0:T(8,128)(2,1)}), bf16[16,64,256]{2,1,0:T(8,128)(2,1)S(1)}, u32[]{:S(2)}, u32[]{:S(2)}) async-start(bf16[16,64,256]{2,1,0:T(8,128)(2,1)} %bitcast.282), calls=%async_computation.2 | async-start | bytes 1048576 | tf_op jit(solution)/shard_map/all_to_all | solution.py:985
  245.1 7.1 %fusion.79 = f32[1024,2048]{1,0:T(8,128)S(1)} fusion(bf16[1024,1024]{1,0:T(8,128)(2,1)} %pad_maximum_fusion.7, bf16[1024,2048]{1,0:T(8,128)(2,1)} %slice_dynamic-update-slice_fusion.2), kind=kOutput, calls=%fused_computation.297 | convolution fusion | flops 4294967296 | bytes 14680064 | tf_op jit(solution)/shard_map/dot_general | solution.py:983
  252.2 15.1 %convert_reduce_fusion = (f32[2048]{0:T(1024)S(1)}, bf16[1024,2048]{1,0:T(8,128)(2,1)}, bf16[1024,2048]{1,0:T(8,128)(2,1)}) fusion(f32[1024,2048]{1,0:T(8,128)S(1)} %fusion.79, f32[2048]{0:T(1024)S(1)} %pad_maximum_fusion.12, bf16[1024,1024]{1,0:T(8,128)(2,1)} %constant_dynamic-update-slice_fusion.10, bf16[2048,1024]{1,0:T(8,128)(2,1)S(1)} %copy-done.26), kind=kOutput, calls=%fused_computation.12 | convolution fusion | flops 4355782656 | bytes 23085056 | tf_op jit(solution)/shard_map/dot_general | solution.py:50
  267.4 8.2 %convolution_convert_fusion.6 = bf16[1024,1024]{1,0:T(8,128)(2,1)S(1)} fusion(bf16[1024,2048]{1,0:T(8,128)(2,1)} %get-tuple-element.105, bf16[1024,2048]{1,0:T(8,128)(2,1)} %slice_dynamic-update-slice_fusion.2), kind=kOutput, calls=%fused_computation.50 | convolution fusion | flops 4296015872 | bytes 10485760 | tf_op jit(solution)/shard_map/dot_general | solution.py:50
  285.3 6.4 %convolution_convert_fusion.1 = bf16[2048,1024]{1,0:T(8,128)(2,1)S(1)} fusion(bf16[1024,2048]{1,0:T(8,128)(2,1)S(1)} %copy-done.64, bf16[1024,1024]{1,0:T(8,128)(2,1)} %constant_dynamic-update-slice_fusion.10), kind=kOutput, calls=%fused_computation.24 | convolution fusion | flops 4297064448 | bytes 10485760 | tf_op jit(solution)/shard_map/dot_general | solution.py:50
  303.5 6.0 %all-to-all-start.3 = ((bf16[16,80,256]{2,1,0:T(8,128)(2,1)}), bf16[16,80,256]{2,1,0:T(8,128)(2,1)}, u32[]{:S(2)}, u32[]{:S(2)}) async-start(bf16[16,80,256]{2,1,0:T(8,128)(2,1)} %fusion.32), calls=%async_computation.3 | async-start | bytes 1310720 | tf_op jit(solution)/shard_map/all_to_all | solution.py:1014
  309.5 7.4 %convolution_convert_fusion = bf16[1024,2048]{1,0:T(8,128)(2,1)S(1)} fusion(bf16[1024,1024]{1,0:T(8,128)(2,1)} %pad_maximum_fusion.7, bf16[1024,2048]{1,0:T(8,128)(2,1)} %get-tuple-element.105), kind=kOutput, calls=%fused_computation.23 | convolution fusion | flops 4297064448 | bytes 10485760 | tf_op jit(solution)/shard_map/dot_general | solution.py:50
  321.1 8.0 %convolution_convert_fusion.5 = bf16[1024,1024]{1,0:T(8,128)(2,1)S(1)} fusion(bf16[1024,2048]{1,0:T(8,128)(2,1)} %get-tuple-element.108, bf16[2048,1024]{1,0:T(8,128)(2,1)} %copy-done.25), kind=kOutput, calls=%fused_computation.49 | convolution fusion | flops 4296015872 | bytes 10485760 | tf_op jit(solution)/shard_map/dot_general | solution.py:1016
  332.4 19.4 %cross_backward.1 = (bf16[16,64,256]{2,1,0:T(8,128)(2,1)}, bf16[2048,128]{1,0:T(8,128)(2,1)}, bf16[16,64,256]{2,1,0:T(8,128)(2,1)}) custom-call(s32[4,8]{1,0:T(4,128)} %get-tuple-element.86.plan, s32[32]{0:T(128)} %get-tuple-element.82.query_slot, s32[2,4096]{1,0:T(2,128)} %get-tuple-element.88.range_ref, bf16[16,64,256]{2,1,0:T(8,128)(2,1)} %copy-done.34, ...), custom_call_target="tpu_custom_call" | custom-call | flops 1 | bytes 1 | tf_op jit(solution)/shard_map/cross_backward/pallas_call | solution.py:577
  400.8 28.0 %self_backward.1 = (bf16[16,256,256]{2,1,0:T(8,128)(2,1)}, bf16[192,4096]{1,0:T(8,128)(2,1)}) custom-call(s32[4,8]{1,0:T(4,128)} %get-tuple-element.81.plan, s32[32]{0:T(128)} %get-tuple-element.82.query_slot, s32[32]{0:T(128)} %get-tuple-element.83.key_slot, s32[2,4096]{1,0:T(2,128)} %get-tuple-element.84.range_ref, bf16[16,192,256]{2,1,0:T(8,128)(2,1)} %copy-done, ...), custom_call_target="tpu_custom_call" | custom-call | flops 1 | bytes 1 | tf_op jit(solution)/shard_map/self_backward/pallas_call | solution.py:509
  431.8 5.6 all-to-all-start.6
  457.6 17.6 %collective-permute-done.25 = bf16[2,256,1024]{2,1,0:T(8,128)(2,1)} collective-permute-done((bf16[2,256,1024]{2,1,0:T(8,128)(2,1)}, bf16[2,256,1024]{2,1,0:T(8,128)(2,1)}, u32[]{:S(2)}, u32[]{:S(2)}) %collective-permute-start.25) | collective-permute-done | bytes 1048608 | tf_op jit(solution)/shard_map/ppermute | solution.py:680
  485.8 8.1 %all-to-all-done.6 = bf16[16,256,256]{2,1,0:T(8,128)(2,1)} async-done(((bf16[16,256,256]{2,1,0:T(8,128)(2,1)}), bf16[16,256,256]{2,1,0:T(8,128)(2,1)}, u32[]{:S(2)}, u32[]{:S(2)}) %all-to-all-start.6) | async-done | bytes 2097184 | tf_op jit(solution)/shard_map/all_to_all | solution.py:1066
  504.2 5.8 %all-to-all-start.7 = ((bf16[32,35,320]{2,1,0:T(8,128)(2,1)}), bf16[32,35,320]{2,1,0:T(8,128)(2,1)}, u32[]{:S(2)}, u32[]{:S(2)}) async-start(bf16[32,35,320]{2,1,0:T(8,128)(2,1)} %pad_maximum_fusion.8), calls=%async_computation.7 | async-start | bytes 1966080 | tf_op jit(solution)/shard_map/all_to_all | solution.py:1130
  512.1 8.7 %collective-permute-done.28 = bf16[4,32,2048]{2,1,0:T(8,128)(2,1)} collective-permute-done((bf16[4,32,2048]{2,1,0:T(8,128)(2,1)}, bf16[4,32,2048]{2,1,0:T(8,128)(2,1)}, u32[]{:S(2)}, u32[]{:S(2)}) %collective-permute-start.28) | collective-permute-done | bytes 524320 | tf_op jit(solution)/shard_map/ppermute | solution.py:680
  532.2 25.1 %all-to-all-done.7.pieces_ref = bf16[32,35,320]{2,1,0:T(8,128)(2,1)} async-done(((bf16[32,35,320]{2,1,0:T(8,128)(2,1)}), bf16[32,35,320]{2,1,0:T(8,128)(2,1)}, u32[]{:S(2)}, u32[]{:S(2)}) %all-to-all-start.7) | async-done | bytes 716832 | tf_op jit(solution)/shard_map/all_to_all | solution.py:1130
  (432 shorter events, 253.5 us)
Async XLA Ops:
  7.2 157.6 %all-gather.6.cloned.1.call-start = ((), (), s32[]{:S(2)}) async-start(), calls=%async_computation.9 | async-start | bytes 4456448 | tf_op jit(solution)/shard_map/all_gather | solution.py:919
  10.1 37.8 %collective-permute-start = (bf16[256,3072]{1,0:T(8,128)(2,1)}, bf16[256,3072]{1,0:T(8,128)(2,1)}, u32[]{:S(2)}, u32[]{:S(2)}) collective-permute-start(bf16[256,3072]{1,0:T(8,128)(2,1)} %constant_dynamic-slice_fusion.11), channel_id=1, source_target_pairs={{0,1},{1,0},{2,3},{3,2},{4,5},{5,4},{6,7},{7,6},{8,9},{9,8},{10,11... | collective-permute-start | bytes 4718600 | tf_op jit(solution)/shard_map/ppermute | solution.py:677
  14.1 34.2 %collective-permute-start.2 = (bf16[15,512]{1,0:T(8,128)(2,1)S(1)}, bf16[15,512]{1,0:T(8,128)(2,1)S(1)}, u32[]{:S(2)}, u32[]{:S(2)}) collective-permute-start(bf16[15,512]{1,0:T(8,128)(2,1)S(1)} %concatenate.96), channel_id=1, source_target_pairs={{0,1},{1,0},{2,3},{3,2},{4,5},{5,4},{6,7},{7,6},{8,9},{9,8},{10,11... | collective-permute-start | bytes 46088 | tf_op jit(solution)/shard_map/ppermute | solution.py:677
  59.9 38.4 %all-to-all-start = ((bf16[16,192,256]{2,1,0:T(8,128)(2,1)}), bf16[16,192,256]{2,1,0:T(8,128)(2,1)S(1)}, u32[]{:S(2)}, u32[]{:S(2)}) async-start(bf16[16,192,256]{2,1,0:T(8,128)(2,1)} %bitcast.272), calls=%async_computation | async-start | bytes 3145728 | tf_op jit(solution)/shard_map/all_to_all | solution.py:928
  66.3 59.6 %collective-permute-start.3 = (bf16[256,5120]{1,0:T(8,128)(2,1)}, bf16[256,5120]{1,0:T(8,128)(2,1)}, u32[]{:S(2)}, u32[]{:S(2)}) collective-permute-start(bf16[256,5120]{1,0:T(8,128)(2,1)} %pad_maximum_fusion.6), channel_id=1, source_target_pairs={{0,1},{1,0},{2,3},{3,2},{4,5},{5,4},{6,7},{7,6},{8,9},{9,8},{10,11... | collective-permute-start | bytes 7864328 | tf_op jit(solution)/shard_map/ppermute | solution.py:677
  131.9 200.5 %all-gather.4.cloned.1.call-start = ((), (), s32[]{:S(2)}) async-start(), calls=%async_computation.8 | async-start | bytes 8912896 | tf_op jit(solution)/shard_map/all_gather | solution.py:950
  133.1 93.2 %collective-permute-start.9 = (bf16[2048,1024]{1,0:T(8,128)(2,1)}, bf16[2048,1024]{1,0:T(8,128)(2,1)}, u32[]{:S(2)}, u32[]{:S(2)}) collective-permute-start(bf16[2048,1024]{1,0:T(8,128)(2,1)} %get-tuple-element.99), channel_id=1, source_target_pairs={{0,1},{1,0},{2,3},{3,2},{4,5},{5,4},{6,7},{7,6},{8,9},{9,8},{10,11... | collective-permute-start | bytes 12582920 | tf_op jit(solution)/shard_map/ppermute | solution.py:677
  294.2 57.6 %collective-permute-start.14 = (bf16[2,2,256,1024]{3,2,1,0:T(8,128)(2,1)}, bf16[2,2,256,1024]{3,2,1,0:T(8,128)(2,1)}, u32[]{:S(2)}, u32[]{:S(2)}) collective-permute-start(bf16[2,2,256,1024]{3,2,1,0:T(8,128)(2,1)} %get-tuple-element.217), channel_id=1, source_target_pairs={{0,1},{1,0},{2,3},{3,2},{4,5},{5,4},{6,7},{7,6},{8,9},{9,8},{10,11... | collective-permute-start | bytes 6291464 | tf_op jit(solution)/shard_map/ppermute | solution.py:677
  319.5 67.4 %collective-permute-start.15 = (bf16[2,2,4,32,2048]{4,3,2,1,0:T(8,128)(2,1)}, bf16[2,2,4,32,2048]{4,3,2,1,0:T(8,128)(2,1)}, u32[]{:S(2)}, u32[]{:S(2)}) collective-permute-start(bf16[2,2,4,32,2048]{4,3,2,1,0:T(8,128)(2,1)} %get-tuple-element.219), channel_id=1, source_target_pairs={{0,1},{1,0},{2,3},{3,2},{4,5},{5,4},{6,7},{7,6},{8,9},{9,8},{10,11... | collective-permute-start | bytes 6291464 | tf_op jit(solution)/shard_map/ppermute | solution.py:677
  330.4 147.6 %collective-permute-start.21 = (bf16[256,1024]{1,0:T(8,128)(2,1)}, bf16[256,1024]{1,0:T(8,128)(2,1)}, u32[]{:S(2)}, u32[]{:S(2)}) collective-permute-start(bf16[256,1024]{1,0:T(8,128)(2,1)} %get-tuple-element.239), channel_id=1, source_target_pairs={{0,2},{2,0},{1,3},{3,1},{4,6},{6,4},{5,7},{7,5},{8,10},{10,8},{9,1... | collective-permute-start | bytes 1572872 | tf_op jit(solution)/shard_map/ppermute | solution.py:677
  330.6 150.3 %collective-permute-start.22 = (bf16[256,1024]{1,0:T(8,128)(2,1)}, bf16[256,1024]{1,0:T(8,128)(2,1)}, u32[]{:S(2)}, u32[]{:S(2)}) collective-permute-start(bf16[256,1024]{1,0:T(8,128)(2,1)} %get-tuple-element.238), channel_id=1, source_target_pairs={{0,4},{4,0},{8,12},{12,8},{16,20},{20,16},{24,28},{28,24},{1,5},{5... | collective-permute-start | bytes 1572872 | tf_op jit(solution)/shard_map/ppermute | solution.py:680
  389.3 91.6 %collective-permute-start.23 = (bf16[256,1024]{1,0:T(8,128)(2,1)}, bf16[256,1024]{1,0:T(8,128)(2,1)}, u32[]{:S(2)}, u32[]{:S(2)}) collective-permute-start(bf16[256,1024]{1,0:T(8,128)(2,1)} %get-tuple-element.237), channel_id=1, source_target_pairs={{0,6},{2,4},{4,2},{6,0},{8,14},{10,12},{12,10},{14,8},{16,22},{18,... | collective-permute-start | bytes 1572872 | tf_op jit(solution)/shard_map/ppermute | solution.py:768
  395.1 36.6 %collective-permute-start.20 = (bf16[8,3,32,1024]{3,2,0,1:T(8,128)(2,1)}, bf16[8,3,32,1024]{3,2,0,1:T(8,128)(2,1)}, u32[]{:S(2)}, u32[]{:S(2)}) collective-permute-start(bf16[8,3,32,1024]{3,2,0,1:T(8,128)(2,1)} %get-tuple-element.223), channel_id=1, source_target_pairs={{0,1},{1,0},{2,3},{3,2},{4,5},{5,4},{6,7},{7,6},{8,9},{9,8},{10,11... | collective-permute-start | bytes 4718600 | tf_op jit(solution)/shard_map/ppermute | solution.py:677
  397.7 33.4 %collective-permute-start.19 = (bf16[2,4,32,2048]{3,2,1,0:T(8,128)(2,1)}, bf16[2,4,32,2048]{3,2,1,0:T(8,128)(2,1)}, u32[]{:S(2)}, u32[]{:S(2)}) collective-permute-start(bf16[2,4,32,2048]{3,2,1,0:T(8,128)(2,1)} %get-tuple-element.235), channel_id=1, source_target_pairs={{0,8},{4,12},{8,0},{12,4},{16,24},{20,28},{24,16},{28,20},{1,9},{5... | collective-permute-start | bytes 3145736 | tf_op jit(solution)/shard_map/ppermute | solution.py:680
  431.1 44.2 %collective-permute-start.25 = (bf16[2,256,1024]{2,1,0:T(8,128)(2,1)}, bf16[2,256,1024]{2,1,0:T(8,128)(2,1)}, u32[]{:S(2)}, u32[]{:S(2)}) collective-permute-start(bf16[2,256,1024]{2,1,0:T(8,128)(2,1)} %get-tuple-element.233), channel_id=1, source_target_pairs={{0,8},{4,12},{8,0},{12,4},{16,24},{20,28},{24,16},{28,20},{1,9},{5... | collective-permute-start | bytes 3145736 | tf_op jit(solution)/shard_map/ppermute | solution.py:680
  431.8 62.1 %all-to-all-start.6 = ((bf16[16,256,256]{2,1,0:T(8,128)(2,1)}), bf16[16,256,256]{2,1,0:T(8,128)(2,1)}, u32[]{:S(2)}, u32[]{:S(2)}) async-start(bf16[16,256,256]{2,1,0:T(8,128)(2,1)} %get-tuple-element.129), calls=%async_computation.6 | async-start | bytes 4194304 | tf_op jit(solution)/shard_map/all_to_all | solution.py:1066
  445.2 38.3 %collective-permute-start.24 = (bf16[2,2,3,32,1024]{4,3,2,0,1:T(8,128)(2,1)}, bf16[2,2,3,32,1024]{4,3,2,0,1:T(8,128)(2,1)}, u32[]{:S(2)}, u32[]{:S(2)}) collective-permute-start(bf16[2,2,3,32,1024]{4,3,2,0,1:T(8,128)(2,1)} %bitcast.262), channel_id=1, source_target_pairs={{0,4},{4,0},{8,12},{12,8},{16,20},{20,16},{24,28},{28,24},{1,5},{5... | collective-permute-start | bytes 2359304 | tf_op jit(solution)/shard_map/ppermute | solution.py:680
  475.3 45.5 %collective-permute-start.28 = (bf16[4,32,2048]{2,1,0:T(8,128)(2,1)}, bf16[4,32,2048]{2,1,0:T(8,128)(2,1)}, u32[]{:S(2)}, u32[]{:S(2)}) collective-permute-start(bf16[4,32,2048]{2,1,0:T(8,128)(2,1)} %get-tuple-element.247), channel_id=1, source_target_pairs={{0,16},{4,20},{8,24},{12,28},{16,0},{20,4},{24,8},{28,12},{1,17},{... | collective-permute-start | bytes 1572872 | tf_op jit(solution)/shard_map/ppermute | solution.py:680
  478.0 87.5 %collective-permute-start.32 = (bf16[256,1024]{1,0:T(8,128)(2,1)}, bf16[256,1024]{1,0:T(8,128)(2,1)}, u32[]{:S(2)}, u32[]{:S(2)}) collective-permute-start(bf16[256,1024]{1,0:T(8,128)(2,1)} %get-tuple-element.245), channel_id=1, source_target_pairs={{0,16},{4,20},{8,24},{12,28},{16,0},{20,4},{24,8},{28,12},{1,17},{... | collective-permute-start | bytes 1572872 | tf_op jit(solution)/shard_map/ppermute | solution.py:680
  485.8 38.5 %collective-permute-start.26 = (bf16[2,3,32,1024]{3,2,1,0:T(8,128)(2,1)}, bf16[2,3,32,1024]{3,2,1,0:T(8,128)(2,1)}, u32[]{:S(2)}, u32[]{:S(2)}) collective-permute-start(bf16[2,3,32,1024]{3,2,1,0:T(8,128)(2,1)} %get-tuple-element.249), channel_id=1, source_target_pairs={{0,8},{4,12},{8,0},{12,4},{16,24},{20,28},{24,16},{28,20},{1,9},{5... | collective-permute-start | bytes 1179656 | tf_op jit(solution)/shard_map/ppermute | solution.py:680
  504.2 53.0 %all-to-all-start.7 = ((bf16[32,35,320]{2,1,0:T(8,128)(2,1)}), bf16[32,35,320]{2,1,0:T(8,128)(2,1)}, u32[]{:S(2)}, u32[]{:S(2)}) async-start(bf16[32,35,320]{2,1,0:T(8,128)(2,1)} %pad_maximum_fusion.8), calls=%async_computation.7 | async-start | bytes 1966080 | tf_op jit(solution)/shard_map/all_to_all | solution.py:1130
  523.5 33.8 %collective-permute-start.31 = (bf16[32,2048]{1,0:T(8,128)(2,1)S(1)}, bf16[32,2048]{1,0:T(8,128)(2,1)S(1)}, u32[]{:S(2)}, u32[]{:S(2)}) collective-permute-start(bf16[32,2048]{1,0:T(8,128)(2,1)S(1)} %get-tuple-element.254), channel_id=1, source_target_pairs={{0,6},{2,4},{4,2},{6,0},{8,14},{10,12},{12,10},{14,8},{16,22},{18,... | collective-permute-start | bytes 393224 | tf_op jit(solution)/shard_map/ppermute | solution.py:846
  523.5 37.6 %collective-permute-start.29 = (bf16[32,2048]{1,0:T(8,128)(2,1)S(1)}, bf16[32,2048]{1,0:T(8,128)(2,1)S(1)}, u32[]{:S(2)}, u32[]{:S(2)}) collective-permute-start(bf16[32,2048]{1,0:T(8,128)(2,1)S(1)} %get-tuple-element.256), channel_id=1, source_target_pairs={{0,2},{2,0},{1,3},{3,1},{4,6},{6,4},{5,7},{7,5},{8,10},{10,8},{9,1... | collective-permute-start | bytes 393224 | tf_op jit(solution)/shard_map/ppermute | solution.py:677
  525.4 39.2 %collective-permute-start.27 = (bf16[3,32,1024]{2,1,0:T(8,128)(2,1)S(1)}, bf16[3,32,1024]{2,1,0:T(8,128)(2,1)S(1)}, u32[]{:S(2)}, u32[]{:S(2)}) collective-permute-start(bf16[3,32,1024]{2,1,0:T(8,128)(2,1)S(1)} %get-tuple-element.264), channel_id=1, source_target_pairs={{0,16},{4,20},{8,24},{12,28},{16,0},{20,4},{24,8},{28,12},{1,17},{... | collective-permute-start | bytes 589832 | tf_op jit(solution)/shard_map/ppermute | solution.py:680
  (84 other events, 1003.5 us)
Sparse Core Ops, SparseCore 0:
  14.3 52.2 all-gather.5
  155.6 77.4 all-gather.3
